TPU v7x, 32 devices: a whole 2x2x4 slice. The times are simulated.
32 devices in a mesh: groups: 2 (over y), ctx: 16 (over z, x, core).
Axes of the slice: x: 2, y: 2, z: 4, core: 2. Of those that a mesh axis runs over, the one named last changes fastest.
Arguments:
- old_cache: bfloat16 [4096, 2048], P(('groups', 'ctx')), parts along dimension 0, may hold values from -10 to 10
- new_slot: int32 [4096], P(('groups', 'ctx')), parts along dimension 0, may hold values from -1 to 1023, as said below
- lengths: int32 [8], P('groups'), parts along dimension 0, may hold values from 1 to 768, 1024 in all
- old_angle: float32 [768, 64], replicated, may hold values from -3.15 to 3.15
- new_angle: float32 [768, 64], replicated, may hold values from -3.15 to 4.15
- queries: bfloat16 [64, 8192], P(('groups', 'ctx')), parts along dimension 0, may hold values from -128 to 128
- new_kv: bfloat16 [64, 2048], P(('groups', 'ctx')), parts along dimension 0, may hold values from -6 to 6
- resid: bfloat16 [64, 8192], P(('groups', 'ctx')), parts along dimension 0, may hold values from -6 to 6
- gain: bfloat16 [8192], replicated, may hold values from 0.25 to 1.75
- w_gate: bfloat16 [8192, 28672], P(None, 'ctx'), may hold values from -0.0625 to 0.0625
- w_up: bfloat16 [8192, 28672], P(None, 'ctx'), may hold values from -0.0625 to 0.0625
- w_down: bfloat16 [28672, 8192], P('ctx'), may hold values from -0.03125 to 0.03125
Outputs:
- new_cache: bfloat16 [2048, 2048], P(('groups', 'ctx')), parts along dimension 0
- layer_out: bfloat16 [64, 8192], P(('groups', 'ctx')), parts along dimension 0
There are 2 independent parts, one for each index of `groups`. A program takes and returns all parts, laid end to end along the dimension named above; an argument that names none is the same for every part. Nothing has to cross between parts.
Inputs may be any that keep to these rules, and one draw needn't show every extreme that they name: `new_slot`: for slots below 1024: distinct slots of the new layout; the tokens of each holding device go to every device of ctx, exactly 8 to each. Slots from 1024 on hold -1.
All inputs are finite; a program needn't handle non-finite values.
Results may differ from a plain program's by a relative error of at most 0.0057.
Values may be sent and summed in bfloat16 or wider, within the bound.
No kernel may reach another device: no remote copies, remote signals or barrier semaphores. Data moves between devices by JAX's collectives and lax.ppermute only.
A program may use at most 128 MiB of HBM per device.

v0:
```python
import jax
import jax.numpy as jnp
from jax import lax
from jax.experimental import pallas as pl
from jax.experimental.pallas import tpu as pltpu
from jax.sharding import PartitionSpec as P

QH = 64
KVH = 8
HD = 128
CTOK_DEV = 64
SAMPLES = 4
CELL = 4
F32 = jnp.float32
BF16 = jnp.bfloat16
EXTRA = 128


def vmem():
    return pl.BlockSpec(memory_space=pltpu.VMEM)


def smem():
    return pl.BlockSpec(memory_space=pltpu.SMEM)


def hbm():
    return pl.BlockSpec(memory_space=pl.ANY)


def in_hbm(x):
    return pltpu.with_memory_space_constraint(x, pltpu.HBM)


def in_vmem(x):
    return pltpu.with_memory_space_constraint(x, pltpu.VMEM)


def call(body, ins, outs, args, limit_mib, scratch=(), fetch=(), moved=0, on_chip=False):
    kind = pltpu.VMEM if on_chip else jax.ShapeDtypeStruct
    shapes = [kind(s, d) for s, d in outs]
    shapes += [pltpu.VMEM(piece_shape(p), BF16) for p in fetch]
    return pl.pallas_call(
        body,
        in_specs=ins,
        out_specs=[vmem() for _ in shapes],
        out_shape=shapes,
        scratch_shapes=list(scratch),
        compiler_params=pltpu.CompilerParams(vmem_limit_bytes=limit_mib << 20),
        cost_estimate=pl.CostEstimate(flops=0, transcendentals=0, bytes_accessed=moved << 20),
    )(*args)


def here():
    return lax.axis_index("ctx").astype(jnp.int32)


def three_parts(value):
    first = value.astype(BF16).astype(F32)
    rest = value - first
    second = rest.astype(BF16).astype(F32)
    return first, second, rest - second


def row_of(tokens, scal, requests):
    end = scal[0]
    passed = tokens >= end
    row = passed.astype(jnp.int32)
    prior = jnp.where(passed, end, 0)
    for r in range(1, requests):
        end = end + scal[r]
        passed = tokens >= end
        row = row + passed.astype(jnp.int32)
        prior = jnp.where(passed, end, prior)
    return row, prior


def to_sublanes(lane_row):
    n = lane_row.shape[1]
    sub = lax.broadcasted_iota(jnp.int32, (n, n), 0)
    lane = lax.broadcasted_iota(jnp.int32, (n, n), 1)
    return jnp.sum(jnp.where(sub == lane, lane_row, 0), axis=1, keepdims=True)


GU_ROWS = 512
DOWN_ROWS = 256


def piece_shape(piece):
    kind, _, n, cols = piece
    return (n * DOWN_ROWS, cols) if kind == "down" else (n, GU_ROWS, cols)


def fetch_copies(fetch, weights, pieces, sem):
    w_gate, w_up, w_down = weights
    copies = []
    for (kind, first, n, _), out in zip(fetch, pieces):
        for i in range(n):
            if kind == "down":
                src = w_down.at[pl.ds((first + i) * DOWN_ROWS, DOWN_ROWS), :]
                dst = out.at[pl.ds(i * DOWN_ROWS, DOWN_ROWS), :]
            else:
                wide = w_gate.shape[0] // CELL
                row = (here() % CELL ^ 1) * wide + (first + i) // 2 * GU_ROWS
                w = w_gate if (first + i) % 2 == 0 else w_up
                src = w.at[pl.ds(pl.multiple_of(row, GU_ROWS), GU_ROWS), :]
                dst = out.at[i]
            copies.append(pltpu.make_async_copy(src, dst, sem.at[len(copies)]))
    return copies


def count_of(fetch):
    return max(1, sum(p[2] for p in fetch))


def warm_body(fetch, dep, w_gate, w_up, w_down, *refs):
    copies = fetch_copies(fetch, (w_gate, w_up, w_down), refs[:-1], refs[-1])
    for c in copies:
        c.start()
    for c in copies:
        c.wait()


def turn_body(requests, devices, fetch, scal, *refs):
    sources, weights, refs = refs[:8], refs[8:11], refs[11:]
    outs, refs = refs[: 3 * CELL + 1], refs[3 * CELL + 1 :]
    msgs, sends, relays = outs[:CELL], outs[CELL : 2 * CELL], outs[2 * CELL : 3 * CELL]
    own_gain = outs[3 * CELL]
    pieces, refs = refs[: len(fetch)], refs[len(fetch) :]
    locals_, sems, fetch_sem = refs[:8], refs[8], refs[9]
    loads = [pltpu.make_async_copy(a, b, sems.at[i]) for i, (a, b) in enumerate(zip(sources, locals_))]
    for c in loads:
        c.start()
    fetched = fetch_copies(fetch, weights, pieces, fetch_sem)
    for c in fetched:
        c.start()
    for c in loads:
        c.wait()
    slot, cache, old_angle, new_angle, q, kv, res, gain = locals_
    me = here()
    pos_in_cell = me % CELL
    tok_n, width = cache.shape
    table_n = old_angle.shape[1]
    heads_here = KVH // CELL
    key_cols = heads_here * HD
    tokens = me * tok_n + lax.broadcasted_iota(jnp.int32, (tok_n, 1), 0)
    _, prior = row_of(tokens, scal, requests)
    position = jnp.clip(tokens - prior, 0, table_n - 1)
    hot = (lax.broadcasted_iota(jnp.int32, (tok_n, table_n), 1) == position).astype(F32)
    diff = new_angle[...] - old_angle[...]
    diff = jnp.concatenate([diff, diff], axis=0)
    delta = lax.dot_general(
        hot,
        diff,
        (((1,), (1,)), ((), ())),
        precision=lax.Precision.HIGHEST,
        preferred_element_type=F32,
    )
    cosine = jnp.cos(delta)
    lane = lax.broadcasted_iota(jnp.int32, (tok_n, HD), 1)
    sine = jnp.where(lane < HD // 2, -jnp.sin(delta), jnp.sin(delta))
    half = width // 2
    keys = []
    for h in range(KVH):
        key = cache[:, h * HD : (h + 1) * HD].astype(F32)
        keys.append((key * cosine + pltpu.roll(key, HD // 2, 1) * sine).astype(BF16))
    turned = jnp.concatenate(keys + [cache[:, half:]], axis=1)
    for k in range(CELL):
        peer = pos_in_cell ^ k
        for g in range(CELL):

            @pl.when(peer == g)
            def _():
                sends[k][:, :key_cols] = turned[:, g * key_cols : (g + 1) * key_cols]
                sends[k][:, key_cols:] = turned[:, half + g * key_cols : half + (g + 1) * key_cols]
                wide = q.shape[1] // CELL
                msgs[k][:, :wide] = q[:, g * wide : (g + 1) * wide]
                msgs[k][:, wide : wide + key_cols] = kv[:, g * key_cols : (g + 1) * key_cols]
                msgs[k][:, wide + key_cols : wide + 2 * key_cols] = kv[
                    :, half + g * key_cols : half + (g + 1) * key_cols
                ]
                msgs[k][:, wide + 2 * key_cols :] = res[:, g * wide : (g + 1) * wide]
                if k == 0:
                    own_gain[...] = gain[:, g * wide : (g + 1) * wide]

    place = slot[...]
    per_peer = tok_n // devices
    lanes = lax.broadcasted_iota(jnp.int32, (1, tok_n), 1)
    target = jnp.where(place >= 0, place // CTOK_DEV, lanes // per_peer)
    landing = jnp.where(place >= 0, place % CTOK_DEV, -1)
    target_s = to_sublanes(target)
    sub2 = lax.broadcasted_iota(jnp.int32, (tok_n, tok_n), 0)
    lane2 = lax.broadcasted_iota(jnp.int32, (tok_n, tok_n), 1)
    ahead = ((target_s == target) & (sub2 < lane2)).astype(jnp.int32)
    rank = jnp.sum(ahead, axis=0, keepdims=True)
    order = (target % CELL) * (devices // CELL) + target // CELL
    pick = sub2 == (order * per_peer + rank)
    moved = jnp.dot(pick.astype(BF16), turned, preferred_element_type=F32).astype(BF16)
    land_s = jnp.sum(jnp.where(pick, landing, 0), axis=1, keepdims=True)
    land_wide = jnp.broadcast_to(land_s.astype(F32), (tok_n, EXTRA)).astype(BF16)
    block = tok_n // CELL
    for k in range(CELL):
        for g in range(CELL):

            @pl.when((pos_in_cell ^ k) == g)
            def _():
                relays[k][:, :width] = moved[g * block : (g + 1) * block]
                relays[k][:, width:] = land_wide[g * block : (g + 1) * block]

    for c in fetched:
        c.wait()


def assemble_body(*refs):
    msgs, cat, query = refs[:CELL], refs[CELL], refs[CELL + 1]
    pos = here() % CELL
    wide = query.shape[1]
    whole = [r[...].astype(F32) for r in msgs]
    for bit in (1, 2):
        flip = (pos & bit) != 0
        whole = [jnp.where(flip, whole[a ^ bit], whole[a]) for a in range(CELL)]
    whole = jnp.concatenate(whole, axis=0).astype(BF16)
    cat[...] = whole
    query[...] = whole[:, :wide]


def place_body(*refs):
    out = refs[-1]
    got = jnp.concatenate([r[...] for r in refs[:-1]], axis=0)
    width = out.shape[1]
    rows = got.shape[0]
    land = got[:, width:].astype(F32)[:, :CTOK_DEV]
    want = lax.broadcasted_iota(jnp.int32, (rows, CTOK_DEV), 1).astype(F32)
    pick = (land == want).astype(BF16)
    out[...] = lax.dot_general(
        pick, got[:, :width], (((0,), (0,)), ((), ())), preferred_element_type=F32
    ).astype(BF16)


def scores_body(requests, planes, fetch, scal, *refs):
    qs, kvs, refs = refs[:planes], refs[planes : planes + CELL], refs[planes + CELL :]
    weights, outs, refs = refs[:3], refs[3 : 3 + planes], refs[3 + planes :]
    fetched = fetch_copies(fetch, weights, refs[: len(fetch)], refs[-1])
    for c in fetched:
        c.start()
    me = here()
    plane, pos_in_cell = me // CELL, me % CELL
    rows = qs[0].shape[0]
    tok_n, both = kvs[0].shape
    key_cols = both // 2
    heads_here = key_cols // HD
    group = QH // KVH
    all_rows = rows * planes
    query = jnp.concatenate([r[...].astype(F32) for r in qs], axis=0).astype(BF16)
    token_rows = []
    for k in range(CELL):
        base = (plane * CELL + (pos_in_cell ^ k)) * tok_n
        tokens = base + lax.broadcasted_iota(jnp.int32, (1, tok_n), 1)
        token_rows.append(row_of(tokens, scal, requests)[0])
    token_row = jnp.concatenate(token_rows, axis=1)
    index = lax.broadcasted_iota(jnp.int32, (group * all_rows, 1), 0)
    query_row = ((index // rows) % planes) ^ plane
    matching = query_row == token_row
    lane = lax.broadcasted_iota(jnp.int32, (all_rows, EXTRA), 1)
    extra = jnp.zeros((all_rows, EXTRA), F32)
    count = heads_here * group
    scale = 1.0 / float(HD) ** 0.5
    for j in range(heads_here):
        keys = jnp.concatenate([r[:, j * HD : (j + 1) * HD] for r in kvs], axis=0)
        values = jnp.concatenate(
            [r[:, key_cols + j * HD : key_cols + (j + 1) * HD] for r in kvs], axis=0
        )
        stacked = jnp.concatenate(
            [query[:, (j * group + g) * HD : (j * group + g + 1) * HD] for g in range(group)],
            axis=0,
        )
        scores = (
            lax.dot_general(stacked, keys, (((1,), (1,)), ((), ())), preferred_element_type=F32)
            * scale
        )
        top = jnp.max(jnp.where(matching, scores, -1e30), axis=1, keepdims=True)
        weights = jnp.where(matching, jnp.exp(scores - top), 0.0)
        total = jnp.sum(weights, axis=1, keepdims=True)
        high = weights.astype(BF16)
        low = (weights - high.astype(F32)).astype(BF16)
        summed = jnp.dot(high, values, preferred_element_type=F32) + jnp.dot(
            low, values, preferred_element_type=F32
        )
        mean = summed / jnp.where(total > 0, total, 1.0)
        top = jnp.where(total > 0, top, 0.0)
        tops = three_parts(top)
        totals = three_parts(total)
        for g in range(group):
            h = j * group + g
            part = slice(g * all_rows, (g + 1) * all_rows)
            for k in range(planes):
                outs[k][:, h * HD : (h + 1) * HD] = mean[
                    g * all_rows + k * rows : g * all_rows + (k + 1) * rows
                ].astype(BF16)
            for i in range(3):
                extra = jnp.where(lane == i * count + h, tops[i][part], extra)
                extra = jnp.where(lane == (3 + i) * count + h, totals[i][part], extra)
    for k in range(planes):
        outs[k][:, count * HD :] = extra[k * rows : (k + 1) * rows].astype(BF16)
    for c in fetched:
        c.wait()


def merge_body(planes, fetch, *refs):
    parts, cat, gain, refs = refs[:planes], *refs[planes : planes + 2], refs[planes + 2 :]
    moved, weights, refs = refs[:CELL], refs[CELL : CELL + 3], refs[CELL + 3 :]
    norm_out, h_out, regrouped, refs = *refs[:2], refs[2 : 2 + planes], refs[2 + planes :]
    fetched = fetch_copies(fetch, weights, refs[: len(fetch)], refs[-1])
    for c in fetched:
        c.start()
    rows = cat.shape[0]
    wide = norm_out.shape[1] - EXTRA
    count = wide // HD
    group = QH // KVH
    heads_here = count // group
    key_cols = heads_here * HD
    scale = 1.0 / float(HD) ** 0.5
    lane = lax.broadcasted_iota(jnp.int32, (rows, EXTRA), 1)
    odd = lax.broadcasted_iota(jnp.int32, (rows, 1), 0) % 2 == 1
    fresh = cat[:, wide : wide + 2 * key_cols].astype(F32)
    before = pltpu.roll(fresh, 1, 0)
    score_self = jnp.zeros((rows, EXTRA), F32)
    score_before = jnp.zeros((rows, EXTRA), F32)
    for h in range(count):
        j = h // group
        query = cat[:, h * HD : (h + 1) * HD].astype(F32)
        one = jnp.sum(query * fresh[:, j * HD : (j + 1) * HD], axis=1, keepdims=True) * scale
        two = jnp.sum(query * before[:, j * HD : (j + 1) * HD], axis=1, keepdims=True) * scale
        score_self = jnp.where(lane == h, one, score_self)
        score_before = jnp.where(lane == h, two, score_before)
    tops, totals = [], []
    for part in parts:
        extra = part[:, wide:].astype(F32)
        shifted = [extra] + [pltpu.roll(extra, EXTRA - i * count, 1) for i in range(1, 6)]
        tops.append(shifted[0] + shifted[1] + shifted[2])
        totals.append(shifted[3] + shifted[4] + shifted[5])
    highest = jnp.where(odd, jnp.maximum(score_self, score_before), score_self)
    for top, total in zip(tops, totals):
        highest = jnp.where(total > 0, jnp.maximum(highest, top), highest)
    shares = [
        jnp.where(total > 0, total * jnp.exp(jnp.where(total > 0, top, highest) - highest), 0.0)
        for top, total in zip(tops, totals)
    ]
    share_self = jnp.exp(score_self - highest)
    share_before = jnp.where(odd, jnp.exp(score_before - highest), 0.0)
    whole = share_self + share_before
    for share in shares:
        whole = whole + share
    squares = jnp.zeros((rows, 1), F32)
    for h in range(count):
        j = h // group
        value = slice(key_cols + j * HD, key_cols + (j + 1) * HD)
        lanes = slice(h * HD, (h + 1) * HD)
        attn = share_self[:, h : h + 1] * fresh[:, value]
        attn = attn + share_before[:, h : h + 1] * before[:, value]
        for part, share in zip(parts, shares):
            attn = attn + share[:, h : h + 1] * part[:, lanes].astype(F32)
        attn = attn / whole[:, h : h + 1]
        base = wide + 2 * key_cols + h * HD
        state = cat[:, base : base + HD].astype(F32) + attn
        h_out[:, lanes] = state
        squares = squares + jnp.sum(state * state, axis=1, keepdims=True)
        norm_out[:, lanes] = (state * gain[:, lanes].astype(F32)).astype(BF16)
    pieces = three_parts(squares)
    extra = jnp.zeros((rows, EXTRA), F32)
    for i in range(3):
        extra = jnp.where(lane == i, pieces[i], extra)
    norm_out[:, wide:] = extra.astype(BF16)
    plane = here() // CELL
    per = moved[0].shape[0] // planes
    for k in range(planes):
        for g in range(planes):

            @pl.when((plane ^ k) == g)
            def _():
                for a in range(CELL):
                    regrouped[k][a * per : (a + 1) * per] = moved[a][g * per : (g + 1) * per]

    for c in fetched:
        c.wait()


def stream(copies, depth):
    for c in copies[:depth]:
        c.start()

    def ready(i):
        copies[i].wait()

    def freed(i):
        if i + depth < len(copies):
            copies[i + depth].start()

    return ready, freed


def gate_up_copies(slices, w_gate, w_up, buf, sem, wide):
    copies = []
    for first_row in slices:
        for i in range(wide // GU_ROWS):
            for w in (w_gate, w_up):
                slot = len(copies) % buf.shape[0]
                rows = pl.ds(pl.multiple_of(first_row + i * GU_ROWS, GU_ROWS), GU_ROWS)
                copies.append(pltpu.make_async_copy(w.at[rows, :], buf.at[slot], sem.at[slot]))
    return copies


def first_gate_up_body(flip, has_acc, *refs):
    if has_acc:
        x, acc_in, w_gate, w_up, acc_out, buf, sem = refs
    else:
        x, w_gate, w_up, acc_out, buf, sem = refs
    wide = x.shape[1] - EXTRA
    ff = w_gate.shape[1]
    pos = (here() % CELL) ^ flip
    copies = gate_up_copies([pos * wide], w_gate, w_up, buf, sem, wide)
    ready, freed = stream(copies, buf.shape[0])
    for i in range(len(copies)):
        ready(i)
        k = i // 2
        cols = slice((i % 2) * ff, (i % 2 + 1) * ff)
        part = jnp.dot(
            x[:, k * GU_ROWS : (k + 1) * GU_ROWS],
            buf[i % buf.shape[0]],
            preferred_element_type=F32,
        )
        if k == 0:
            acc_out[:, cols] = acc_in[:, cols] + part if has_acc else part
        else:
            acc_out[:, cols] += part
        freed(i)


def rest_body(planes, nears, downs, own, xs, near, far, acc_in, h, *refs):
    near_refs, refs = refs[: len(nears)], refs[len(nears) :]
    down_refs, refs = refs[: len(downs)], refs[len(downs) :]
    w_gate, w_up, send, keep, acc, out, buf, sem = refs
    wide = near.shape[1] - EXTRA
    ff = w_gate.shape[1]
    me = here()
    pos = me % CELL
    depth = buf.shape[0]
    copies = gate_up_copies([(pos ^ 3) * wide], w_gate, w_up, buf, sem, wide)
    ready, freed = stream(copies, depth)
    near_w = {}
    for (_, first, n, _), r in zip(nears, near_refs):
        for i in range(n):
            near_w[first + i] = r.at[i]
    down_w = {}
    for (_, first, n, _), r in zip(downs, down_refs):
        for i in range(n):
            down_w[first + i] = r.at[pl.ds(i * DOWN_ROWS, DOWN_ROWS), :]
    for x, streamed in ((near, False), (far, True)):
        for i in range(len(copies)):
            k = i // 2
            cols = slice((i % 2) * ff, (i % 2 + 1) * ff)
            if streamed:
                ready(i)
            w = buf.at[i % depth] if streamed else near_w[i]
            part = jnp.dot(
                x[:, k * GU_ROWS : (k + 1) * GU_ROWS], w[...], preferred_element_type=F32
            )
            if i < 2 and not streamed:
                acc[:, cols] = acc_in[:, cols] + part
            else:
                acc[:, cols] += part
            if streamed:
                freed(i)
    squares = jnp.zeros((near.shape[0], 1), F32)
    for x in (own, xs, near, far):
        extra = x[:, wide : wide + EXTRA].astype(F32)
        squares = squares + extra[:, 0:1] + extra[:, 1:2] + extra[:, 2:3]
    inv = lax.rsqrt(squares / float(wide * CELL) + 1e-05)
    gate = acc[:, :ff] * inv
    hidden = gate / (1.0 + jnp.exp(-gate)) * (acc[:, ff:] * inv)
    hidden = jnp.concatenate(
        [
            hidden[k * 2 * CELL + a * 2 : k * 2 * CELL + a * 2 + 2]
            for a in (0, 2, 1, 3)
            for k in range(planes)
        ],
        axis=0,
    ).astype(BF16)
    for i in range(ff // DOWN_ROWS):
        part = jnp.dot(
            hidden[:, i * DOWN_ROWS : (i + 1) * DOWN_ROWS],
            down_w[i][...],
            preferred_element_type=F32,
        )
        if i == 0:
            out[...] = part
        else:
            out[...] += part
    per = 2 * planes
    for g in range(CELL):

        @pl.when(pos == g)
        def _():
            cols = slice(g * wide, (g + 1) * wide)
            for n, a in enumerate((0, 2, 1, 3)):
                out[n * per : n * per + 2, cols] += h[2 * a : 2 * a + 2]

    half = 2 * per
    other = jnp.where(pos % 2 == 0, out[half:], out[:half])
    mine = jnp.where(pos % 2 == 0, out[:half], out[half:])
    send[...] = other
    keep[...] = mine


def halve_body(mine, got, send, send_low, keep):
    total = mine[...] + got[...]
    half = total.shape[0] // 2
    low = (here() % CELL) // 2 == 0
    other = jnp.where(low, total[half:], total[:half])
    high = other.astype(BF16)
    send[...] = high
    send_low[...] = (other[:2] - high[:2].astype(F32)).astype(BF16)
    keep[...] = jnp.where(low, total[:half], total[half:])


def spread_body(planes, mine, got, got_low, *outs):
    total = mine[...] + got[...].astype(F32)
    outs[0][...] = total[0:2] + got_low[...].astype(F32)
    for k in range(1, planes):
        outs[k][...] = total[2 * k : 2 * k + 2].astype(BF16)


def final_body(mine, *refs):
    total = mine[...]
    for r in refs[:-1]:
        total = total + r[...].astype(F32)
    refs[-1][...] = total.astype(BF16)


def swap(x, k, devices):
    return lax.ppermute(x, "ctx", [(i, i ^ k) for i in range(devices)])


def cells_program(*args):
    return cells_steps(*args)


def cells_steps(
    old_cache,
    new_slot,
    lengths,
    old_angle,
    new_angle,
    queries,
    new_kv,
    resid,
    gain,
    w_gate,
    w_up,
    w_down,
):
    devices = lax.axis_size("ctx")
    planes = devices // CELL
    tok_n, width = old_cache.shape
    requests = lengths.shape[0]
    rows_dev, model = queries.shape
    wide = model // CELL
    key_cols = KVH // CELL * HD
    msg_cols = 2 * wide + 2 * key_cols
    cell_rows = rows_dev * CELL
    all_rows = cell_rows * planes
    ff = w_gate.shape[1]
    w_gate, w_up, w_down = in_hbm(w_gate), in_hbm(w_up), in_hbm(w_down)
    weights = (w_gate, w_up, w_down)
    n_down = ff // DOWN_ROWS
    n_near = 2 * wide // GU_ROWS
    plans = {
        "turn": [("down", 0, 2, model)],
        "warm_q": [("down", 2, 3, model)],
        "scores": [("down", 5, 1, model)],
        "warm_p": [("near", 0, 4, ff)],
        "merge": [("down", 6, n_down - 6, model)],
        "warm_z": [("near", 4, n_near - 4, ff)],
    }
    held = []

    def keep_pieces(name, values):
        held.extend(zip(plans[name], values))

    def warm(name, dep):
        plan = plans[name]
        keep_pieces(
            name,
            call(
                lambda *r: warm_body(plan, *r),
                [hbm()] * 4,
                [],
                (dep, *weights),
                1,
                [pltpu.SemaphoreType.DMA((count_of(plan),))],
                plan,
                8,
            ),
        )

    sources = (
        new_slot[None, :],
        old_cache,
        old_angle.T,
        new_angle.T,
        queries,
        new_kv,
        resid,
        gain[None, :],
    )
    plan = plans["turn"]
    turned = call(
        lambda *r: turn_body(requests, devices, plan, *r),
        [smem()] + [hbm()] * 11,
        [((rows_dev, msg_cols), BF16)] * CELL
        + [((tok_n, 2 * key_cols), BF16)] * CELL
        + [((tok_n // CELL, width + EXTRA), BF16)] * CELL
        + [((1, wide), BF16)],
        (lengths, *[in_hbm(x) for x in sources], *weights),
        10,
        [pltpu.VMEM(x.shape, x.dtype) for x in sources]
        + [pltpu.SemaphoreType.DMA((len(sources),)), pltpu.SemaphoreType.DMA((count_of(plan),))],
        plan,
        8,
    )
    msgs, sends = turned[:CELL], turned[CELL : 2 * CELL]
    relays, own_gain = turned[2 * CELL : 3 * CELL], turned[3 * CELL]
    keep_pieces("turn", turned[3 * CELL + 1 :])
    msgs = [msgs[0]] + [swap(msgs[k], k, devices) for k in range(1, CELL)]
    kvs = [sends[0]] + [swap(sends[k], k, devices) for k in range(1, CELL)]
    cat, own_q = call(
        assemble_body,
        [vmem()] * CELL,
        [((cell_rows, msg_cols), BF16), ((cell_rows, wide), BF16)],
        tuple(msgs),
        4,
    )
    qs = [own_q] + [swap(own_q, CELL * k, devices) for k in range(1, planes)]
    warm("warm_q", own_q)
    relays = [relays[0]] + [swap(relays[k], k, devices) for k in range(1, CELL)]
    plan = plans["scores"]
    parts = call(
        lambda *r: scores_body(requests, planes, plan, *r),
        [smem()] + [vmem()] * (planes + CELL) + [hbm()] * 3,
        [((cell_rows, wide + EXTRA), BF16)] * planes,
        (lengths, *qs, *kvs, *weights),
        10,
        [pltpu.SemaphoreType.DMA((count_of(plan),))],
        plan,
        5,
    )
    keep_pieces("scores", parts[planes:])
    warm("warm_p", parts[0])
    parts = [parts[0]] + [swap(parts[k], CELL * k, devices) for k in range(1, planes)]
    plan = plans["merge"]
    merged = call(
        lambda *r: merge_body(planes, plan, *r),
        [vmem()] * (planes + 2 + CELL) + [hbm()] * 3,
        [((cell_rows, wide + EXTRA), BF16), ((cell_rows, wide), F32)]
        + [((tok_n // planes, width + EXTRA), BF16)] * planes,
        (*parts, cat, own_gain, *relays, *weights),
        6,
        [pltpu.SemaphoreType.DMA((count_of(plan),))],
        plan,
        4,
    )
    normed, hstate = merged[:2]
    relays = merged[2 : 2 + planes]
    keep_pieces("merge", merged[2 + planes :])
    warm("warm_z", normed)
    blocks = [normed] + [swap(normed, CELL * k, devices) for k in range(1, planes)]
    own = jnp.concatenate(blocks, axis=0)
    across = swap(own, 2, devices)
    near = swap(own, 1, devices)
    gu_scratch = [pltpu.VMEM((4, GU_ROWS, ff), BF16), pltpu.SemaphoreType.DMA((4,))]
    acc = call(
        lambda *r: first_gate_up_body(0, False, *r),
        [vmem(), hbm(), hbm()],
        [((all_rows, 2 * ff), F32)],
        (own, w_gate, w_up),
        9,
        gu_scratch,
        moved=14,
    )[0]
    far = swap(across, 1, devices)
    acc = call(
        lambda *r: first_gate_up_body(2, True, *r),
        [vmem(), vmem(), hbm(), hbm()],
        [((all_rows, 2 * ff), F32)],
        (across, acc, w_gate, w_up),
        9,
        gu_scratch,
        moved=14,
    )[0]
    relays = [relays[0]] + [swap(relays[k], CELL * k, devices) for k in range(1, planes)]
    nears = [h for h in held if h[0][0] == "near"]
    downs = [h for h in held if h[0][0] == "down"]
    send, keep = call(
        lambda *r: rest_body(planes, [h[0] for h in nears], [h[0] for h in downs], *r),
        [vmem()] * (6 + len(held)) + [hbm()] * 2,
        [((all_rows // 2, model), F32)] * 2,
        (
            own,
            across,
            near,
            far,
            acc,
            hstate,
            *[in_vmem(h[1]) for h in nears],
            *[in_vmem(h[1]) for h in downs],
            w_gate,
            w_up,
        ),
        10,
        [pltpu.VMEM((all_rows, 2 * ff), F32), pltpu.VMEM((all_rows, model), F32)] + gu_scratch,
        moved=40,
        on_chip=True,
    )
    got = swap(send, 1, devices)
    send, send_low, keep = call(
        lambda *r: halve_body(*r),
        [vmem(), vmem()],
        [((all_rows // 4, model), BF16), ((rows_dev, model), BF16), ((all_rows // 4, model), F32)],
        (in_vmem(keep), got),
        8,
    )
    got = swap(send, 2, devices)
    got_low = swap(send_low, 2, devices)
    pieces = call(
        lambda *r: spread_body(planes, *r),
        [vmem()] * 3,
        [((rows_dev, model), F32)] + [((rows_dev, model), BF16)] * (planes - 1),
        (keep, got, got_low),
        8,
    )
    pieces = [pieces[0]] + [swap(pieces[k], CELL * k, devices) for k in range(1, planes)]
    layer_out = call(
        final_body, [vmem()] * planes, [((rows_dev, model), BF16)], tuple(pieces), 8
    )[0]
    new_cache = call(
        place_body, [vmem()] * planes, [((CTOK_DEV, width), BF16)], tuple(relays), 8, moved=1
    )[0]
    return (new_cache, layer_out)


def rotate_block(block, where_pos, old_angle, new_angle):
    rows_here = block.shape[0]
    half_size = HD // 2
    parts = block.reshape(rows_here, 2, KVH, HD)
    keys = parts[:, 0].astype(jnp.float32)
    delta = jnp.take(new_angle, where_pos, axis=0) - jnp.take(old_angle, where_pos, axis=0)
    cosine = jnp.cos(delta)[:, None, :]
    sine = jnp.sin(delta)[:, None, :]
    first = keys[..., :half_size]
    second = keys[..., half_size:]
    turned = jnp.concatenate(
        [first * cosine - second * sine, second * cosine + first * sine], axis=-1
    ).astype(jnp.bfloat16)
    return jnp.stack([turned, parts[:, 1]], axis=1).reshape(rows_here, 2 * KVH * HD)


def general_program(
    old_cache,
    new_slot,
    lengths,
    old_angle,
    new_angle,
    queries,
    new_kv,
    resid,
    gain,
    w_gate,
    w_up,
    w_down,
):
    devices = lax.axis_size("ctx")
    own_index = lax.axis_index("ctx")
    slot_count = old_cache.shape[0]
    row_width = old_cache.shape[1]
    per_peer = slot_count // devices
    rows_dev = queries.shape[0]
    all_rows = rows_dev * devices
    group_size = QH // KVH
    high = lax.Precision.HIGHEST
    scale = 1.0 / float(HD) ** 0.5
    tokens = own_index * slot_count + jnp.arange(slot_count, dtype=jnp.int32)
    row_ends = jnp.cumsum(lengths)
    passed = row_ends[None, :] <= tokens[:, None]
    owner_row = jnp.minimum(jnp.sum(passed.astype(jnp.int32), axis=1), lengths.shape[0] - 1)
    row_prior = jnp.sum(jnp.where(passed, lengths[None, :], 0), axis=1)
    position = jnp.clip(tokens - row_prior, 0, old_angle.shape[0] - 1)
    filled = new_slot >= 0
    all_queries = lax.all_gather(queries, "ctx", axis=0, tiled=True)
    target = jnp.where(
        filled, new_slot // CTOK_DEV, jnp.arange(slot_count, dtype=jnp.int32) // per_peer
    )
    sorted_order = jnp.argsort(target, stable=True)
    new_place = jnp.where(filled, new_slot % CTOK_DEV, -1)
    slot_info = jnp.stack([new_place, owner_row, position], axis=1)[sorted_order]
    sent_rows = old_cache[sorted_order].reshape(devices, per_peer, row_width)
    got_rows = lax.all_to_all(sent_rows, "ctx", split_axis=0, concat_axis=0, tiled=True)
    got_info = lax.all_to_all(
        slot_info.reshape(devices, per_peer, 3), "ctx", split_axis=0, concat_axis=0, tiled=True
    )
    got_rows = got_rows.reshape(slot_count, row_width)
    got_info = got_info.reshape(slot_count, 3)
    landing = jnp.where(got_info[:, 0] >= 0, got_info[:, 0], CTOK_DEV)
    placed = jnp.zeros((CTOK_DEV, row_width), jnp.bfloat16).at[landing].set(got_rows, mode="drop")
    placed_row = jnp.zeros((CTOK_DEV,), jnp.int32).at[landing].set(got_info[:, 1], mode="drop")
    placed_pos = jnp.zeros((CTOK_DEV,), jnp.int32).at[landing].set(got_info[:, 2], mode="drop")
    placed, moved_row, moved_pos = (placed, placed_row, placed_pos)
    new_cache = rotate_block(placed, moved_pos, old_angle, new_angle)
    key_count = new_cache.shape[0]
    key_split = new_cache.reshape(key_count, 2, KVH, HD)
    value_four = key_split[:, 1].astype(jnp.float32)
    query_four = all_queries.reshape(all_rows, KVH, group_size, HD)
    scores = (
        jnp.einsum(
            "mjge,cje->mjgc", query_four, key_split[:, 0], preferred_element_type=jnp.float32
        )
        * scale
    )
    query_row = jnp.arange(all_rows, dtype=jnp.int32) // (2 * SAMPLES)
    matching = query_row[:, None] == moved_row[None, :]
    scores = jnp.where(matching[:, None, None, :], scores, -1e30)
    local_top = jnp.max(scores, axis=-1)
    own_query = queries.reshape(rows_dev, KVH, group_size, HD).astype(jnp.float32)
    fresh_kv = jnp.repeat(new_kv.reshape(rows_dev // 2, 2, 2, KVH, HD), 2, axis=0).astype(
        jnp.float32
    )
    own_steps = (
        jnp.arange(2, dtype=jnp.int32)[None, :]
        <= (jnp.arange(rows_dev, dtype=jnp.int32) % 2)[:, None]
    )
    own_scores = jnp.einsum("mjge,msje->mjgs", own_query, fresh_kv[:, :, 0], precision=high) * scale
    own_scores = jnp.where(own_steps[:, None, None, :], own_scores, -1e30)
    own_top = jnp.max(own_scores, axis=-1)
    floor_top = jnp.maximum(local_top, -10000.0)
    weights_local = jnp.exp(scores - floor_top[..., None])
    summed = jnp.einsum("mjgc,cje->mjge", weights_local, value_four, precision=high)
    totals = jnp.sum(weights_local, axis=-1)
    got_sums, got_totals, got_tops = (
        lax.all_to_all(
            summed.reshape(devices, rows_dev, QH * HD),
            "ctx",
            split_axis=0,
            concat_axis=0,
            tiled=True,
        ),
        lax.all_to_all(
            totals.reshape(devices, rows_dev, QH), "ctx", split_axis=0, concat_axis=0, tiled=True
        ),
        lax.all_to_all(
            floor_top.reshape(devices, rows_dev, QH), "ctx", split_axis=0, concat_axis=0, tiled=True
        ),
    )
    got_tops = got_tops.reshape(devices, rows_dev, KVH, group_size)
    row_top = jnp.maximum(jnp.max(got_tops, axis=0), own_top)
    rescale = jnp.exp(got_tops - row_top[None])
    weights_own = jnp.exp(own_scores - row_top[..., None])
    row_sums = jnp.sum(
        rescale[..., None] * got_sums.reshape(devices, rows_dev, KVH, group_size, HD), axis=0
    )
    row_sums = row_sums + jnp.einsum(
        "mjgs,msje->mjge", weights_own, fresh_kv[:, :, 1], precision=high
    )
    row_totals = jnp.sum(
        rescale * got_totals.reshape(devices, rows_dev, KVH, group_size), axis=0
    ) + jnp.sum(weights_own, axis=-1)
    attn = (row_sums / row_totals[..., None]).reshape(rows_dev, QH * HD)
    hstate = resid.astype(jnp.float32) + attn
    normed = (
        hstate
        * lax.rsqrt(jnp.mean(hstate * hstate, axis=-1, keepdims=True) + 1e-05)
        * gain.astype(jnp.float32)
    ).astype(jnp.bfloat16)
    piece = lax.all_gather(normed, "ctx", axis=0, tiled=True)
    gate_out = jnp.dot(piece, w_gate, preferred_element_type=jnp.float32)
    up_out = jnp.dot(piece, w_up, preferred_element_type=jnp.float32)
    hidden_all = (jax.nn.silu(gate_out) * up_out).astype(jnp.bfloat16)
    ffn_out = lax.psum_scatter(
        jnp.dot(hidden_all, w_down, preferred_element_type=jnp.float32),
        "ctx",
        scatter_dimension=0,
        tiled=True,
    )
    layer_out = (hstate + ffn_out).astype(jnp.bfloat16)
    return (new_cache, layer_out)


def solution(mesh):
    per_device = cells_program if mesh.shape["ctx"] == 4 * CELL else general_program
    return jax.shard_map(
        per_device,
        mesh=mesh,
        in_specs=(
            P(("groups", "ctx"), None),
            P(("groups", "ctx")),
            P("groups"),
            P(),
            P(),
            P(("groups", "ctx"), None),
            P(("groups", "ctx"), None),
            P(("groups", "ctx"), None),
            P(),
            P(None, "ctx"),
            P(None, "ctx"),
            P("ctx", None),
        ),
        out_specs=(P(("groups", "ctx"), None), P(("groups", "ctx"), None)),
        check_vma=False,
    )
```

profile of v0, /device:TPU:0, one launch (start us, length us, event | category | flops | bytes accessed | tf_op | source)
XLA Modules:
  0.0 116.0 jit_solution(18441988517864575102)
XLA Ops:
  0.6 1.4 %broadcast_in_dim.7.r_8_ = bf16[1,8192]{1,0:T(2,128)(2,1)} reshape(bf16[8192]{0:T(1024)(128)(2,1)} %param.20) | data formatting | bytes 32768 | tf_op jit(solution)/shard_map/broadcast_in_dim | solution.py:614
  2.6 5.8 %shard_map.131 = (bf16[2,4608]{1,0:T(2,128)(2,1)S(1)}, bf16[2,4608]{1,0:T(2,128)(2,1)S(1)}, bf16[2,4608]{1,0:T(2,128)(2,1)S(1)}, bf16[2,4608]{1,0:T(2,128)(2,1)S...) custom-call(s32[4]{0:T(128)S(1)} %copy-done.1, ...), custom_call_target="tpu_custom_call" | custom-call | bytes 8388608 | tf_op jit(solution)/shard_map/pallas_call | solution.py:43
  9.1 2.9 %collective-permute-start.1 = (bf16[2,4608]{1,0:T(2,128)(2,1)S(1)}, bf16[2,4608]{1,0:T(2,128)(2,1)S(1)}, u32[]{:S(2)}, u32[]{:S(2)}) collective-permute-start(bf16[2,4608]{1,0:T(2,128)(2,1)S(1)} %get-tuple-element.41), channel_id=1, source_target_pairs={{0,2},{1,3},{2,0},{3,1},{4,6},{5,7},{6,4},{7,5},{8,10},{9,11},{10,... | collective-permute-start | bytes 55304 | tf_op jit(solution)/shard_map/ppermute | solution.py:541
  12.0 1.7 %collective-permute-done.1.refs_2_ = bf16[2,4608]{1,0:T(2,128)(2,1)S(1)} collective-permute-done((bf16[2,4608]{1,0:T(2,128)(2,1)S(1)}, bf16[2,4608]{1,0:T(2,128)(2,1)S(1)}, u32[]{:S(2)}, u32[]{:S(2)}) %collective-permute-start.1) | collective-permute-done | bytes 18464 | tf_op jit(solution)/shard_map/ppermute | solution.py:541
  13.7 1.6 %collective-permute-done.2.refs_3_ = bf16[2,4608]{1,0:T(2,128)(2,1)S(1)} collective-permute-done((bf16[2,4608]{1,0:T(2,128)(2,1)S(1)}, bf16[2,4608]{1,0:T(2,128)(2,1)S(1)}, u32[]{:S(2)}, u32[]{:S(2)}) %collective-permute-start.2) | collective-permute-done | bytes 18464 | tf_op jit(solution)/shard_map/ppermute | solution.py:541
  15.4 3.7 %collective-permute-start.5 = (bf16[8,2048]{1,0:T(8,128)(2,1)S(1)}, bf16[8,2048]{1,0:T(8,128)(2,1)S(1)}, u32[]{:S(2)}, u32[]{:S(2)}) collective-permute-start(bf16[8,2048]{1,0:T(8,128)(2,1)S(1)} %get-tuple-element.43.r_1_.r_0_), channel_id=1, source_target_pairs={{0,12},{1,13},{2,14},{3,15},{4,8},{5,9},{6,10},{7,11},{8,4},{9,5},... | collective-permute-start | bytes 98312 | tf_op jit(solution)/shard_map/ppermute | solution.py:541
  19.9 1.3 %collective-permute-done.5.r_4_ = bf16[8,2048]{1,0:T(8,128)(2,1)S(1)} collective-permute-done((bf16[8,2048]{1,0:T(8,128)(2,1)S(1)}, bf16[8,2048]{1,0:T(8,128)(2,1)S(1)}, u32[]{:S(2)}, u32[]{:S(2)}) %collective-permute-start.5) | collective-permute-done | bytes 32800 | tf_op jit(solution)/shard_map/ppermute | solution.py:541
  21.6 2.3 %collective-permute-done.4.r_3_ = bf16[8,2048]{1,0:T(8,128)(2,1)S(1)} collective-permute-done((bf16[8,2048]{1,0:T(8,128)(2,1)S(1)}, bf16[8,2048]{1,0:T(8,128)(2,1)S(1)}, u32[]{:S(2)}, u32[]{:S(2)}) %collective-permute-start.4) | collective-permute-done | bytes 32800 | tf_op jit(solution)/shard_map/ppermute | solution.py:541
  24.6 1.4 %collective-permute-start.14 = (bf16[32,2176]{1,0:T(8,128)(2,1)S(1)}, bf16[32,2176]{1,0:T(8,128)(2,1)S(1)}, u32[]{:S(2)}, u32[]{:S(2)}) collective-permute-start(bf16[32,2176]{1,0:T(8,128)(2,1)S(1)} %get-tuple-element.57), channel_id=1, source_target_pairs={{0,3},{1,2},{2,1},{3,0},{4,7},{5,6},{6,5},{7,4},{8,11},{9,10},{10,... | collective-permute-start | bytes 417800 | tf_op jit(solution)/shard_map/ppermute | solution.py:541
  26.2 3.5 %collective-permute-done.8.r_8_ = bf16[128,512]{1,0:T(8,128)(2,1)S(1)} collective-permute-done((bf16[128,512]{1,0:T(8,128)(2,1)S(1)}, bf16[128,512]{1,0:T(8,128)(2,1)S(1)}, u32[]{:S(2)}, u32[]{:S(2)}) %collective-permute-start.8) | collective-permute-done | bytes 131104 | tf_op jit(solution)/shard_map/ppermute | solution.py:541
  29.7 3.5 %shard_map.133 = (bf16[8,2176]{1,0:T(8,128)(2,1)S(1)}, bf16[8,2176]{1,0:T(8,128)(2,1)S(1)}, bf16[8,2176]{1,0:T(8,128)(2,1)S(1)}, bf16[8,2176]{1,0:T(8,128)(2,1)S(1)}, bf16[256,8192]{1,0:T(8,128)(2,1)S(1)}) custom-call(s32[4]{0:T(128)S(1)} %copy-done.1, bf16[8,2048]{1,0:T(8,128)(2,1)S(1)} %get-tuple-element.43.r_1_.r_0_, ...), custom_call_target="tpu_custom_call" | custom-call | bytes 5242880 | tf_op jit(solution)/shard_map/pallas_call | solution.py:43
  33.3 2.4 %collective-permute-start.10 = (bf16[8,2176]{1,0:T(8,128)(2,1)S(1)}, bf16[8,2176]{1,0:T(8,128)(2,1)S(1)}, u32[]{:S(2)}, u32[]{:S(2)}) collective-permute-start(bf16[8,2176]{1,0:T(8,128)(2,1)S(1)} %get-tuple-element.50), channel_id=1, source_target_pairs={{0,8},{1,9},{2,10},{3,11},{4,12},{5,13},{6,14},{7,15},{8,0},{9,1},... | collective-permute-start | bytes 104456 | tf_op jit(solution)/shard_map/ppermute | solution.py:541
  35.7 2.0 %collective-permute-start.11 = (bf16[8,2176]{1,0:T(8,128)(2,1)S(1)}, bf16[8,2176]{1,0:T(8,128)(2,1)S(1)}, u32[]{:S(2)}, u32[]{:S(2)}) collective-permute-start(bf16[8,2176]{1,0:T(8,128)(2,1)S(1)} %get-tuple-element.51), channel_id=1, source_target_pairs={{0,12},{1,13},{2,14},{3,15},{4,8},{5,9},{6,10},{7,11},{8,4},{9,5},... | collective-permute-start | bytes 104456 | tf_op jit(solution)/shard_map/ppermute | solution.py:541
  38.2 3.2 %collective-permute-done.11.r_3_ = bf16[8,2176]{1,0:T(8,128)(2,1)S(1)} collective-permute-done((bf16[8,2176]{1,0:T(8,128)(2,1)S(1)}, bf16[8,2176]{1,0:T(8,128)(2,1)S(1)}, u32[]{:S(2)}, u32[]{:S(2)}) %collective-permute-start.11) | collective-permute-done | bytes 34848 | tf_op jit(solution)/shard_map/ppermute | solution.py:541
  41.4 2.9 %shard_map.134 = (bf16[8,2176]{1,0:T(8,128)(2,1)S(1)}, f32[8,2048]{1,0:T(8,128)S(1)}, bf16[32,2176]{1,0:T(8,128)(2,1)S(1)}, bf16[32,2176]{1,0:T(8,128)(2,1)S(1)}...) custom-call(bf16[8,2176]{1,0:T(8,128)(2,1)S(1)} %get-tuple-element.48.r_0_, ...), custom_call_target="tpu_custom_call" | custom-call | bytes 4194304 | tf_op jit(solution)/shard_map/pallas_call | solution.py:43
  44.3 2.1 %collective-permute-start.20 = (bf16[8,2176]{1,0:T(8,128)(2,1)S(1)}, bf16[8,2176]{1,0:T(8,128)(2,1)S(1)}, u32[]{:S(2)}, u32[]{:S(2)}) collective-permute-start(bf16[8,2176]{1,0:T(8,128)(2,1)S(1)} %get-tuple-element.62.r_0_), channel_id=1, source_target_pairs={{0,12},{1,13},{2,14},{3,15},{4,8},{5,9},{6,10},{7,11},{8,4},{9,5},... | collective-permute-start | bytes 104456 | tf_op jit(solution)/shard_map/ppermute | solution.py:541
  46.4 2.4 %collective-permute-start.18 = (bf16[8,2176]{1,0:T(8,128)(2,1)S(1)}, bf16[8,2176]{1,0:T(8,128)(2,1)S(1)}, u32[]{:S(2)}, u32[]{:S(2)}) collective-permute-start(bf16[8,2176]{1,0:T(8,128)(2,1)S(1)} %get-tuple-element.62.r_0_), channel_id=1, source_target_pairs={{0,4},{1,5},{2,6},{3,7},{4,0},{5,1},{6,2},{7,3},{8,12},{9,13},{10,... | collective-permute-start | bytes 104456 | tf_op jit(solution)/shard_map/ppermute | solution.py:541
  48.8 2.0 %collective-permute-done.18 = bf16[8,2176]{1,0:T(8,128)(2,1)S(1)} collective-permute-done((bf16[8,2176]{1,0:T(8,128)(2,1)S(1)}, bf16[8,2176]{1,0:T(8,128)(2,1)S(1)}, u32[]{:S(2)}, u32[]{:S(2)}) %collective-permute-start.18) | collective-permute-done | bytes 34848 | tf_op jit(solution)/shard_map/ppermute | solution.py:541
  52.7 3.8 %collective-permute-done.21.r_0_.r_1_ = bf16[32,2176]{1,0:T(8,128)(2,1)S(1)} collective-permute-done((bf16[32,2176]{1,0:T(8,128)(2,1)S(1)}, bf16[32,2176]{1,0:T(8,128)(2,1)S(1)}, u32[]{:S(2)}, u32[]{:S(2)}) %collective-permute-start.21) | collective-permute-done | bytes 139296 | tf_op jit(solution)/shard_map/ppermute | solution.py:541
  56.6 4.7 %shard_map.140.r_9_ = bf16[768,8192]{1,0:T(8,128)(2,1)S(1)} custom-call(bf16[8,2048]{1,0:T(8,128)(2,1)S(1)} %get-tuple-element.43.r_1_.r_0_, bf16[8192,1792]{1,0:T(8,128)(2,1)} %r_12_.3, bf16[8192,1792]{1,0:T(8,128)(2,1)} %r_13_.1, bf16[1792,8192]{1,0:T(8,128)(2,1)} %r_3_.7), custom_call_target="tpu_custom_call" | custom-call | bytes 8388608 | tf_op jit(solution)/shard_map/pallas_call | solution.py:43
  61.3 3.2 %shard_map.138.r_6_ = bf16[4,512,1792]{2,1,0:T(8,128)(2,1)S(1)} custom-call(bf16[8,2176]{1,0:T(8,128)(2,1)S(1)} %get-tuple-element.48.r_0_, bf16[8192,1792]{1,0:T(8,128)(2,1)} %r_12_.3, bf16[8192,1792]{1,0:T(8,128)(2,1)} %r_13_.1, bf16[1792,8192]{1,0:T(8,128)(2,1)} %r_3_.7), custom_call_target="tpu_custom_call" | custom-call | bytes 8388608 | tf_op jit(solution)/shard_map/pallas_call | solution.py:43
  64.5 3.2 %shard_map.139.r_7_ = bf16[4,512,1792]{2,1,0:T(8,128)(2,1)S(1)} custom-call(bf16[8,2176]{1,0:T(8,128)(2,1)S(1)} %get-tuple-element.62.r_0_, bf16[8192,1792]{1,0:T(8,128)(2,1)} %r_12_.3, bf16[8192,1792]{1,0:T(8,128)(2,1)} %r_13_.1, bf16[1792,8192]{1,0:T(8,128)(2,1)} %r_3_.7), custom_call_target="tpu_custom_call" | custom-call | bytes 8388608 | tf_op jit(solution)/shard_map/pallas_call | solution.py:43
  67.7 6.0 %shard_map.136.r_1_ = f32[32,3584]{1,0:T(8,128)S(1)} custom-call(bf16[32,2176]{1,0:T(8,128)(2,1)S(1)} %constant_dynamic-update-slice_fusion.r_0_, bf16[8192,1792]{1,0:T(8,128)(2,1)} %r_12_.3, bf16[8192,1792]{1,0:T(8,128)(2,1)} %r_13_.1), custom_call_target="tpu_custom_call" | custom-call | bytes 14680064 | tf_op jit(solution)/shard_map/pallas_call | solution.py:43
  73.6 6.0 %shard_map.137.r_4_ = f32[32,3584]{1,0:T(8,128)S(1)} custom-call(bf16[32,2176]{1,0:T(8,128)(2,1)S(1)} %collective-permute-done.21.r_0_.r_1_, f32[32,3584]{1,0:T(8,128)S(1)} %shard_map.136.r_1_, bf16[8192,1792]{1,0:T(8,128)(2,1)} %r_12_.3, bf16[8192,1792]{1,0:T(8,128)(2,1)} %r_13_.1), custom_call_target="tpu_custom_call" | custom-call | bytes 14680064 | tf_op jit(solution)/shard_map/pallas_call | solution.py:43
  80.4 13.4 %shard_map.141 = (f32[16,8192]{1,0:T(8,128)S(1)}, f32[16,8192]{1,0:T(8,128)S(1)}) custom-call(bf16[32,2176]{1,0:T(8,128)(2,1)S(1)} %constant_dynamic-update-slice_fusion.r_0_, bf16[32,2176]{1,0:T(8,128)(2,1)S(1)} %collective-permute-done.21.r_0_.r_1_, bf16[32,2176]{1,0:T(8,128)(2,1)S(1)} %collective-permute-done.22.r_2_, ...), custom_call_target="tpu_custom_call" | custom-call | bytes 41943040 | tf_op jit(solution)/shard_map/pallas_call | solution.py:43
  96.1 1.7 %collective-permute-start.25 = (bf16[8,8192]{1,0:T(8,128)(2,1)S(1)}, bf16[8,8192]{1,0:T(8,128)(2,1)S(1)}, u32[]{:S(2)}, u32[]{:S(2)}) collective-permute-start(bf16[8,8192]{1,0:T(8,128)(2,1)S(1)} %get-tuple-element.70), channel_id=1, source_target_pairs={{0,2},{1,3},{2,0},{3,1},{4,6},{5,7},{6,4},{7,5},{8,10},{9,11},{10,... | collective-permute-start | bytes 393224 | tf_op jit(solution)/shard_map/ppermute | solution.py:541
  98.7 3.0 %collective-permute-start.17 = (bf16[32,2176]{1,0:T(8,128)(2,1)S(1)}, bf16[32,2176]{1,0:T(8,128)(2,1)S(1)}, u32[]{:S(2)}, u32[]{:S(2)}) collective-permute-start(bf16[32,2176]{1,0:T(8,128)(2,1)S(1)} %get-tuple-element.61), channel_id=1, source_target_pairs={{0,12},{1,13},{2,14},{3,15},{4,8},{5,9},{6,10},{7,11},{8,4},{9,5},... | collective-permute-start | bytes 417800 | tf_op jit(solution)/shard_map/ppermute | solution.py:541
  101.9 3.8 %collective-permute-done.26.r_2_ = bf16[2,8192]{1,0:T(2,128)(2,1)S(1)} collective-permute-done((bf16[2,8192]{1,0:T(2,128)(2,1)S(1)}, bf16[2,8192]{1,0:T(2,128)(2,1)S(1)}, u32[]{:S(2)}, u32[]{:S(2)}) %collective-permute-start.26) | collective-permute-done | bytes 32800 | tf_op jit(solution)/shard_map/ppermute | solution.py:541
  105.8 1.4 %collective-permute-start.28 = (bf16[2,8192]{1,0:T(2,128)(2,1)S(1)}, bf16[2,8192]{1,0:T(2,128)(2,1)S(1)}, u32[]{:S(2)}, u32[]{:S(2)}) collective-permute-start(bf16[2,8192]{1,0:T(2,128)(2,1)S(1)} %get-tuple-element.74), channel_id=1, source_target_pairs={{0,8},{1,9},{2,10},{3,11},{4,12},{5,13},{6,14},{7,15},{8,0},{9,1},... | collective-permute-start | bytes 98312 | tf_op jit(solution)/shard_map/ppermute | solution.py:541
  107.1 3.0 %collective-permute-start.29 = (bf16[2,8192]{1,0:T(2,128)(2,1)S(1)}, bf16[2,8192]{1,0:T(2,128)(2,1)S(1)}, u32[]{:S(2)}, u32[]{:S(2)}) collective-permute-start(bf16[2,8192]{1,0:T(2,128)(2,1)S(1)} %get-tuple-element.75), channel_id=1, source_target_pairs={{0,12},{1,13},{2,14},{3,15},{4,8},{5,9},{6,10},{7,11},{8,4},{9,5},... | collective-permute-start | bytes 98312 | tf_op jit(solution)/shard_map/ppermute | solution.py:541
  110.2 2.1 %collective-permute-done.16.refs_2_ = bf16[32,2176]{1,0:T(8,128)(2,1)S(1)} collective-permute-done((bf16[32,2176]{1,0:T(8,128)(2,1)S(1)}, bf16[32,2176]{1,0:T(8,128)(2,1)S(1)}, u32[]{:S(2)}, u32[]{:S(2)}) %collective-permute-start.16) | collective-permute-done | bytes 139296 | tf_op jit(solution)/shard_map/ppermute | solution.py:541
  113.2 2.1 %collective-permute-done.28.refs_1_ = bf16[2,8192]{1,0:T(2,128)(2,1)S(1)} collective-permute-done((bf16[2,8192]{1,0:T(2,128)(2,1)S(1)}, bf16[2,8192]{1,0:T(2,128)(2,1)S(1)}, u32[]{:S(2)}, u32[]{:S(2)}) %collective-permute-start.28) | collective-permute-done | bytes 32800 | tf_op jit(solution)/shard_map/ppermute | solution.py:541
  (51 shorter events, 11.8 us)
Async XLA Ops:
  2.0 0.7 copy-start.1
  8.4 16.1 %collective-permute-start.6 = (bf16[128,512]{1,0:T(8,128)(2,1)S(1)}, bf16[128,512]{1,0:T(8,128)(2,1)S(1)}, u32[]{:S(2)}, u32[]{:S(2)}) collective-permute-start(bf16[128,512]{1,0:T(8,128)(2,1)S(1)} %get-tuple-element.45), channel_id=1, source_target_pairs={{0,1},{1,0},{2,3},{3,2},{4,5},{5,4},{6,7},{7,6},{8,9},{9,8},{10,11... | collective-permute-start | bytes 393224 | tf_op jit(solution)/shard_map/ppermute | solution.py:541
  9.0 3.0 %collective-permute-start = (bf16[2,4608]{1,0:T(2,128)(2,1)S(1)}, bf16[2,4608]{1,0:T(2,128)(2,1)S(1)}, u32[]{:S(2)}, u32[]{:S(2)}) collective-permute-start(bf16[2,4608]{1,0:T(2,128)(2,1)S(1)} %get-tuple-element.40), channel_id=1, source_target_pairs={{0,1},{1,0},{2,3},{3,2},{4,5},{5,4},{6,7},{7,6},{8,9},{9,8},{10,11... | collective-permute-start | bytes 55304 | tf_op jit(solution)/shard_map/ppermute | solution.py:541
  9.1 4.6 %collective-permute-start.1 = (bf16[2,4608]{1,0:T(2,128)(2,1)S(1)}, bf16[2,4608]{1,0:T(2,128)(2,1)S(1)}, u32[]{:S(2)}, u32[]{:S(2)}) collective-permute-start(bf16[2,4608]{1,0:T(2,128)(2,1)S(1)} %get-tuple-element.41), channel_id=1, source_target_pairs={{0,2},{1,3},{2,0},{3,1},{4,6},{5,7},{6,4},{7,5},{8,10},{9,11},{10,... | collective-permute-start | bytes 55304 | tf_op jit(solution)/shard_map/ppermute | solution.py:541
  12.0 3.4 %collective-permute-start.2 = (bf16[2,4608]{1,0:T(2,128)(2,1)S(1)}, bf16[2,4608]{1,0:T(2,128)(2,1)S(1)}, u32[]{:S(2)}, u32[]{:S(2)}) collective-permute-start(bf16[2,4608]{1,0:T(2,128)(2,1)S(1)} %get-tuple-element.42), channel_id=1, source_target_pairs={{0,3},{1,2},{2,1},{3,0},{4,7},{5,6},{6,5},{7,4},{8,11},{9,10},{10,... | collective-permute-start | bytes 55304 | tf_op jit(solution)/shard_map/ppermute | solution.py:541
  15.4 5.8 %collective-permute-start.5 = (bf16[8,2048]{1,0:T(8,128)(2,1)S(1)}, bf16[8,2048]{1,0:T(8,128)(2,1)S(1)}, u32[]{:S(2)}, u32[]{:S(2)}) collective-permute-start(bf16[8,2048]{1,0:T(8,128)(2,1)S(1)} %get-tuple-element.43.r_1_.r_0_), channel_id=1, source_target_pairs={{0,12},{1,13},{2,14},{3,15},{4,8},{5,9},{6,10},{7,11},{8,4},{9,5},... | collective-permute-start | bytes 98312 | tf_op jit(solution)/shard_map/ppermute | solution.py:541
  19.1 4.8 %collective-permute-start.4 = (bf16[8,2048]{1,0:T(8,128)(2,1)S(1)}, bf16[8,2048]{1,0:T(8,128)(2,1)S(1)}, u32[]{:S(2)}, u32[]{:S(2)}) collective-permute-start(bf16[8,2048]{1,0:T(8,128)(2,1)S(1)} %get-tuple-element.43.r_1_.r_0_), channel_id=1, source_target_pairs={{0,8},{1,9},{2,10},{3,11},{4,12},{5,13},{6,14},{7,15},{8,0},{9,1},... | collective-permute-start | bytes 98312 | tf_op jit(solution)/shard_map/ppermute | solution.py:541
  19.1 16.6 %collective-permute-start.12 = (bf16[32,2176]{1,0:T(8,128)(2,1)S(1)}, bf16[32,2176]{1,0:T(8,128)(2,1)S(1)}, u32[]{:S(2)}, u32[]{:S(2)}) collective-permute-start(bf16[32,2176]{1,0:T(8,128)(2,1)S(1)} %get-tuple-element.55), channel_id=1, source_target_pairs={{0,1},{1,0},{2,3},{3,2},{4,5},{5,4},{6,7},{7,6},{8,9},{9,8},{10,11... | collective-permute-start | bytes 417800 | tf_op jit(solution)/shard_map/ppermute | solution.py:541
  19.1 4.8 %collective-permute-start.3 = (bf16[8,2048]{1,0:T(8,128)(2,1)S(1)}, bf16[8,2048]{1,0:T(8,128)(2,1)S(1)}, u32[]{:S(2)}, u32[]{:S(2)}) collective-permute-start(bf16[8,2048]{1,0:T(8,128)(2,1)S(1)} %get-tuple-element.43.r_1_.r_0_), channel_id=1, source_target_pairs={{0,4},{1,5},{2,6},{3,7},{4,0},{5,1},{6,2},{7,3},{8,12},{9,13},{10,... | collective-permute-start | bytes 98312 | tf_op jit(solution)/shard_map/ppermute | solution.py:541
  21.2 5.0 %collective-permute-start.7 = (bf16[128,512]{1,0:T(8,128)(2,1)S(1)}, bf16[128,512]{1,0:T(8,128)(2,1)S(1)}, u32[]{:S(2)}, u32[]{:S(2)}) collective-permute-start(bf16[128,512]{1,0:T(8,128)(2,1)S(1)} %get-tuple-element.46), channel_id=1, source_target_pairs={{0,2},{1,3},{2,0},{3,1},{4,6},{5,7},{6,4},{7,5},{8,10},{9,11},{10,... | collective-permute-start | bytes 393224 | tf_op jit(solution)/shard_map/ppermute | solution.py:541
  23.9 5.8 %collective-permute-start.8 = (bf16[128,512]{1,0:T(8,128)(2,1)S(1)}, bf16[128,512]{1,0:T(8,128)(2,1)S(1)}, u32[]{:S(2)}, u32[]{:S(2)}) collective-permute-start(bf16[128,512]{1,0:T(8,128)(2,1)S(1)} %get-tuple-element.47), channel_id=1, source_target_pairs={{0,3},{1,2},{2,1},{3,0},{4,7},{5,6},{6,5},{7,4},{8,11},{9,10},{10,... | collective-permute-start | bytes 393224 | tf_op jit(solution)/shard_map/ppermute | solution.py:541
  23.9 13.8 %collective-permute-start.13 = (bf16[32,2176]{1,0:T(8,128)(2,1)S(1)}, bf16[32,2176]{1,0:T(8,128)(2,1)S(1)}, u32[]{:S(2)}, u32[]{:S(2)}) collective-permute-start(bf16[32,2176]{1,0:T(8,128)(2,1)S(1)} %get-tuple-element.56), channel_id=1, source_target_pairs={{0,2},{1,3},{2,0},{3,1},{4,6},{5,7},{6,4},{7,5},{8,10},{9,11},{10,... | collective-permute-start | bytes 417800 | tf_op jit(solution)/shard_map/ppermute | solution.py:541
  24.6 13.1 %collective-permute-start.14 = (bf16[32,2176]{1,0:T(8,128)(2,1)S(1)}, bf16[32,2176]{1,0:T(8,128)(2,1)S(1)}, u32[]{:S(2)}, u32[]{:S(2)}) collective-permute-start(bf16[32,2176]{1,0:T(8,128)(2,1)S(1)} %get-tuple-element.57), channel_id=1, source_target_pairs={{0,3},{1,2},{2,1},{3,0},{4,7},{5,6},{6,5},{7,4},{8,11},{9,10},{10,... | collective-permute-start | bytes 417800 | tf_op jit(solution)/shard_map/ppermute | solution.py:541
  33.2 4.5 %collective-permute-start.9 = (bf16[8,2176]{1,0:T(8,128)(2,1)S(1)}, bf16[8,2176]{1,0:T(8,128)(2,1)S(1)}, u32[]{:S(2)}, u32[]{:S(2)}) collective-permute-start(bf16[8,2176]{1,0:T(8,128)(2,1)S(1)} %get-tuple-element.49), channel_id=1, source_target_pairs={{0,4},{1,5},{2,6},{3,7},{4,0},{5,1},{6,2},{7,3},{8,12},{9,13},{10,... | collective-permute-start | bytes 104456 | tf_op jit(solution)/shard_map/ppermute | solution.py:541
  33.3 4.9 %collective-permute-start.10 = (bf16[8,2176]{1,0:T(8,128)(2,1)S(1)}, bf16[8,2176]{1,0:T(8,128)(2,1)S(1)}, u32[]{:S(2)}, u32[]{:S(2)}) collective-permute-start(bf16[8,2176]{1,0:T(8,128)(2,1)S(1)} %get-tuple-element.50), channel_id=1, source_target_pairs={{0,8},{1,9},{2,10},{3,11},{4,12},{5,13},{6,14},{7,15},{8,0},{9,1},... | collective-permute-start | bytes 104456 | tf_op jit(solution)/shard_map/ppermute | solution.py:541
  35.7 5.7 %collective-permute-start.11 = (bf16[8,2176]{1,0:T(8,128)(2,1)S(1)}, bf16[8,2176]{1,0:T(8,128)(2,1)S(1)}, u32[]{:S(2)}, u32[]{:S(2)}) collective-permute-start(bf16[8,2176]{1,0:T(8,128)(2,1)S(1)} %get-tuple-element.51), channel_id=1, source_target_pairs={{0,12},{1,13},{2,14},{3,15},{4,8},{5,9},{6,10},{7,11},{8,4},{9,5},... | collective-permute-start | bytes 104456 | tf_op jit(solution)/shard_map/ppermute | solution.py:541
  44.3 7.1 %collective-permute-start.20 = (bf16[8,2176]{1,0:T(8,128)(2,1)S(1)}, bf16[8,2176]{1,0:T(8,128)(2,1)S(1)}, u32[]{:S(2)}, u32[]{:S(2)}) collective-permute-start(bf16[8,2176]{1,0:T(8,128)(2,1)S(1)} %get-tuple-element.62.r_0_), channel_id=1, source_target_pairs={{0,12},{1,13},{2,14},{3,15},{4,8},{5,9},{6,10},{7,11},{8,4},{9,5},... | collective-permute-start | bytes 104456 | tf_op jit(solution)/shard_map/ppermute | solution.py:541
  46.4 5.0 %collective-permute-start.19 = (bf16[8,2176]{1,0:T(8,128)(2,1)S(1)}, bf16[8,2176]{1,0:T(8,128)(2,1)S(1)}, u32[]{:S(2)}, u32[]{:S(2)}) collective-permute-start(bf16[8,2176]{1,0:T(8,128)(2,1)S(1)} %get-tuple-element.62.r_0_), channel_id=1, source_target_pairs={{0,8},{1,9},{2,10},{3,11},{4,12},{5,13},{6,14},{7,15},{8,0},{9,1},... | collective-permute-start | bytes 104456 | tf_op jit(solution)/shard_map/ppermute | solution.py:541
  46.4 4.4 %collective-permute-start.18 = (bf16[8,2176]{1,0:T(8,128)(2,1)S(1)}, bf16[8,2176]{1,0:T(8,128)(2,1)S(1)}, u32[]{:S(2)}, u32[]{:S(2)}) collective-permute-start(bf16[8,2176]{1,0:T(8,128)(2,1)S(1)} %get-tuple-element.62.r_0_), channel_id=1, source_target_pairs={{0,4},{1,5},{2,6},{3,7},{4,0},{5,1},{6,2},{7,3},{8,12},{9,13},{10,... | collective-permute-start | bytes 104456 | tf_op jit(solution)/shard_map/ppermute | solution.py:541
  51.4 5.1 %collective-permute-start.21 = (bf16[32,2176]{1,0:T(8,128)(2,1)S(1)}, bf16[32,2176]{1,0:T(8,128)(2,1)S(1)}, u32[]{:S(2)}, u32[]{:S(2)}) collective-permute-start(bf16[32,2176]{1,0:T(8,128)(2,1)S(1)} %constant_dynamic-update-slice_fusion.r_0_), channel_id=1, source_target_pairs={{0,2},{1,3},{2,0},{3,1},{4,6},{5,7},{6,4},{7,5},{8,10},{9,11},{10,... | collective-permute-start | bytes 417800 | tf_op jit(solution)/shard_map/ppermute | solution.py:541
  52.7 27.7 %collective-permute-start.22 = (bf16[32,2176]{1,0:T(8,128)(2,1)S(1)}, bf16[32,2176]{1,0:T(8,128)(2,1)S(1)}, u32[]{:S(2)}, u32[]{:S(2)}) collective-permute-start(bf16[32,2176]{1,0:T(8,128)(2,1)S(1)} %constant_dynamic-update-slice_fusion.r_0_), channel_id=1, source_target_pairs={{0,1},{1,0},{2,3},{3,2},{4,5},{5,4},{6,7},{7,6},{8,9},{9,8},{10,11... | collective-permute-start | bytes 417800 | tf_op jit(solution)/shard_map/ppermute | solution.py:541
  56.6 23.8 %collective-permute-start.23 = (bf16[32,2176]{1,0:T(8,128)(2,1)S(1)}, bf16[32,2176]{1,0:T(8,128)(2,1)S(1)}, u32[]{:S(2)}, u32[]{:S(2)}) collective-permute-start(bf16[32,2176]{1,0:T(8,128)(2,1)S(1)} %collective-permute-done.21.r_0_.r_1_), channel_id=1, source_target_pairs={{0,1},{1,0},{2,3},{3,2},{4,5},{5,4},{6,7},{7,6},{8,9},{9,8},{10,11... | collective-permute-start | bytes 417800 | tf_op jit(solution)/shard_map/ppermute | solution.py:541
  79.6 0.8 copy-start
  93.8 2.1 %collective-permute-start.24 = (f32[16,8192]{1,0:T(8,128)S(1)}, f32[16,8192]{1,0:T(8,128)S(1)}, u32[]{:S(2)}, u32[]{:S(2)}) collective-permute-start(f32[16,8192]{1,0:T(8,128)S(1)} %get-tuple-element.68), channel_id=1, source_target_pairs={{0,1},{1,0},{2,3},{3,2},{4,5},{5,4},{6,7},{7,6},{8,9},{9,8},{10,11... | collective-permute-start | bytes 1572872 | tf_op jit(solution)/shard_map/ppermute | solution.py:541
  94.4 12.7 %collective-permute-start.15 = (bf16[32,2176]{1,0:T(8,128)(2,1)S(1)}, bf16[32,2176]{1,0:T(8,128)(2,1)S(1)}, u32[]{:S(2)}, u32[]{:S(2)}) collective-permute-start(bf16[32,2176]{1,0:T(8,128)(2,1)S(1)} %get-tuple-element.59), channel_id=1, source_target_pairs={{0,4},{1,5},{2,6},{3,7},{4,0},{5,1},{6,2},{7,3},{8,12},{9,13},{10,... | collective-permute-start | bytes 417800 | tf_op jit(solution)/shard_map/ppermute | solution.py:541
  96.1 9.5 %collective-permute-start.25 = (bf16[8,8192]{1,0:T(8,128)(2,1)S(1)}, bf16[8,8192]{1,0:T(8,128)(2,1)S(1)}, u32[]{:S(2)}, u32[]{:S(2)}) collective-permute-start(bf16[8,8192]{1,0:T(8,128)(2,1)S(1)} %get-tuple-element.70), channel_id=1, source_target_pairs={{0,2},{1,3},{2,0},{3,1},{4,6},{5,7},{6,4},{7,5},{8,10},{9,11},{10,... | collective-permute-start | bytes 393224 | tf_op jit(solution)/shard_map/ppermute | solution.py:541
  97.8 14.5 %collective-permute-start.16 = (bf16[32,2176]{1,0:T(8,128)(2,1)S(1)}, bf16[32,2176]{1,0:T(8,128)(2,1)S(1)}, u32[]{:S(2)}, u32[]{:S(2)}) collective-permute-start(bf16[32,2176]{1,0:T(8,128)(2,1)S(1)} %get-tuple-element.60), channel_id=1, source_target_pairs={{0,8},{1,9},{2,10},{3,11},{4,12},{5,13},{6,14},{7,15},{8,0},{9,1},... | collective-permute-start | bytes 417800 | tf_op jit(solution)/shard_map/ppermute | solution.py:541
  98.7 13.6 %collective-permute-start.17 = (bf16[32,2176]{1,0:T(8,128)(2,1)S(1)}, bf16[32,2176]{1,0:T(8,128)(2,1)S(1)}, u32[]{:S(2)}, u32[]{:S(2)}) collective-permute-start(bf16[32,2176]{1,0:T(8,128)(2,1)S(1)} %get-tuple-element.61), channel_id=1, source_target_pairs={{0,12},{1,13},{2,14},{3,15},{4,8},{5,9},{6,10},{7,11},{8,4},{9,5},... | collective-permute-start | bytes 417800 | tf_op jit(solution)/shard_map/ppermute | solution.py:541
  101.7 3.9 %collective-permute-start.26 = (bf16[2,8192]{1,0:T(2,128)(2,1)S(1)}, bf16[2,8192]{1,0:T(2,128)(2,1)S(1)}, u32[]{:S(2)}, u32[]{:S(2)}) collective-permute-start(bf16[2,8192]{1,0:T(2,128)(2,1)S(1)} %get-tuple-element.71), channel_id=1, source_target_pairs={{0,2},{1,3},{2,0},{3,1},{4,6},{5,7},{6,4},{7,5},{8,10},{9,11},{10,... | collective-permute-start | bytes 98312 | tf_op jit(solution)/shard_map/ppermute | solution.py:541
  105.7 7.5 %collective-permute-start.27 = (bf16[2,8192]{1,0:T(2,128)(2,1)S(1)}, bf16[2,8192]{1,0:T(2,128)(2,1)S(1)}, u32[]{:S(2)}, u32[]{:S(2)}) collective-permute-start(bf16[2,8192]{1,0:T(2,128)(2,1)S(1)} %get-tuple-element.73), channel_id=1, source_target_pairs={{0,4},{1,5},{2,6},{3,7},{4,0},{5,1},{6,2},{7,3},{8,12},{9,13},{10,... | collective-permute-start | bytes 98312 | tf_op jit(solution)/shard_map/ppermute | solution.py:541
  105.8 9.6 %collective-permute-start.28 = (bf16[2,8192]{1,0:T(2,128)(2,1)S(1)}, bf16[2,8192]{1,0:T(2,128)(2,1)S(1)}, u32[]{:S(2)}, u32[]{:S(2)}) collective-permute-start(bf16[2,8192]{1,0:T(2,128)(2,1)S(1)} %get-tuple-element.74), channel_id=1, source_target_pairs={{0,8},{1,9},{2,10},{3,11},{4,12},{5,13},{6,14},{7,15},{8,0},{9,1},... | collective-permute-start | bytes 98312 | tf_op jit(solution)/shard_map/ppermute | solution.py:541
  107.1 8.2 %collective-permute-start.29 = (bf16[2,8192]{1,0:T(2,128)(2,1)S(1)}, bf16[2,8192]{1,0:T(2,128)(2,1)S(1)}, u32[]{:S(2)}, u32[]{:S(2)}) collective-permute-start(bf16[2,8192]{1,0:T(2,128)(2,1)S(1)} %get-tuple-element.75), channel_id=1, source_target_pairs={{0,12},{1,13},{2,14},{3,15},{4,8},{5,9},{6,10},{7,11},{8,4},{9,5},... | collective-permute-start | bytes 98312 | tf_op jit(solution)/shard_map/ppermute | solution.py:541
where the time goes:
time: 116 us
  Pallas kernels  50.5 us (44%)
  starting transfers between devices  32.8 us (28%)
  waiting for transfers between devices  29.1 us (25%)
  local copies, waits for them, and re-layouts  2.8 us (2%)
    pallas_call x14, Pallas kernels, call(): pl.pallas_call(body, in_specs=ins, out_specs=[vmem() for _ in shapes], ou...  50.5 us
    ppermute x30, starting transfers between devices, swap(): return lax.ppermute(x, 'ctx', [(i, i ^ k) for i in range(devices)])  32.8 us
    ppermute x30, waiting for transfers between devices, swap(): return lax.ppermute(x, 'ctx', [(i, i ^ k) for i in range(devices)])  29.1 us
  transfers between devices with their start and end apart: 30, of which 15 were waited for; matrix products, arithmetic and copies ran while one was open for 0% of the time, Pallas kernels for 24%

commit v1 on v0

--- a/solution.py
+++ b/solution.py
@@ -20,10 +20,6 @@
     return pl.BlockSpec(memory_space=pltpu.VMEM)
 
 
-def smem():
-    return pl.BlockSpec(memory_space=pltpu.SMEM)
-
-
 def hbm():
     return pl.BlockSpec(memory_space=pl.ANY)
 
@@ -36,17 +32,18 @@
     return pltpu.with_memory_space_constraint(x, pltpu.VMEM)
 
 
-def call(body, ins, outs, args, limit_mib, scratch=(), fetch=(), moved=0, on_chip=False):
+def call(body, ins, outs, args, limit_mib, scratch=(), fetch=(), moved=0, on_chip=False, flags=None):
     kind = pltpu.VMEM if on_chip else jax.ShapeDtypeStruct
     shapes = [kind(s, d) for s, d in outs]
     shapes += [pltpu.VMEM(piece_shape(p), BF16) for p in fetch]
+    extra = {} if flags is None else {"flags": flags}
     return pl.pallas_call(
         body,
         in_specs=ins,
         out_specs=[vmem() for _ in shapes],
         out_shape=shapes,
         scratch_shapes=list(scratch),
-        compiler_params=pltpu.CompilerParams(vmem_limit_bytes=limit_mib << 20),
+        compiler_params=pltpu.CompilerParams(vmem_limit_bytes=limit_mib << 20, **extra),
         cost_estimate=pl.CostEstimate(flops=0, transcendentals=0, bytes_accessed=moved << 20),
     )(*args)
 
@@ -91,6 +88,13 @@
     return (n * DOWN_ROWS, cols) if kind == "down" else (n, GU_ROWS, cols)
 
 
+def gate_up_block(flip, i, w_gate, w_up):
+    wide = w_gate.shape[0] // CELL
+    row = (here() % CELL ^ flip) * wide + i // 2 * GU_ROWS
+    w = w_gate if i % 2 == 0 else w_up
+    return w.at[pl.ds(pl.multiple_of(row, GU_ROWS), GU_ROWS), :]
+
+
 def fetch_copies(fetch, weights, pieces, sem):
     w_gate, w_up, w_down = weights
     copies = []
@@ -100,11 +104,7 @@
                 src = w_down.at[pl.ds((first + i) * DOWN_ROWS, DOWN_ROWS), :]
                 dst = out.at[pl.ds(i * DOWN_ROWS, DOWN_ROWS), :]
             else:
-                wide = w_gate.shape[0] // CELL
-                row = (here() % CELL ^ 1) * wide + (first + i) // 2 * GU_ROWS
-                w = w_gate if (first + i) % 2 == 0 else w_up
-                src = w.at[pl.ds(pl.multiple_of(row, GU_ROWS), GU_ROWS), :]
-                dst = out.at[i]
+                src, dst = gate_up_block(kind, first + i, w_gate, w_up), out.at[i]
             copies.append(pltpu.make_async_copy(src, dst, sem.at[len(copies)]))
     return copies
 
@@ -121,13 +121,40 @@
         c.wait()
 
 
-def turn_body(requests, devices, fetch, scal, *refs):
-    sources, weights, refs = refs[:8], refs[8:11], refs[11:]
-    outs, refs = refs[: 3 * CELL + 1], refs[3 * CELL + 1 :]
-    msgs, sends, relays = outs[:CELL], outs[CELL : 2 * CELL], outs[2 * CELL : 3 * CELL]
-    own_gain = outs[3 * CELL]
+def prep_body(q, kv, res, gain, *refs):
+    msgs, own_gain, sem = refs[:CELL], refs[CELL], refs[CELL + 1]
+    pos = here() % CELL
+    wide, key_cols = q.shape[1] // CELL, kv.shape[1] // (2 * CELL)
+    copies = []
+
+    def move(src, width, first, dst):
+        at = pl.multiple_of(first, HD)
+        src = src.at[:, pl.ds(at, width)]
+        copies.append(pltpu.make_async_copy(src, dst, sem.at[len(copies)]))
+
+    for k in range(CELL):
+        g = pos ^ k
+        half = kv.shape[1] // 2
+        ends = [0, wide, wide + key_cols, wide + 2 * key_cols, 2 * wide + 2 * key_cols]
+        dst = [msgs[k].at[:, a:b] for a, b in zip(ends, ends[1:])]
+        move(q, wide, g * wide, dst[0])
+        move(kv, key_cols, g * key_cols, dst[1])
+        move(kv, key_cols, half + g * key_cols, dst[2])
+        move(res, wide, g * wide, dst[3])
+    rows = own_gain.shape[0]
+    src = gain.at[pl.ds(pl.multiple_of(pos * rows, rows), rows), :]
+    copies.append(pltpu.make_async_copy(src, own_gain, sem.at[len(copies)]))
+    for c in copies:
+        c.start()
+    for c in copies:
+        c.wait()
+
+
+def turn_body(requests, devices, fetch, *refs):
+    sources, weights, refs = refs[:5], refs[5:8], refs[8:]
+    sends, relays, refs = refs[:CELL], refs[CELL : 2 * CELL], refs[2 * CELL :]
     pieces, refs = refs[: len(fetch)], refs[len(fetch) :]
-    locals_, sems, fetch_sem = refs[:8], refs[8], refs[9]
+    locals_, sems, fetch_sem = refs[:5], refs[5], refs[6]
     loads = [pltpu.make_async_copy(a, b, sems.at[i]) for i, (a, b) in enumerate(zip(sources, locals_))]
     for c in loads:
         c.start()
@@ -136,7 +163,16 @@
         c.start()
     for c in loads:
         c.wait()
-    slot, cache, old_angle, new_angle, q, kv, res, gain = locals_
+
+    @pl.when(here() >= 0)
+    def _():
+        turn_steps(requests, devices, *locals_, sends, relays)
+
+    for c in fetched:
+        c.wait()
+
+
+def turn_steps(requests, devices, scal, slot, cache, old_angle, new_angle, sends, relays):
     me = here()
     pos_in_cell = me % CELL
     tok_n, width = cache.shape
@@ -173,15 +209,6 @@
             def _():
                 sends[k][:, :key_cols] = turned[:, g * key_cols : (g + 1) * key_cols]
                 sends[k][:, key_cols:] = turned[:, half + g * key_cols : half + (g + 1) * key_cols]
-                wide = q.shape[1] // CELL
-                msgs[k][:, :wide] = q[:, g * wide : (g + 1) * wide]
-                msgs[k][:, wide : wide + key_cols] = kv[:, g * key_cols : (g + 1) * key_cols]
-                msgs[k][:, wide + key_cols : wide + 2 * key_cols] = kv[
-                    :, half + g * key_cols : half + (g + 1) * key_cols
-                ]
-                msgs[k][:, wide + 2 * key_cols :] = res[:, g * wide : (g + 1) * wide]
-                if k == 0:
-                    own_gain[...] = gain[:, g * wide : (g + 1) * wide]
 
     place = slot[...]
     per_peer = tok_n // devices
@@ -207,9 +234,6 @@
                 relays[k][:, :width] = moved[g * block : (g + 1) * block]
                 relays[k][:, width:] = land_wide[g * block : (g + 1) * block]
 
-    for c in fetched:
-        c.wait()
-
 
 def assemble_body(*refs):
     msgs, cat, query = refs[:CELL], refs[CELL], refs[CELL + 1]
@@ -224,9 +248,8 @@
     query[...] = whole[:, :wide]
 
 
-def place_body(*refs):
-    out = refs[-1]
-    got = jnp.concatenate([r[...] for r in refs[:-1]], axis=0)
+def place_body(mine, far, near, out):
+    got = jnp.concatenate([mine[...], far[: mine.shape[0]], near[...]], axis=0)
     width = out.shape[1]
     rows = got.shape[0]
     land = got[:, width:].astype(F32)[:, :CTOK_DEV]
@@ -237,12 +260,26 @@
     ).astype(BF16)
 
 
-def scores_body(requests, planes, fetch, scal, *refs):
+def scores_body(requests, planes, fetch, lengths, *refs):
     qs, kvs, refs = refs[:planes], refs[planes : planes + CELL], refs[planes + CELL :]
     weights, outs, refs = refs[:3], refs[3 : 3 + planes], refs[3 + planes :]
-    fetched = fetch_copies(fetch, weights, refs[: len(fetch)], refs[-1])
+    scal, sem, fetch_sem = refs[len(fetch) :]
+    load = pltpu.make_async_copy(lengths, scal, sem.at[0])
+    load.start()
+    fetched = fetch_copies(fetch, weights, refs[: len(fetch)], fetch_sem)
     for c in fetched:
         c.start()
+    load.wait()
+
+    @pl.when(here() >= 0)
+    def _():
+        scores_steps(requests, planes, scal, qs, kvs, outs)
+
+    for c in fetched:
+        c.wait()
+
+
+def scores_steps(requests, planes, scal, qs, kvs, outs):
     me = here()
     plane, pos_in_cell = me // CELL, me % CELL
     rows = qs[0].shape[0]
@@ -302,17 +339,38 @@
                 extra = jnp.where(lane == (3 + i) * count + h, totals[i][part], extra)
     for k in range(planes):
         outs[k][:, count * HD :] = extra[k * rows : (k + 1) * rows].astype(BF16)
-    for c in fetched:
-        c.wait()
+
+
+def regroup_body(planes, *refs):
+    moved, (mine, far, near) = refs[:CELL], refs[CELL:]
+    plane = here() // CELL
+    per = moved[0].shape[0] // planes
+    block = CELL * per
+    for out, at, k in ((mine, 0, 0), (far, 0, 2), (far, block, 3), (near, 0, 1)):
+        for g in range(planes):
+
+            @pl.when((plane ^ k) == g)
+            def _():
+                for a in range(CELL):
+                    out[at + a * per : at + (a + 1) * per] = moved[a][g * per : (g + 1) * per]
 
 
 def merge_body(planes, fetch, *refs):
     parts, cat, gain, refs = refs[:planes], *refs[planes : planes + 2], refs[planes + 2 :]
-    moved, weights, refs = refs[:CELL], refs[CELL : CELL + 3], refs[CELL + 3 :]
-    norm_out, h_out, regrouped, refs = *refs[:2], refs[2 : 2 + planes], refs[2 + planes :]
+    weights, norm_out, h_out, refs = refs[:3], *refs[3:5], refs[5:]
     fetched = fetch_copies(fetch, weights, refs[: len(fetch)], refs[-1])
     for c in fetched:
         c.start()
+
+    @pl.when(here() >= 0)
+    def _():
+        merge_steps(parts, cat, gain, norm_out, h_out)
+
+    for c in fetched:
+        c.wait()
+
+
+def merge_steps(parts, cat, gain, norm_out, h_out):
     rows = cat.shape[0]
     wide = norm_out.shape[1] - EXTRA
     count = wide // HD
@@ -365,24 +423,12 @@
         state = cat[:, base : base + HD].astype(F32) + attn
         h_out[:, lanes] = state
         squares = squares + jnp.sum(state * state, axis=1, keepdims=True)
-        norm_out[:, lanes] = (state * gain[:, lanes].astype(F32)).astype(BF16)
+        norm_out[:, lanes] = (state * gain[h : h + 1, :].astype(F32)).astype(BF16)
     pieces = three_parts(squares)
     extra = jnp.zeros((rows, EXTRA), F32)
     for i in range(3):
         extra = jnp.where(lane == i, pieces[i], extra)
     norm_out[:, wide:] = extra.astype(BF16)
-    plane = here() // CELL
-    per = moved[0].shape[0] // planes
-    for k in range(planes):
-        for g in range(planes):
-
-            @pl.when((plane ^ k) == g)
-            def _():
-                for a in range(CELL):
-                    regrouped[k][a * per : (a + 1) * per] = moved[a][g * per : (g + 1) * per]
-
-    for c in fetched:
-        c.wait()
 
 
 def stream(copies, depth):
@@ -399,78 +445,76 @@
     return ready, freed
 
 
-def gate_up_copies(slices, w_gate, w_up, buf, sem, wide):
+def ring_copies(blocks, w_gate, w_up, buf, sem):
     copies = []
-    for first_row in slices:
-        for i in range(wide // GU_ROWS):
-            for w in (w_gate, w_up):
-                slot = len(copies) % buf.shape[0]
-                rows = pl.ds(pl.multiple_of(first_row + i * GU_ROWS, GU_ROWS), GU_ROWS)
-                copies.append(pltpu.make_async_copy(w.at[rows, :], buf.at[slot], sem.at[slot]))
+    for flip, i in blocks:
+        slot = len(copies) % buf.shape[0]
+        src = gate_up_block(flip, i, w_gate, w_up)
+        copies.append(pltpu.make_async_copy(src, buf.at[slot], sem.at[slot]))
     return copies
 
 
-def first_gate_up_body(flip, has_acc, *refs):
+def gate_up_body(flip, fetch, has_acc, *refs):
     if has_acc:
-        x, acc_in, w_gate, w_up, acc_out, buf, sem = refs
+        x, acc_in, held, refs = *refs[:3], refs[3:]
     else:
-        x, w_gate, w_up, acc_out, buf, sem = refs
-    wide = x.shape[1] - EXTRA
+        x, held, acc_in, refs = *refs[:2], None, refs[2:]
+    w_gate, w_up, w_down, acc_out, piece, buf, sem, fetch_sem = refs
     ff = w_gate.shape[1]
-    pos = (here() % CELL) ^ flip
-    copies = gate_up_copies([pos * wide], w_gate, w_up, buf, sem, wide)
+    n_held = held.shape[0]
+    total = 2 * (x.shape[1] - EXTRA) // GU_ROWS
+    copies = ring_copies([(flip, i) for i in range(n_held, total)], w_gate, w_up, buf, sem)
     ready, freed = stream(copies, buf.shape[0])
-    for i in range(len(copies)):
-        ready(i)
+    fetched = fetch_copies(fetch, (w_gate, w_up, w_down), [piece], fetch_sem)
+    for c in fetched:
+        c.start()
+    for i in range(total):
         k = i // 2
         cols = slice((i % 2) * ff, (i % 2 + 1) * ff)
-        part = jnp.dot(
-            x[:, k * GU_ROWS : (k + 1) * GU_ROWS],
-            buf[i % buf.shape[0]],
-            preferred_element_type=F32,
-        )
+        if i >= n_held:
+            ready(i - n_held)
+        w = held[i] if i < n_held else buf[(i - n_held) % buf.shape[0]]
+        part = jnp.dot(x[:, k * GU_ROWS : (k + 1) * GU_ROWS], w, preferred_element_type=F32)
         if k == 0:
             acc_out[:, cols] = acc_in[:, cols] + part if has_acc else part
         else:
             acc_out[:, cols] += part
-        freed(i)
-
-
-def rest_body(planes, nears, downs, own, xs, near, far, acc_in, h, *refs):
-    near_refs, refs = refs[: len(nears)], refs[len(nears) :]
+        if i >= n_held:
+            freed(i - n_held)
+    for c in fetched:
+        c.wait()
+
+
+def rest_body(planes, downs, own, xs, near, far, acc_in, h, held, *refs):
     down_refs, refs = refs[: len(downs)], refs[len(downs) :]
     w_gate, w_up, send, keep, acc, out, buf, sem = refs
     wide = near.shape[1] - EXTRA
     ff = w_gate.shape[1]
-    me = here()
-    pos = me % CELL
+    pos = here() % CELL
     depth = buf.shape[0]
-    copies = gate_up_copies([(pos ^ 3) * wide], w_gate, w_up, buf, sem, wide)
+    n_held = held.shape[0]
+    per = 2 * wide // GU_ROWS
+    blocks = [(1, i) for i in range(per)] + [(3, i) for i in range(per)]
+    copies = ring_copies(blocks[n_held:], w_gate, w_up, buf, sem)
     ready, freed = stream(copies, depth)
-    near_w = {}
-    for (_, first, n, _), r in zip(nears, near_refs):
-        for i in range(n):
-            near_w[first + i] = r.at[i]
     down_w = {}
     for (_, first, n, _), r in zip(downs, down_refs):
         for i in range(n):
             down_w[first + i] = r.at[pl.ds(i * DOWN_ROWS, DOWN_ROWS), :]
-    for x, streamed in ((near, False), (far, True)):
-        for i in range(len(copies)):
-            k = i // 2
-            cols = slice((i % 2) * ff, (i % 2 + 1) * ff)
-            if streamed:
-                ready(i)
-            w = buf.at[i % depth] if streamed else near_w[i]
-            part = jnp.dot(
-                x[:, k * GU_ROWS : (k + 1) * GU_ROWS], w[...], preferred_element_type=F32
-            )
-            if i < 2 and not streamed:
-                acc[:, cols] = acc_in[:, cols] + part
-            else:
-                acc[:, cols] += part
-            if streamed:
-                freed(i)
+    for n, (flip, i) in enumerate(blocks):
+        x = near if flip == 1 else far
+        k = i // 2
+        cols = slice((i % 2) * ff, (i % 2 + 1) * ff)
+        if n >= n_held:
+            ready(n - n_held)
+        w = held[n] if n < n_held else buf[(n - n_held) % depth]
+        part = jnp.dot(x[:, k * GU_ROWS : (k + 1) * GU_ROWS], w, preferred_element_type=F32)
+        if n < 2:
+            acc[:, cols] = acc_in[:, cols] + part
+        else:
+            acc[:, cols] += part
+        if n >= n_held:
+            freed(n - n_held)
     squares = jnp.zeros((near.shape[0], 1), F32)
     for x in (own, xs, near, far):
         extra = x[:, wide : wide + EXTRA].astype(F32)
@@ -486,16 +530,17 @@
         ],
         axis=0,
     ).astype(BF16)
-    for i in range(ff // DOWN_ROWS):
-        part = jnp.dot(
-            hidden[:, i * DOWN_ROWS : (i + 1) * DOWN_ROWS],
-            down_w[i][...],
-            preferred_element_type=F32,
-        )
-        if i == 0:
-            out[...] = part
-        else:
-            out[...] += part
+    step = 1024
+    for n in range(out.shape[1] // step):
+        total = None
+        for i in range(ff // DOWN_ROWS):
+            part = jnp.dot(
+                hidden[:, i * DOWN_ROWS : (i + 1) * DOWN_ROWS],
+                down_w[i][:, n * step : (n + 1) * step],
+                preferred_element_type=F32,
+            )
+            total = part if total is None else total + part
+        out[:, n * step : (n + 1) * step] = total
     per = 2 * planes
     for g in range(CELL):
 
@@ -573,14 +618,13 @@
     w_gate, w_up, w_down = in_hbm(w_gate), in_hbm(w_up), in_hbm(w_down)
     weights = (w_gate, w_up, w_down)
     n_down = ff // DOWN_ROWS
-    n_near = 2 * wide // GU_ROWS
     plans = {
         "turn": [("down", 0, 2, model)],
         "warm_q": [("down", 2, 3, model)],
-        "scores": [("down", 5, 1, model)],
-        "warm_p": [("near", 0, 4, ff)],
-        "merge": [("down", 6, n_down - 6, model)],
-        "warm_z": [("near", 4, n_near - 4, ff)],
+        "scores": [("down", 5, n_down - 5, model)],
+        "merge": [(0, 0, 2, ff)],
+        "gate_up_own": [(2, 0, 2, ff)],
+        "gate_up_x": [(1, 0, 2, ff)],
     }
     held = []
 
@@ -603,35 +647,34 @@
             ),
         )
 
-    sources = (
-        new_slot[None, :],
-        old_cache,
-        old_angle.T,
-        new_angle.T,
-        queries,
-        new_kv,
-        resid,
-        gain[None, :],
-    )
+    sources = (queries, new_kv, resid, gain.reshape(model // HD, HD))
+    prepared = call(
+        prep_body,
+        [hbm()] * 4,
+        [((rows_dev, msg_cols), BF16)] * CELL + [((wide // HD, HD), BF16)],
+        tuple(in_hbm(x) for x in sources),
+        2,
+        [pltpu.SemaphoreType.DMA((4 * CELL + 1,))],
+    )
+    msgs, own_gain = prepared[:CELL], prepared[CELL]
+    msgs = [msgs[0]] + [swap(msgs[k], k, devices) for k in range(1, CELL)]
     plan = plans["turn"]
+    sources = (lengths, new_slot[None, :], old_cache, old_angle.T, new_angle.T)
     turned = call(
         lambda *r: turn_body(requests, devices, plan, *r),
-        [smem()] + [hbm()] * 11,
-        [((rows_dev, msg_cols), BF16)] * CELL
-        + [((tok_n, 2 * key_cols), BF16)] * CELL
-        + [((tok_n // CELL, width + EXTRA), BF16)] * CELL
-        + [((1, wide), BF16)],
-        (lengths, *[in_hbm(x) for x in sources], *weights),
+        [hbm()] * 8,
+        [((tok_n, 2 * key_cols), BF16)] * CELL
+        + [((tok_n // CELL, width + EXTRA), BF16)] * CELL,
+        (*[in_hbm(x) for x in sources], *weights),
         10,
-        [pltpu.VMEM(x.shape, x.dtype) for x in sources]
+        [pltpu.SMEM(lengths.shape, lengths.dtype)]
+        + [pltpu.VMEM(x.shape, x.dtype) for x in sources[1:]]
         + [pltpu.SemaphoreType.DMA((len(sources),)), pltpu.SemaphoreType.DMA((count_of(plan),))],
         plan,
         8,
     )
-    msgs, sends = turned[:CELL], turned[CELL : 2 * CELL]
-    relays, own_gain = turned[2 * CELL : 3 * CELL], turned[3 * CELL]
-    keep_pieces("turn", turned[3 * CELL + 1 :])
-    msgs = [msgs[0]] + [swap(msgs[k], k, devices) for k in range(1, CELL)]
+    sends, relays = turned[:CELL], turned[CELL : 2 * CELL]
+    keep_pieces("turn", turned[2 * CELL :])
     kvs = [sends[0]] + [swap(sends[k], k, devices) for k in range(1, CELL)]
     cat, own_q = call(
         assemble_body,
@@ -646,78 +689,94 @@
     plan = plans["scores"]
     parts = call(
         lambda *r: scores_body(requests, planes, plan, *r),
-        [smem()] + [vmem()] * (planes + CELL) + [hbm()] * 3,
+        [hbm()] + [vmem()] * (planes + CELL) + [hbm()] * 3,
         [((cell_rows, wide + EXTRA), BF16)] * planes,
-        (lengths, *qs, *kvs, *weights),
+        (in_hbm(lengths), *qs, *kvs, *weights),
         10,
-        [pltpu.SemaphoreType.DMA((count_of(plan),))],
+        [
+            pltpu.SMEM(lengths.shape, lengths.dtype),
+            pltpu.SemaphoreType.DMA((1,)),
+            pltpu.SemaphoreType.DMA((count_of(plan),)),
+        ],
         plan,
         5,
     )
     keep_pieces("scores", parts[planes:])
-    warm("warm_p", parts[0])
     parts = [parts[0]] + [swap(parts[k], CELL * k, devices) for k in range(1, planes)]
     plan = plans["merge"]
     merged = call(
         lambda *r: merge_body(planes, plan, *r),
-        [vmem()] * (planes + 2 + CELL) + [hbm()] * 3,
-        [((cell_rows, wide + EXTRA), BF16), ((cell_rows, wide), F32)]
-        + [((tok_n // planes, width + EXTRA), BF16)] * planes,
-        (*parts, cat, own_gain, *relays, *weights),
+        [vmem()] * (planes + 2) + [hbm()] * 3,
+        [((cell_rows, wide + EXTRA), BF16), ((cell_rows, wide), F32)],
+        (*parts, cat, own_gain, *weights),
         6,
         [pltpu.SemaphoreType.DMA((count_of(plan),))],
         plan,
         4,
     )
-    normed, hstate = merged[:2]
-    relays = merged[2 : 2 + planes]
-    keep_pieces("merge", merged[2 + planes :])
-    warm("warm_z", normed)
+    normed, hstate, own_held = merged
+    block = tok_n // planes
+    relay_mine, relay_far, relay_near = call(
+        lambda *r: regroup_body(planes, *r),
+        [vmem()] * CELL,
+        [((n * block, width + EXTRA), BF16) for n in (1, 2, 1)],
+        tuple(relays),
+        4,
+    )
+    relay_far = swap(relay_far, 2 * CELL, devices)
     blocks = [normed] + [swap(normed, CELL * k, devices) for k in range(1, planes)]
     own = jnp.concatenate(blocks, axis=0)
     across = swap(own, 2, devices)
     near = swap(own, 1, devices)
-    gu_scratch = [pltpu.VMEM((4, GU_ROWS, ff), BF16), pltpu.SemaphoreType.DMA((4,))]
-    acc = call(
-        lambda *r: first_gate_up_body(0, False, *r),
-        [vmem(), hbm(), hbm()],
+    gu_scratch = [pltpu.VMEM((6, GU_ROWS, ff), BF16), pltpu.SemaphoreType.DMA((6,))]
+    fetch_sem = [pltpu.SemaphoreType.DMA((2,))]
+    acc, x_held = call(
+        lambda *r: gate_up_body(0, plans["gate_up_own"], False, *r),
+        [vmem()] * 2 + [hbm()] * 3,
         [((all_rows, 2 * ff), F32)],
-        (own, w_gate, w_up),
-        9,
-        gu_scratch,
-        moved=14,
-    )[0]
+        (own, in_vmem(own_held), *weights),
+        12,
+        gu_scratch + fetch_sem,
+        plans["gate_up_own"],
+        14,
+    )
     far = swap(across, 1, devices)
-    acc = call(
-        lambda *r: first_gate_up_body(2, True, *r),
-        [vmem(), vmem(), hbm(), hbm()],
+    acc, near_held = call(
+        lambda *r: gate_up_body(2, plans["gate_up_x"], True, *r),
+        [vmem()] * 3 + [hbm()] * 3,
         [((all_rows, 2 * ff), F32)],
-        (across, acc, w_gate, w_up),
-        9,
-        gu_scratch,
-        moved=14,
-    )[0]
-    relays = [relays[0]] + [swap(relays[k], CELL * k, devices) for k in range(1, planes)]
-    nears = [h for h in held if h[0][0] == "near"]
+        (across, acc, in_vmem(x_held), *weights),
+        12,
+        gu_scratch + fetch_sem,
+        plans["gate_up_x"],
+        14,
+    )
+    relay_near = jnp.concatenate([relay_near, relay_far[block:]], axis=0)
+    relay_near = swap(relay_near, CELL, devices)
     downs = [h for h in held if h[0][0] == "down"]
     send, keep = call(
-        lambda *r: rest_body(planes, [h[0] for h in nears], [h[0] for h in downs], *r),
-        [vmem()] * (6 + len(held)) + [hbm()] * 2,
+        lambda *r: rest_body(planes, [h[0] for h in downs], *r),
+        [vmem()] * (7 + len(downs)) + [hbm()] * 2,
         [((all_rows // 2, model), F32)] * 2,
         (
             own,
             across,
-            near,
-            far,
+            in_vmem(near),
+            in_vmem(far),
             acc,
             hstate,
-            *[in_vmem(h[1]) for h in nears],
+            in_vmem(near_held),
             *[in_vmem(h[1]) for h in downs],
             w_gate,
             w_up,
         ),
-        10,
-        [pltpu.VMEM((all_rows, 2 * ff), F32), pltpu.VMEM((all_rows, model), F32)] + gu_scratch,
+        18,
+        [
+            pltpu.VMEM((all_rows, 2 * ff), F32),
+            pltpu.VMEM((all_rows, model), F32),
+            pltpu.VMEM((8, GU_ROWS, ff), BF16),
+            pltpu.SemaphoreType.DMA((8,)),
+        ],
         moved=40,
         on_chip=True,
     )
@@ -743,7 +802,12 @@
         final_body, [vmem()] * planes, [((rows_dev, model), BF16)], tuple(pieces), 8
     )[0]
     new_cache = call(
-        place_body, [vmem()] * planes, [((CTOK_DEV, width), BF16)], tuple(relays), 8, moved=1
+        place_body,
+        [vmem()] * 3,
+        [((CTOK_DEV, width), BF16)],
+        (relay_mine, relay_far, relay_near),
+        8,
+        moved=1,
     )[0]
     return (new_cache, layer_out)
 

time: 116 us -> 108 us (0.931)
  Pallas kernels: 50.5 us -> 42.8 us
  starting transfers between devices: 32.8 us -> 35.8 us
  local copies, waits for them, and re-layouts: 2.8 us -> 0.04 us
    pallas_call x14, Pallas kernels: 50.5 us -> 42.8 us  [call(): pl.pallas_call(body, in_specs=ins, out_specs=[vmem() for _ in shapes], ou...]
    ppermute x30 -> x29, starting transfers between devices: 32.8 us -> 35.8 us  [swap(): return lax.ppermute(x, 'ctx', [(i, i ^ k) for i in range(devices)])]
    unnamed x7 -> x3, local copies, waits for them, and re-layouts: 1.44 us -> 0.02 us
    broadcast_in_dim x1 -> x0, local copies, waits for them, and re-layouts: 1.35 us -> none  [cells_steps(): gain[None, :]]
    ppermute x30 -> x29, waiting for transfers between devices: 29.1 us -> 28.4 us  [swap(): return lax.ppermute(x, 'ctx', [(i, i ^ k) for i in range(devices)])]
  transfers between devices with their start and end apart: 30 -> 29, of which waited for: 15 -> 12; matrix products, arithmetic and copies ran while one was open for 0% -> 0% of each run, Pallas kernels for 24% -> 32%
where the time goes in v1:
time: 108 us
  Pallas kernels  42.8 us (40%)
  starting transfers between devices  35.8 us (33%)
  waiting for transfers between devices  28.4 us (26%)
    pallas_call x14, Pallas kernels, call(): pl.pallas_call(body, in_specs=ins, out_specs=[vmem() for _ in shapes], ou...  42.8 us
    ppermute x29, starting transfers between devices, swap(): return lax.ppermute(x, 'ctx', [(i, i ^ k) for i in range(devices)])  35.8 us
    ppermute x29, waiting for transfers between devices, swap(): return lax.ppermute(x, 'ctx', [(i, i ^ k) for i in range(devices)])  28.4 us
  transfers between devices with their start and end apart: 29, of which 12 were waited for; matrix products, arithmetic and copies ran while one was open for 0% of the time, Pallas kernels for 32%

profile of v1, /device:TPU:0, one launch (start us, length us, event | category | flops | bytes accessed | tf_op | source)
XLA Modules:
  0.0 107.8 jit_solution(311111982077530643)
XLA Ops:
  0.6 4.1 %shard_map.131 = (bf16[128,512]{1,0:T(8,128)(2,1)S(1)}, bf16[128,512]{1,0:T(8,128)(2,1)S(1)}, bf16[128,512]{1,0:T(8,128)(2,1)S(1)}, bf16[128,512]{1,0:T(8,128)(2...) custom-call(s32[4]{0:T(128)} %r_0_.3, ...), custom_call_target="tpu_custom_call" | custom-call | bytes 8388608 | tf_op jit(solution)/shard_map/pallas_call | solution.py:40
  5.3 2.5 %collective-permute-start.12 = (bf16[128,512]{1,0:T(8,128)(2,1)S(1)}, bf16[128,512]{1,0:T(8,128)(2,1)S(1)}, u32[]{:S(2)}, u32[]{:S(2)}) collective-permute-start(bf16[128,512]{1,0:T(8,128)(2,1)S(1)} %get-tuple-element.56), channel_id=1, source_target_pairs={{0,2},{1,3},{2,0},{3,1},{4,6},{5,7},{6,4},{7,5},{8,10},{9,11},{10,... | collective-permute-start | bytes 393224 | tf_op jit(solution)/shard_map/ppermute | solution.py:586
  7.9 1.0 shard_map.134
  9.1 1.9 %collective-permute-start.6 = (bf16[2,4608]{1,0:T(2,128)(2,1)S(1)}, bf16[2,4608]{1,0:T(2,128)(2,1)S(1)}, u32[]{:S(2)}, u32[]{:S(2)}) collective-permute-start(bf16[2,4608]{1,0:T(2,128)(2,1)S(1)} %get-tuple-element.51), channel_id=1, source_target_pairs={{0,2},{1,3},{2,0},{3,1},{4,6},{5,7},{6,4},{7,5},{8,10},{9,11},{10,... | collective-permute-start | bytes 55304 | tf_op jit(solution)/shard_map/ppermute | solution.py:586
  11.9 3.5 %collective-permute-done.6.refs_2_ = bf16[2,4608]{1,0:T(2,128)(2,1)S(1)} collective-permute-done((bf16[2,4608]{1,0:T(2,128)(2,1)S(1)}, bf16[2,4608]{1,0:T(2,128)(2,1)S(1)}, u32[]{:S(2)}, u32[]{:S(2)}) %collective-permute-start.6) | collective-permute-done | bytes 18464 | tf_op jit(solution)/shard_map/ppermute | solution.py:586
  15.4 3.9 %collective-permute-start.10 = (bf16[8,2048]{1,0:T(8,128)(2,1)S(1)}, bf16[8,2048]{1,0:T(8,128)(2,1)S(1)}, u32[]{:S(2)}, u32[]{:S(2)}) collective-permute-start(bf16[8,2048]{1,0:T(8,128)(2,1)S(1)} %get-tuple-element.53.r_1_.r_0_), channel_id=1, source_target_pairs={{0,12},{1,13},{2,14},{3,15},{4,8},{5,9},{6,10},{7,11},{8,4},{9,5},... | collective-permute-start | bytes 98312 | tf_op jit(solution)/shard_map/ppermute | solution.py:586
  19.3 1.9 %collective-permute-done.10.r_4_ = bf16[8,2048]{1,0:T(8,128)(2,1)S(1)} collective-permute-done((bf16[8,2048]{1,0:T(8,128)(2,1)S(1)}, bf16[8,2048]{1,0:T(8,128)(2,1)S(1)}, u32[]{:S(2)}, u32[]{:S(2)}) %collective-permute-start.10) | collective-permute-done | bytes 32800 | tf_op jit(solution)/shard_map/ppermute | solution.py:586
  21.9 2.2 %collective-permute-done.9.r_3_ = bf16[8,2048]{1,0:T(8,128)(2,1)S(1)} collective-permute-done((bf16[8,2048]{1,0:T(8,128)(2,1)S(1)}, bf16[8,2048]{1,0:T(8,128)(2,1)S(1)}, u32[]{:S(2)}, u32[]{:S(2)}) %collective-permute-start.9) | collective-permute-done | bytes 32800 | tf_op jit(solution)/shard_map/ppermute | solution.py:586
  24.2 1.0 collective-permute-done.8.r_2_
  25.2 3.5 %shard_map.136 = (bf16[8,2176]{1,0:T(8,128)(2,1)S(1)}, bf16[8,2176]{1,0:T(8,128)(2,1)S(1)}, bf16[8,2176]{1,0:T(8,128)(2,1)S(1)}, bf16[8,2176]{1,0:T(8,128)(2,1)S(1)}, bf16[512,8192]{1,0:T(8,128)(2,1)S(1)}) custom-call(s32[4]{0:T(128)} %r_0_.3, bf16[8,2048]{1,0:T(8,128)(2,1)S(1)} %get-tuple-element.53.r_1_.r_0_, ...), custom_call_target="tpu_custom_call" | custom-call | bytes 5242880 | tf_op jit(solution)/shard_map/pallas_call | solution.py:40
  29.4 3.7 %collective-permute-start.15 = (bf16[8,2176]{1,0:T(8,128)(2,1)S(1)}, bf16[8,2176]{1,0:T(8,128)(2,1)S(1)}, u32[]{:S(2)}, u32[]{:S(2)}) collective-permute-start(bf16[8,2176]{1,0:T(8,128)(2,1)S(1)} %get-tuple-element.60), channel_id=1, source_target_pairs={{0,8},{1,9},{2,10},{3,11},{4,12},{5,13},{6,14},{7,15},{8,0},{9,1},... | collective-permute-start | bytes 104456 | tf_op jit(solution)/shard_map/ppermute | solution.py:586
  33.1 1.7 %collective-permute-start.1 = (bf16[32,2176]{1,0:T(8,128)(2,1)S(1)}, bf16[32,2176]{1,0:T(8,128)(2,1)S(1)}, u32[]{:S(2)}, u32[]{:S(2)}) collective-permute-start(bf16[32,2176]{1,0:T(8,128)(2,1)S(1)} %get-tuple-element.44), channel_id=1, source_target_pairs={{0,2},{1,3},{2,0},{3,1},{4,6},{5,7},{6,4},{7,5},{8,10},{9,11},{10,... | collective-permute-start | bytes 417800 | tf_op jit(solution)/shard_map/ppermute | solution.py:586
  35.8 3.1 %collective-permute-done.16.r_3_ = bf16[8,2176]{1,0:T(8,128)(2,1)S(1)} collective-permute-done((bf16[8,2176]{1,0:T(8,128)(2,1)S(1)}, bf16[8,2176]{1,0:T(8,128)(2,1)S(1)}, u32[]{:S(2)}, u32[]{:S(2)}) %collective-permute-start.16) | collective-permute-done | bytes 34848 | tf_op jit(solution)/shard_map/ppermute | solution.py:586
  38.9 2.1 %shard_map.137 = (bf16[8,2176]{1,0:T(8,128)(2,1)S(1)}, f32[8,2048]{1,0:T(8,128)S(1)}, bf16[2,512,1792]{2,1,0:T(8,128)(2,1)S(1)}) custom-call(bf16[8,2176]{1,0:T(8,128)(2,1)S(1)} %get-tuple-element.58.r_0_, bf16[8,2176]{1,0:T(8,128)(2,1)S(1)} %collective-permute-done.14.r_1_, bf16[8,2176]{1,0:T(8,128)(2,1)S(1)} %collective-permute-done.15.r_2_, ...), custom_call_target="tpu_custom_call" | custom-call | bytes 4194304 | tf_op jit(solution)/shard_map/pallas_call | solution.py:40
  41.4 3.9 %collective-permute-done.17 = bf16[8,2176]{1,0:T(8,128)(2,1)S(1)} collective-permute-done((bf16[8,2176]{1,0:T(8,128)(2,1)S(1)}, bf16[8,2176]{1,0:T(8,128)(2,1)S(1)}, u32[]{:S(2)}, u32[]{:S(2)}) %collective-permute-start.17) | collective-permute-done | bytes 34848 | tf_op jit(solution)/shard_map/ppermute | solution.py:586
  45.3 2.4 %collective-permute-start.18 = (bf16[8,2176]{1,0:T(8,128)(2,1)S(1)}, bf16[8,2176]{1,0:T(8,128)(2,1)S(1)}, u32[]{:S(2)}, u32[]{:S(2)}) collective-permute-start(bf16[8,2176]{1,0:T(8,128)(2,1)S(1)} %get-tuple-element.64), channel_id=1, source_target_pairs={{0,8},{1,9},{2,10},{3,11},{4,12},{5,13},{6,14},{7,15},{8,0},{9,1},... | collective-permute-start | bytes 104456 | tf_op jit(solution)/shard_map/ppermute | solution.py:586
  47.7 2.5 %collective-permute-done.18 = bf16[8,2176]{1,0:T(8,128)(2,1)S(1)} collective-permute-done((bf16[8,2176]{1,0:T(8,128)(2,1)S(1)}, bf16[8,2176]{1,0:T(8,128)(2,1)S(1)}, u32[]{:S(2)}, u32[]{:S(2)}) %collective-permute-start.18) | collective-permute-done | bytes 34848 | tf_op jit(solution)/shard_map/ppermute | solution.py:586
  50.2 1.6 %collective-permute-start.20 = (bf16[32,2176]{1,0:T(8,128)(2,1)S(1)}, bf16[32,2176]{1,0:T(8,128)(2,1)S(1)}, u32[]{:S(2)}, u32[]{:S(2)}) collective-permute-start(bf16[32,2176]{1,0:T(8,128)(2,1)S(1)} %constant_dynamic-update-slice_fusion.r_0_), channel_id=1, source_target_pairs={{0,2},{1,3},{2,0},{3,1},{4,6},{5,7},{6,4},{7,5},{8,10},{9,11},{10,... | collective-permute-start | bytes 417800 | tf_op jit(solution)/shard_map/ppermute | solution.py:586
  52.0 2.7 %collective-permute-start.3 = (bf16[64,2176]{1,0:T(8,128)(2,1)S(1)}, bf16[64,2176]{1,0:T(8,128)(2,1)S(1)}, u32[]{:S(2)}, u32[]{:S(2)}) collective-permute-start(bf16[64,2176]{1,0:T(8,128)(2,1)S(1)} %get-tuple-element.47), channel_id=1, source_target_pairs={{0,8},{1,9},{2,10},{3,11},{4,12},{5,13},{6,14},{7,15},{8,0},{9,1},... | collective-permute-start | bytes 835592 | tf_op jit(solution)/shard_map/ppermute | solution.py:586
  55.3 4.7 %shard_map.140.r_8_ = bf16[768,8192]{1,0:T(8,128)(2,1)S(1)} custom-call(bf16[8,2048]{1,0:T(8,128)(2,1)S(1)} %get-tuple-element.53.r_1_.r_0_, bf16[8192,1792]{1,0:T(8,128)(2,1)} %r_10_.3, bf16[8192,1792]{1,0:T(8,128)(2,1)} %r_11_.3, bf16[1792,8192]{1,0:T(8,128)(2,1)} %r_3_.5), custom_call_target="tpu_custom_call" | custom-call | bytes 8388608 | tf_op jit(solution)/shard_map/pallas_call | solution.py:40
  60.0 5.5 %shard_map.138 = (f32[32,3584]{1,0:T(8,128)S(1)}, bf16[2,512,1792]{2,1,0:T(8,128)(2,1)S(1)}) custom-call(bf16[32,2176]{1,0:T(8,128)(2,1)S(1)} %constant_dynamic-update-slice_fusion.r_0_, bf16[2,512,1792]{2,1,0:T(8,128)(2,1)S(1)} %get-tuple-element.65.r_1_, bf16[8192,1792]{1,0:T(8,128)(2,1)} %r_10_.3, bf16[8192,1792]{1,0:T(8,128)(2,1)} %r_11_.3, ...), custom_call_target="tpu_custom_call" | custom-call | bytes 14680064 | tf_op jit(solution)/shard_map/pallas_call | solution.py:40
  65.5 5.3 %shard_map.139 = (f32[32,3584]{1,0:T(8,128)S(1)}, bf16[2,512,1792]{2,1,0:T(8,128)(2,1)S(1)}) custom-call(bf16[32,2176]{1,0:T(8,128)(2,1)S(1)} %collective-permute-done.20.r_0_.r_1_, f32[32,3584]{1,0:T(8,128)S(1)} %get-tuple-element.66.r_1_, bf16[2,512,1792]{2,1,0:T(8,128)(2,1)S(1)} %get-tuple-element.67.r_2_, bf16[8192,1792]{1,0:T(8,128)(2,1)} %r_10_.3, ...), custom_call_target="tpu_custom_call" | custom-call | bytes 14680064 | tf_op jit(solution)/shard_map/pallas_call | solution.py:40
  70.9 14.4 %shard_map.141 = (f32[16,8192]{1,0:T(8,128)S(1)}, f32[16,8192]{1,0:T(8,128)S(1)}) custom-call(bf16[32,2176]{1,0:T(8,128)(2,1)S(1)} %constant_dynamic-update-slice_fusion.r_0_, bf16[32,2176]{1,0:T(8,128)(2,1)S(1)} %collective-permute-done.20.r_0_.r_1_, bf16[32,2176]{1,0:T(8,128)(2,1)S(1)} %collective-permute-done.21.r_2_, ...), custom_call_target="tpu_custom_call" | custom-call | bytes 41943040 | tf_op jit(solution)/shard_map/pallas_call | solution.py:40
  85.9 4.5 %collective-permute-start.4 = (bf16[64,2176]{1,0:T(8,128)(2,1)S(1)}, bf16[64,2176]{1,0:T(8,128)(2,1)S(1)}, u32[]{:S(2)}, u32[]{:S(2)}) collective-permute-start(bf16[64,2176]{1,0:T(8,128)(2,1)S(1)} %pad_maximum_fusion), channel_id=1, source_target_pairs={{0,4},{1,5},{2,6},{3,7},{4,0},{5,1},{6,2},{7,3},{8,12},{9,13},{10,... | collective-permute-start | bytes 835592 | tf_op jit(solution)/shard_map/ppermute | solution.py:586
  90.6 1.0 collective-permute-start.24
  91.6 1.1 %collective-permute-start.25 = (bf16[2,8192]{1,0:T(2,128)(2,1)S(1)}, bf16[2,8192]{1,0:T(2,128)(2,1)S(1)}, u32[]{:S(2)}, u32[]{:S(2)}) collective-permute-start(bf16[2,8192]{1,0:T(2,128)(2,1)S(1)} %get-tuple-element.77), channel_id=1, source_target_pairs={{0,2},{1,3},{2,0},{3,1},{4,6},{5,7},{6,4},{7,5},{8,10},{9,11},{10,... | collective-permute-start | bytes 98312 | tf_op jit(solution)/shard_map/ppermute | solution.py:586
  92.7 4.3 %collective-permute-done.25.r_2_ = bf16[2,8192]{1,0:T(2,128)(2,1)S(1)} collective-permute-done((bf16[2,8192]{1,0:T(2,128)(2,1)S(1)}, bf16[2,8192]{1,0:T(2,128)(2,1)S(1)}, u32[]{:S(2)}, u32[]{:S(2)}) %collective-permute-start.25) | collective-permute-done | bytes 32800 | tf_op jit(solution)/shard_map/ppermute | solution.py:586
  97.0 1.8 %collective-permute-start.26 = (bf16[2,8192]{1,0:T(2,128)(2,1)S(1)}, bf16[2,8192]{1,0:T(2,128)(2,1)S(1)}, u32[]{:S(2)}, u32[]{:S(2)}) collective-permute-start(bf16[2,8192]{1,0:T(2,128)(2,1)S(1)} %get-tuple-element.79), channel_id=1, source_target_pairs={{0,4},{1,5},{2,6},{3,7},{4,0},{5,1},{6,2},{7,3},{8,12},{9,13},{10,... | collective-permute-start | bytes 98312 | tf_op jit(solution)/shard_map/ppermute | solution.py:586
  98.8 2.6 %collective-permute-start.27 = (bf16[2,8192]{1,0:T(2,128)(2,1)S(1)}, bf16[2,8192]{1,0:T(2,128)(2,1)S(1)}, u32[]{:S(2)}, u32[]{:S(2)}) collective-permute-start(bf16[2,8192]{1,0:T(2,128)(2,1)S(1)} %get-tuple-element.80), channel_id=1, source_target_pairs={{0,8},{1,9},{2,10},{3,11},{4,12},{5,13},{6,14},{7,15},{8,0},{9,1},... | collective-permute-start | bytes 98312 | tf_op jit(solution)/shard_map/ppermute | solution.py:586
  101.5 1.0 shard_map.133
  102.5 1.4 %collective-permute-done.27.refs_1_ = bf16[2,8192]{1,0:T(2,128)(2,1)S(1)} collective-permute-done((bf16[2,8192]{1,0:T(2,128)(2,1)S(1)}, bf16[2,8192]{1,0:T(2,128)(2,1)S(1)}, u32[]{:S(2)}, u32[]{:S(2)}) %collective-permute-start.27) | collective-permute-done | bytes 32800 | tf_op jit(solution)/shard_map/ppermute | solution.py:586
  103.9 3.2 %collective-permute-done.28.refs_2_ = bf16[2,8192]{1,0:T(2,128)(2,1)S(1)} collective-permute-done((bf16[2,8192]{1,0:T(2,128)(2,1)S(1)}, bf16[2,8192]{1,0:T(2,128)(2,1)S(1)}, u32[]{:S(2)}, u32[]{:S(2)}) %collective-permute-start.28) | collective-permute-done | bytes 32800 | tf_op jit(solution)/shard_map/ppermute | solution.py:586
  (46 shorter events, 7.0 us)
Async XLA Ops:
  4.7 20.4 %collective-permute-start.11 = (bf16[128,512]{1,0:T(8,128)(2,1)S(1)}, bf16[128,512]{1,0:T(8,128)(2,1)S(1)}, u32[]{:S(2)}, u32[]{:S(2)}) collective-permute-start(bf16[128,512]{1,0:T(8,128)(2,1)S(1)} %get-tuple-element.55), channel_id=1, source_target_pairs={{0,1},{1,0},{2,3},{3,2},{4,5},{5,4},{6,7},{7,6},{8,9},{9,8},{10,11... | collective-permute-start | bytes 393224 | tf_op jit(solution)/shard_map/ppermute | solution.py:586
  5.3 19.9 %collective-permute-start.12 = (bf16[128,512]{1,0:T(8,128)(2,1)S(1)}, bf16[128,512]{1,0:T(8,128)(2,1)S(1)}, u32[]{:S(2)}, u32[]{:S(2)}) collective-permute-start(bf16[128,512]{1,0:T(8,128)(2,1)S(1)} %get-tuple-element.56), channel_id=1, source_target_pairs={{0,2},{1,3},{2,0},{3,1},{4,6},{5,7},{6,4},{7,5},{8,10},{9,11},{10,... | collective-permute-start | bytes 393224 | tf_op jit(solution)/shard_map/ppermute | solution.py:586
  7.8 17.3 %collective-permute-start.13 = (bf16[128,512]{1,0:T(8,128)(2,1)S(1)}, bf16[128,512]{1,0:T(8,128)(2,1)S(1)}, u32[]{:S(2)}, u32[]{:S(2)}) collective-permute-start(bf16[128,512]{1,0:T(8,128)(2,1)S(1)} %get-tuple-element.57), channel_id=1, source_target_pairs={{0,3},{1,2},{2,1},{3,0},{4,7},{5,6},{6,5},{7,4},{8,11},{9,10},{10,... | collective-permute-start | bytes 393224 | tf_op jit(solution)/shard_map/ppermute | solution.py:586
  8.9 2.2 %collective-permute-start.5 = (bf16[2,4608]{1,0:T(2,128)(2,1)S(1)}, bf16[2,4608]{1,0:T(2,128)(2,1)S(1)}, u32[]{:S(2)}, u32[]{:S(2)}) collective-permute-start(bf16[2,4608]{1,0:T(2,128)(2,1)S(1)} %get-tuple-element.50), channel_id=1, source_target_pairs={{0,1},{1,0},{2,3},{3,2},{4,5},{5,4},{6,7},{7,6},{8,9},{9,8},{10,11... | collective-permute-start | bytes 55304 | tf_op jit(solution)/shard_map/ppermute | solution.py:586
  9.1 6.2 %collective-permute-start.6 = (bf16[2,4608]{1,0:T(2,128)(2,1)S(1)}, bf16[2,4608]{1,0:T(2,128)(2,1)S(1)}, u32[]{:S(2)}, u32[]{:S(2)}) collective-permute-start(bf16[2,4608]{1,0:T(2,128)(2,1)S(1)} %get-tuple-element.51), channel_id=1, source_target_pairs={{0,2},{1,3},{2,0},{3,1},{4,6},{5,7},{6,4},{7,5},{8,10},{9,11},{10,... | collective-permute-start | bytes 55304 | tf_op jit(solution)/shard_map/ppermute | solution.py:586
  11.1 4.3 %collective-permute-start.7 = (bf16[2,4608]{1,0:T(2,128)(2,1)S(1)}, bf16[2,4608]{1,0:T(2,128)(2,1)S(1)}, u32[]{:S(2)}, u32[]{:S(2)}) collective-permute-start(bf16[2,4608]{1,0:T(2,128)(2,1)S(1)} %get-tuple-element.52), channel_id=1, source_target_pairs={{0,3},{1,2},{2,1},{3,0},{4,7},{5,6},{6,5},{7,4},{8,11},{9,10},{10,... | collective-permute-start | bytes 55304 | tf_op jit(solution)/shard_map/ppermute | solution.py:586
  15.4 5.8 %collective-permute-start.10 = (bf16[8,2048]{1,0:T(8,128)(2,1)S(1)}, bf16[8,2048]{1,0:T(8,128)(2,1)S(1)}, u32[]{:S(2)}, u32[]{:S(2)}) collective-permute-start(bf16[8,2048]{1,0:T(8,128)(2,1)S(1)} %get-tuple-element.53.r_1_.r_0_), channel_id=1, source_target_pairs={{0,12},{1,13},{2,14},{3,15},{4,8},{5,9},{6,10},{7,11},{8,4},{9,5},... | collective-permute-start | bytes 98312 | tf_op jit(solution)/shard_map/ppermute | solution.py:586
  19.3 4.8 %collective-permute-start.9 = (bf16[8,2048]{1,0:T(8,128)(2,1)S(1)}, bf16[8,2048]{1,0:T(8,128)(2,1)S(1)}, u32[]{:S(2)}, u32[]{:S(2)}) collective-permute-start(bf16[8,2048]{1,0:T(8,128)(2,1)S(1)} %get-tuple-element.53.r_1_.r_0_), channel_id=1, source_target_pairs={{0,8},{1,9},{2,10},{3,11},{4,12},{5,13},{6,14},{7,15},{8,0},{9,1},... | collective-permute-start | bytes 98312 | tf_op jit(solution)/shard_map/ppermute | solution.py:586
  21.2 3.9 %collective-permute-start.8 = (bf16[8,2048]{1,0:T(8,128)(2,1)S(1)}, bf16[8,2048]{1,0:T(8,128)(2,1)S(1)}, u32[]{:S(2)}, u32[]{:S(2)}) collective-permute-start(bf16[8,2048]{1,0:T(8,128)(2,1)S(1)} %get-tuple-element.53.r_1_.r_0_), channel_id=1, source_target_pairs={{0,4},{1,5},{2,6},{3,7},{4,0},{5,1},{6,2},{7,3},{8,12},{9,13},{10,... | collective-permute-start | bytes 98312 | tf_op jit(solution)/shard_map/ppermute | solution.py:586
  28.7 6.2 %collective-permute-start.14 = (bf16[8,2176]{1,0:T(8,128)(2,1)S(1)}, bf16[8,2176]{1,0:T(8,128)(2,1)S(1)}, u32[]{:S(2)}, u32[]{:S(2)}) collective-permute-start(bf16[8,2176]{1,0:T(8,128)(2,1)S(1)} %get-tuple-element.59), channel_id=1, source_target_pairs={{0,4},{1,5},{2,6},{3,7},{4,0},{5,1},{6,2},{7,3},{8,12},{9,13},{10,... | collective-permute-start | bytes 104456 | tf_op jit(solution)/shard_map/ppermute | solution.py:586
  29.4 6.4 %collective-permute-start.15 = (bf16[8,2176]{1,0:T(8,128)(2,1)S(1)}, bf16[8,2176]{1,0:T(8,128)(2,1)S(1)}, u32[]{:S(2)}, u32[]{:S(2)}) collective-permute-start(bf16[8,2176]{1,0:T(8,128)(2,1)S(1)} %get-tuple-element.60), channel_id=1, source_target_pairs={{0,8},{1,9},{2,10},{3,11},{4,12},{5,13},{6,14},{7,15},{8,0},{9,1},... | collective-permute-start | bytes 104456 | tf_op jit(solution)/shard_map/ppermute | solution.py:586
  33.1 5.7 %collective-permute-start.16 = (bf16[8,2176]{1,0:T(8,128)(2,1)S(1)}, bf16[8,2176]{1,0:T(8,128)(2,1)S(1)}, u32[]{:S(2)}, u32[]{:S(2)}) collective-permute-start(bf16[8,2176]{1,0:T(8,128)(2,1)S(1)} %get-tuple-element.61), channel_id=1, source_target_pairs={{0,12},{1,13},{2,14},{3,15},{4,8},{5,9},{6,10},{7,11},{8,4},{9,5},... | collective-permute-start | bytes 104456 | tf_op jit(solution)/shard_map/ppermute | solution.py:586
  33.1 18.6 %collective-permute-start = (bf16[32,2176]{1,0:T(8,128)(2,1)S(1)}, bf16[32,2176]{1,0:T(8,128)(2,1)S(1)}, u32[]{:S(2)}, u32[]{:S(2)}) collective-permute-start(bf16[32,2176]{1,0:T(8,128)(2,1)S(1)} %get-tuple-element.43), channel_id=1, source_target_pairs={{0,1},{1,0},{2,3},{3,2},{4,5},{5,4},{6,7},{7,6},{8,9},{9,8},{10,11... | collective-permute-start | bytes 417800 | tf_op jit(solution)/shard_map/ppermute | solution.py:586
  33.1 18.6 %collective-permute-start.1 = (bf16[32,2176]{1,0:T(8,128)(2,1)S(1)}, bf16[32,2176]{1,0:T(8,128)(2,1)S(1)}, u32[]{:S(2)}, u32[]{:S(2)}) collective-permute-start(bf16[32,2176]{1,0:T(8,128)(2,1)S(1)} %get-tuple-element.44), channel_id=1, source_target_pairs={{0,2},{1,3},{2,0},{3,1},{4,6},{5,7},{6,4},{7,5},{8,10},{9,11},{10,... | collective-permute-start | bytes 417800 | tf_op jit(solution)/shard_map/ppermute | solution.py:586
  34.8 16.9 %collective-permute-start.2 = (bf16[32,2176]{1,0:T(8,128)(2,1)S(1)}, bf16[32,2176]{1,0:T(8,128)(2,1)S(1)}, u32[]{:S(2)}, u32[]{:S(2)}) collective-permute-start(bf16[32,2176]{1,0:T(8,128)(2,1)S(1)} %get-tuple-element.45), channel_id=1, source_target_pairs={{0,3},{1,2},{2,1},{3,0},{4,7},{5,6},{6,5},{7,4},{8,11},{9,10},{10,... | collective-permute-start | bytes 417800 | tf_op jit(solution)/shard_map/ppermute | solution.py:586
  40.9 9.2 %collective-permute-start.19 = (bf16[8,2176]{1,0:T(8,128)(2,1)S(1)}, bf16[8,2176]{1,0:T(8,128)(2,1)S(1)}, u32[]{:S(2)}, u32[]{:S(2)}) collective-permute-start(bf16[8,2176]{1,0:T(8,128)(2,1)S(1)} %get-tuple-element.64), channel_id=1, source_target_pairs={{0,12},{1,13},{2,14},{3,15},{4,8},{5,9},{6,10},{7,11},{8,4},{9,5},... | collective-permute-start | bytes 104456 | tf_op jit(solution)/shard_map/ppermute | solution.py:586
  41.4 3.9 %collective-permute-start.17 = (bf16[8,2176]{1,0:T(8,128)(2,1)S(1)}, bf16[8,2176]{1,0:T(8,128)(2,1)S(1)}, u32[]{:S(2)}, u32[]{:S(2)}) collective-permute-start(bf16[8,2176]{1,0:T(8,128)(2,1)S(1)} %get-tuple-element.64), channel_id=1, source_target_pairs={{0,4},{1,5},{2,6},{3,7},{4,0},{5,1},{6,2},{7,3},{8,12},{9,13},{10,... | collective-permute-start | bytes 104456 | tf_op jit(solution)/shard_map/ppermute | solution.py:586
  45.3 4.8 %collective-permute-start.18 = (bf16[8,2176]{1,0:T(8,128)(2,1)S(1)}, bf16[8,2176]{1,0:T(8,128)(2,1)S(1)}, u32[]{:S(2)}, u32[]{:S(2)}) collective-permute-start(bf16[8,2176]{1,0:T(8,128)(2,1)S(1)} %get-tuple-element.64), channel_id=1, source_target_pairs={{0,8},{1,9},{2,10},{3,11},{4,12},{5,13},{6,14},{7,15},{8,0},{9,1},... | collective-permute-start | bytes 104456 | tf_op jit(solution)/shard_map/ppermute | solution.py:586
  50.2 5.1 %collective-permute-start.20 = (bf16[32,2176]{1,0:T(8,128)(2,1)S(1)}, bf16[32,2176]{1,0:T(8,128)(2,1)S(1)}, u32[]{:S(2)}, u32[]{:S(2)}) collective-permute-start(bf16[32,2176]{1,0:T(8,128)(2,1)S(1)} %constant_dynamic-update-slice_fusion.r_0_), channel_id=1, source_target_pairs={{0,2},{1,3},{2,0},{3,1},{4,6},{5,7},{6,4},{7,5},{8,10},{9,11},{10,... | collective-permute-start | bytes 417800 | tf_op jit(solution)/shard_map/ppermute | solution.py:586
  52.0 33.8 %collective-permute-start.3 = (bf16[64,2176]{1,0:T(8,128)(2,1)S(1)}, bf16[64,2176]{1,0:T(8,128)(2,1)S(1)}, u32[]{:S(2)}, u32[]{:S(2)}) collective-permute-start(bf16[64,2176]{1,0:T(8,128)(2,1)S(1)} %get-tuple-element.47), channel_id=1, source_target_pairs={{0,8},{1,9},{2,10},{3,11},{4,12},{5,13},{6,14},{7,15},{8,0},{9,1},... | collective-permute-start | bytes 835592 | tf_op jit(solution)/shard_map/ppermute | solution.py:586
  54.8 16.1 %collective-permute-start.21 = (bf16[32,2176]{1,0:T(8,128)(2,1)S(1)}, bf16[32,2176]{1,0:T(8,128)(2,1)S(1)}, u32[]{:S(2)}, u32[]{:S(2)}) collective-permute-start(bf16[32,2176]{1,0:T(8,128)(2,1)S(1)} %constant_dynamic-update-slice_fusion.r_0_), channel_id=1, source_target_pairs={{0,1},{1,0},{2,3},{3,2},{4,5},{5,4},{6,7},{7,6},{8,9},{9,8},{10,11... | collective-permute-start | bytes 417800 | tf_op jit(solution)/shard_map/ppermute | solution.py:586
  55.3 15.6 %collective-permute-start.22 = (bf16[32,2176]{1,0:T(8,128)(2,1)S(1)}, bf16[32,2176]{1,0:T(8,128)(2,1)S(1)}, u32[]{:S(2)}, u32[]{:S(2)}) collective-permute-start(bf16[32,2176]{1,0:T(8,128)(2,1)S(1)} %collective-permute-done.20.r_0_.r_1_), channel_id=1, source_target_pairs={{0,1},{1,0},{2,3},{3,2},{4,5},{5,4},{6,7},{7,6},{8,9},{9,8},{10,11... | collective-permute-start | bytes 417800 | tf_op jit(solution)/shard_map/ppermute | solution.py:586
  85.3 5.2 %collective-permute-start.23 = (f32[16,8192]{1,0:T(8,128)S(1)}, f32[16,8192]{1,0:T(8,128)S(1)}, u32[]{:S(2)}, u32[]{:S(2)}) collective-permute-start(f32[16,8192]{1,0:T(8,128)S(1)} %get-tuple-element.74), channel_id=1, source_target_pairs={{0,1},{1,0},{2,3},{3,2},{4,5},{5,4},{6,7},{7,6},{8,9},{9,8},{10,11... | collective-permute-start | bytes 1572872 | tf_op jit(solution)/shard_map/ppermute | solution.py:586
  85.9 15.6 %collective-permute-start.4 = (bf16[64,2176]{1,0:T(8,128)(2,1)S(1)}, bf16[64,2176]{1,0:T(8,128)(2,1)S(1)}, u32[]{:S(2)}, u32[]{:S(2)}) collective-permute-start(bf16[64,2176]{1,0:T(8,128)(2,1)S(1)} %pad_maximum_fusion), channel_id=1, source_target_pairs={{0,4},{1,5},{2,6},{3,7},{4,0},{5,1},{6,2},{7,3},{8,12},{9,13},{10,... | collective-permute-start | bytes 835592 | tf_op jit(solution)/shard_map/ppermute | solution.py:586
  90.6 6.4 %collective-permute-start.24 = (bf16[8,8192]{1,0:T(8,128)(2,1)S(1)}, bf16[8,8192]{1,0:T(8,128)(2,1)S(1)}, u32[]{:S(2)}, u32[]{:S(2)}) collective-permute-start(bf16[8,8192]{1,0:T(8,128)(2,1)S(1)} %get-tuple-element.76), channel_id=1, source_target_pairs={{0,2},{1,3},{2,0},{3,1},{4,6},{5,7},{6,4},{7,5},{8,10},{9,11},{10,... | collective-permute-start | bytes 393224 | tf_op jit(solution)/shard_map/ppermute | solution.py:586
  91.6 5.4 %collective-permute-start.25 = (bf16[2,8192]{1,0:T(2,128)(2,1)S(1)}, bf16[2,8192]{1,0:T(2,128)(2,1)S(1)}, u32[]{:S(2)}, u32[]{:S(2)}) collective-permute-start(bf16[2,8192]{1,0:T(2,128)(2,1)S(1)} %get-tuple-element.77), channel_id=1, source_target_pairs={{0,2},{1,3},{2,0},{3,1},{4,6},{5,7},{6,4},{7,5},{8,10},{9,11},{10,... | collective-permute-start | bytes 98312 | tf_op jit(solution)/shard_map/ppermute | solution.py:586
  97.0 5.4 %collective-permute-start.26 = (bf16[2,8192]{1,0:T(2,128)(2,1)S(1)}, bf16[2,8192]{1,0:T(2,128)(2,1)S(1)}, u32[]{:S(2)}, u32[]{:S(2)}) collective-permute-start(bf16[2,8192]{1,0:T(2,128)(2,1)S(1)} %get-tuple-element.79), channel_id=1, source_target_pairs={{0,4},{1,5},{2,6},{3,7},{4,0},{5,1},{6,2},{7,3},{8,12},{9,13},{10,... | collective-permute-start | bytes 98312 | tf_op jit(solution)/shard_map/ppermute | solution.py:586
  98.8 5.1 %collective-permute-start.27 = (bf16[2,8192]{1,0:T(2,128)(2,1)S(1)}, bf16[2,8192]{1,0:T(2,128)(2,1)S(1)}, u32[]{:S(2)}, u32[]{:S(2)}) collective-permute-start(bf16[2,8192]{1,0:T(2,128)(2,1)S(1)} %get-tuple-element.80), channel_id=1, source_target_pairs={{0,8},{1,9},{2,10},{3,11},{4,12},{5,13},{6,14},{7,15},{8,0},{9,1},... | collective-permute-start | bytes 98312 | tf_op jit(solution)/shard_map/ppermute | solution.py:586
  101.4 5.7 %collective-permute-start.28 = (bf16[2,8192]{1,0:T(2,128)(2,1)S(1)}, bf16[2,8192]{1,0:T(2,128)(2,1)S(1)}, u32[]{:S(2)}, u32[]{:S(2)}) collective-permute-start(bf16[2,8192]{1,0:T(2,128)(2,1)S(1)} %get-tuple-element.81), channel_id=1, source_target_pairs={{0,12},{1,13},{2,14},{3,15},{4,8},{5,9},{6,10},{7,11},{8,4},{9,5},... | collective-permute-start | bytes 98312 | tf_op jit(solution)/shard_map/ppermute | solution.py:586

commit v2 on v1

--- a/solution.py
+++ b/solution.py
@@ -80,12 +80,12 @@
 
 
 GU_ROWS = 512
-DOWN_ROWS = 256
+DOWN_COLS = 1024
 
 
 def piece_shape(piece):
-    kind, _, n, cols = piece
-    return (n * DOWN_ROWS, cols) if kind == "down" else (n, GU_ROWS, cols)
+    _, _, n, cols = piece
+    return (n, GU_ROWS, cols)
 
 
 def gate_up_block(flip, i, w_gate, w_up):
@@ -96,25 +96,28 @@
 
 
 def fetch_copies(fetch, weights, pieces, sem):
-    w_gate, w_up, w_down = weights
     copies = []
-    for (kind, first, n, _), out in zip(fetch, pieces):
+    for (flip, first, n, _), out in zip(fetch, pieces):
         for i in range(n):
-            if kind == "down":
-                src = w_down.at[pl.ds((first + i) * DOWN_ROWS, DOWN_ROWS), :]
-                dst = out.at[pl.ds(i * DOWN_ROWS, DOWN_ROWS), :]
-            else:
-                src, dst = gate_up_block(kind, first + i, w_gate, w_up), out.at[i]
-            copies.append(pltpu.make_async_copy(src, dst, sem.at[len(copies)]))
+            src = gate_up_block(flip, first + i, *weights)
+            copies.append(pltpu.make_async_copy(src, out.at[i], sem.at[len(copies)]))
     return copies
+
+
+def blocks_of(held, refs):
+    found = {}
+    for (flip, first, n, _), r in zip(held, refs):
+        for i in range(n):
+            found[flip, first + i] = r.at[i]
+    return found
 
 
 def count_of(fetch):
     return max(1, sum(p[2] for p in fetch))
 
 
-def warm_body(fetch, dep, w_gate, w_up, w_down, *refs):
-    copies = fetch_copies(fetch, (w_gate, w_up, w_down), refs[:-1], refs[-1])
+def warm_body(fetch, dep, w_gate, w_up, *refs):
+    copies = fetch_copies(fetch, (w_gate, w_up), refs[:-1], refs[-1])
     for c in copies:
         c.start()
     for c in copies:
@@ -151,8 +154,9 @@
 
 
 def turn_body(requests, devices, fetch, *refs):
-    sources, weights, refs = refs[:5], refs[5:8], refs[8:]
-    sends, relays, refs = refs[:CELL], refs[CELL : 2 * CELL], refs[2 * CELL :]
+    sources, weights, refs = refs[:5], refs[5:7], refs[7:]
+    sends, relays, token_row = refs[:CELL], refs[CELL : 2 * CELL], refs[2 * CELL]
+    refs = refs[2 * CELL + 1 :]
     pieces, refs = refs[: len(fetch)], refs[len(fetch) :]
     locals_, sems, fetch_sem = refs[:5], refs[5], refs[6]
     loads = [pltpu.make_async_copy(a, b, sems.at[i]) for i, (a, b) in enumerate(zip(sources, locals_))]
@@ -166,13 +170,15 @@
 
     @pl.when(here() >= 0)
     def _():
-        turn_steps(requests, devices, *locals_, sends, relays)
+        turn_steps(requests, devices, *locals_, sends, relays, token_row)
 
     for c in fetched:
         c.wait()
 
 
-def turn_steps(requests, devices, scal, slot, cache, old_angle, new_angle, sends, relays):
+def turn_steps(
+    requests, devices, scal, slot, cache, old_angle, new_angle, sends, relays, token_row
+):
     me = here()
     pos_in_cell = me % CELL
     tok_n, width = cache.shape
@@ -180,6 +186,10 @@
     heads_here = KVH // CELL
     key_cols = heads_here * HD
     tokens = me * tok_n + lax.broadcasted_iota(jnp.int32, (tok_n, 1), 0)
+    for k in range(CELL):
+        base = (me - pos_in_cell + (pos_in_cell ^ k)) * tok_n
+        wide_tokens = base + lax.broadcasted_iota(jnp.int32, (1, tok_n), 1)
+        token_row[:, k * tok_n : (k + 1) * tok_n] = row_of(wide_tokens, scal, requests)[0]
     _, prior = row_of(tokens, scal, requests)
     position = jnp.clip(tokens - prior, 0, table_n - 1)
     hot = (lax.broadcasted_iota(jnp.int32, (tok_n, table_n), 1) == position).astype(F32)
@@ -260,44 +270,33 @@
     ).astype(BF16)
 
 
-def scores_body(requests, planes, fetch, lengths, *refs):
+def scores_body(planes, fetch, token_row, *refs):
     qs, kvs, refs = refs[:planes], refs[planes : planes + CELL], refs[planes + CELL :]
-    weights, outs, refs = refs[:3], refs[3 : 3 + planes], refs[3 + planes :]
-    scal, sem, fetch_sem = refs[len(fetch) :]
-    load = pltpu.make_async_copy(lengths, scal, sem.at[0])
-    load.start()
-    fetched = fetch_copies(fetch, weights, refs[: len(fetch)], fetch_sem)
+    weights, outs, refs = refs[:2], refs[2 : 2 + planes], refs[2 + planes :]
+    fetched = fetch_copies(fetch, weights, refs[: len(fetch)], refs[-1])
     for c in fetched:
         c.start()
-    load.wait()
 
     @pl.when(here() >= 0)
     def _():
-        scores_steps(requests, planes, scal, qs, kvs, outs)
+        scores_steps(planes, token_row, qs, kvs, outs)
 
     for c in fetched:
         c.wait()
 
 
-def scores_steps(requests, planes, scal, qs, kvs, outs):
-    me = here()
-    plane, pos_in_cell = me // CELL, me % CELL
+def scores_steps(planes, token_row, qs, kvs, outs):
+    plane = here() // CELL
     rows = qs[0].shape[0]
-    tok_n, both = kvs[0].shape
+    _, both = kvs[0].shape
     key_cols = both // 2
     heads_here = key_cols // HD
     group = QH // KVH
     all_rows = rows * planes
     query = jnp.concatenate([r[...].astype(F32) for r in qs], axis=0).astype(BF16)
-    token_rows = []
-    for k in range(CELL):
-        base = (plane * CELL + (pos_in_cell ^ k)) * tok_n
-        tokens = base + lax.broadcasted_iota(jnp.int32, (1, tok_n), 1)
-        token_rows.append(row_of(tokens, scal, requests)[0])
-    token_row = jnp.concatenate(token_rows, axis=1)
     index = lax.broadcasted_iota(jnp.int32, (group * all_rows, 1), 0)
     query_row = ((index // rows) % planes) ^ plane
-    matching = query_row == token_row
+    matching = query_row == token_row[...]
     lane = lax.broadcasted_iota(jnp.int32, (all_rows, EXTRA), 1)
     extra = jnp.zeros((all_rows, EXTRA), F32)
     count = heads_here * group
@@ -341,8 +340,11 @@
         outs[k][:, count * HD :] = extra[k * rows : (k + 1) * rows].astype(BF16)
 
 
-def regroup_body(planes, *refs):
-    moved, (mine, far, near) = refs[:CELL], refs[CELL:]
+def regroup_body(planes, fetch, *refs):
+    moved, weights, (mine, far, near, *refs) = refs[:CELL], refs[CELL : CELL + 2], refs[CELL + 2 :]
+    fetched = fetch_copies(fetch, weights, refs[: len(fetch)], refs[-1])
+    for c in fetched:
+        c.start()
     plane = here() // CELL
     per = moved[0].shape[0] // planes
     block = CELL * per
@@ -354,10 +356,13 @@
                 for a in range(CELL):
                     out[at + a * per : at + (a + 1) * per] = moved[a][g * per : (g + 1) * per]
 
+    for c in fetched:
+        c.wait()
+
 
 def merge_body(planes, fetch, *refs):
     parts, cat, gain, refs = refs[:planes], *refs[planes : planes + 2], refs[planes + 2 :]
-    weights, norm_out, h_out, refs = refs[:3], *refs[3:5], refs[5:]
+    weights, norm_out, h_out, refs = refs[:2], *refs[2:4], refs[4:]
     fetched = fetch_copies(fetch, weights, refs[: len(fetch)], refs[-1])
     for c in fetched:
         c.start()
@@ -431,90 +436,73 @@
     norm_out[:, wide:] = extra.astype(BF16)
 
 
-def stream(copies, depth):
-    for c in copies[:depth]:
-        c.start()
-
-    def ready(i):
-        copies[i].wait()
-
-    def freed(i):
-        if i + depth < len(copies):
-            copies[i + depth].start()
-
-    return ready, freed
-
-
-def ring_copies(blocks, w_gate, w_up, buf, sem):
-    copies = []
-    for flip, i in blocks:
-        slot = len(copies) % buf.shape[0]
-        src = gate_up_block(flip, i, w_gate, w_up)
-        copies.append(pltpu.make_async_copy(src, buf.at[slot], sem.at[slot]))
-    return copies
-
-
-def gate_up_body(flip, fetch, has_acc, *refs):
-    if has_acc:
-        x, acc_in, held, refs = *refs[:3], refs[3:]
-    else:
-        x, held, acc_in, refs = *refs[:2], None, refs[2:]
-    w_gate, w_up, w_down, acc_out, piece, buf, sem, fetch_sem = refs
+def gate_up_body(flip, held, fetch, has_acc, *refs):
+    x, refs = refs[0], refs[1:]
+    acc_in, refs = (refs[0], refs[1:]) if has_acc else (None, refs)
+    blocks, refs = blocks_of(held, refs[: len(held)]), refs[len(held) :]
+    w_gate, w_up, acc_out, *pieces, fetch_sem = refs
     ff = w_gate.shape[1]
-    n_held = held.shape[0]
-    total = 2 * (x.shape[1] - EXTRA) // GU_ROWS
-    copies = ring_copies([(flip, i) for i in range(n_held, total)], w_gate, w_up, buf, sem)
-    ready, freed = stream(copies, buf.shape[0])
-    fetched = fetch_copies(fetch, (w_gate, w_up, w_down), [piece], fetch_sem)
+    fetched = fetch_copies(fetch, (w_gate, w_up), pieces, fetch_sem)
     for c in fetched:
         c.start()
-    for i in range(total):
-        k = i // 2
-        cols = slice((i % 2) * ff, (i % 2 + 1) * ff)
-        if i >= n_held:
-            ready(i - n_held)
-        w = held[i] if i < n_held else buf[(i - n_held) % buf.shape[0]]
-        part = jnp.dot(x[:, k * GU_ROWS : (k + 1) * GU_ROWS], w, preferred_element_type=F32)
-        if k == 0:
-            acc_out[:, cols] = acc_in[:, cols] + part if has_acc else part
-        else:
-            acc_out[:, cols] += part
-        if i >= n_held:
-            freed(i - n_held)
+
+    @pl.when(here() >= 0)
+    def _():
+        for i in range(2 * (x.shape[1] - EXTRA) // GU_ROWS):
+            k = i // 2
+            cols = slice((i % 2) * ff, (i % 2 + 1) * ff)
+            part = jnp.dot(
+                x[:, k * GU_ROWS : (k + 1) * GU_ROWS],
+                blocks[flip, i][...],
+                preferred_element_type=F32,
+            )
+            if k == 0:
+                acc_out[:, cols] = acc_in[:, cols] + part if has_acc else part
+            else:
+                acc_out[:, cols] += part
+
     for c in fetched:
         c.wait()
 
 
-def rest_body(planes, downs, own, xs, near, far, acc_in, h, held, *refs):
-    down_refs, refs = refs[: len(downs)], refs[len(downs) :]
-    w_gate, w_up, send, keep, acc, out, buf, sem = refs
+def rest_body(planes, held, late, own, xs, near, far, acc_in, h, *refs):
+    blocks, refs = blocks_of(held, refs[: len(held)]), refs[len(held) :]
+    w_gate, w_up, w_down, send, keep, acc, out, buf, sem, dbuf, dsem = refs
     wide = near.shape[1] - EXTRA
     ff = w_gate.shape[1]
     pos = here() % CELL
-    depth = buf.shape[0]
-    n_held = held.shape[0]
+    depth = dbuf.shape[0]
+    fetched = fetch_copies([late], (w_gate, w_up), [buf], sem)
+    downs = []
+    for n in range(out.shape[1] // DOWN_COLS):
+        src = w_down.at[:, n * DOWN_COLS : (n + 1) * DOWN_COLS]
+        downs.append(pltpu.make_async_copy(src, dbuf.at[n % depth], dsem.at[n % depth]))
+    for c in fetched + downs[:depth]:
+        c.start()
     per = 2 * wide // GU_ROWS
-    blocks = [(1, i) for i in range(per)] + [(3, i) for i in range(per)]
-    copies = ring_copies(blocks[n_held:], w_gate, w_up, buf, sem)
-    ready, freed = stream(copies, depth)
-    down_w = {}
-    for (_, first, n, _), r in zip(downs, down_refs):
-        for i in range(n):
-            down_w[first + i] = r.at[pl.ds(i * DOWN_ROWS, DOWN_ROWS), :]
-    for n, (flip, i) in enumerate(blocks):
-        x = near if flip == 1 else far
+    x_of = {1: near, 3: far}
+
+    def add(flip, i, w):
         k = i // 2
         cols = slice((i % 2) * ff, (i % 2 + 1) * ff)
-        if n >= n_held:
-            ready(n - n_held)
-        w = held[n] if n < n_held else buf[(n - n_held) % depth]
-        part = jnp.dot(x[:, k * GU_ROWS : (k + 1) * GU_ROWS], w, preferred_element_type=F32)
-        if n < 2:
+        part = jnp.dot(
+            x_of[flip][:, k * GU_ROWS : (k + 1) * GU_ROWS], w, preferred_element_type=F32
+        )
+        if flip == 1 and k == 0:
             acc[:, cols] = acc_in[:, cols] + part
         else:
             acc[:, cols] += part
-        if n >= n_held:
-            freed(n - n_held)
+
+    @pl.when(pos >= 0)
+    def _():
+        for flip in (1, 3):
+            for i in range(per):
+                if (flip, i) in blocks:
+                    add(flip, i, blocks[flip, i][...])
+
+    for n, c in enumerate(fetched):
+        c.wait()
+        add(late[0], late[1] + n, buf[n])
     squares = jnp.zeros((near.shape[0], 1), F32)
     for x in (own, xs, near, far):
         extra = x[:, wide : wide + EXTRA].astype(F32)
@@ -530,17 +518,13 @@
         ],
         axis=0,
     ).astype(BF16)
-    step = 1024
-    for n in range(out.shape[1] // step):
-        total = None
-        for i in range(ff // DOWN_ROWS):
-            part = jnp.dot(
-                hidden[:, i * DOWN_ROWS : (i + 1) * DOWN_ROWS],
-                down_w[i][:, n * step : (n + 1) * step],
-                preferred_element_type=F32,
-            )
-            total = part if total is None else total + part
-        out[:, n * step : (n + 1) * step] = total
+    for n, c in enumerate(downs):
+        c.wait()
+        out[:, n * DOWN_COLS : (n + 1) * DOWN_COLS] = jnp.dot(
+            hidden, dbuf[n % depth], preferred_element_type=F32
+        )
+        if n + depth < len(downs):
+            downs[n + depth].start()
     per = 2 * planes
     for g in range(CELL):
 
@@ -557,20 +541,17 @@
     keep[...] = mine
 
 
-def halve_body(mine, got, send, send_low, keep):
+def halve_body(mine, got, send, keep):
     total = mine[...] + got[...]
     half = total.shape[0] // 2
     low = (here() % CELL) // 2 == 0
-    other = jnp.where(low, total[half:], total[:half])
-    high = other.astype(BF16)
-    send[...] = high
-    send_low[...] = (other[:2] - high[:2].astype(F32)).astype(BF16)
+    send[...] = jnp.where(low, total[half:], total[:half]).astype(BF16)
     keep[...] = jnp.where(low, total[:half], total[half:])
 
 
-def spread_body(planes, mine, got, got_low, *outs):
+def spread_body(planes, mine, got, *outs):
     total = mine[...] + got[...].astype(F32)
-    outs[0][...] = total[0:2] + got_low[...].astype(F32)
+    outs[0][...] = total[0:2]
     for k in range(1, planes):
         outs[k][...] = total[2 * k : 2 * k + 2].astype(BF16)
 
@@ -582,8 +563,9 @@
     refs[-1][...] = total.astype(BF16)
 
 
-def swap(x, k, devices):
-    return lax.ppermute(x, "ctx", [(i, i ^ k) for i in range(devices)])
+def swap(x, k, devices, sends=None):
+    pairs = [(i, i ^ k) for i in range(devices) if sends is None or sends(i)]
+    return lax.ppermute(x, "ctx", pairs)
 
 
 def cells_program(*args):
@@ -615,37 +597,43 @@
     cell_rows = rows_dev * CELL
     all_rows = cell_rows * planes
     ff = w_gate.shape[1]
-    w_gate, w_up, w_down = in_hbm(w_gate), in_hbm(w_up), in_hbm(w_down)
-    weights = (w_gate, w_up, w_down)
-    n_down = ff // DOWN_ROWS
+    weights = (in_hbm(w_gate), in_hbm(w_up))
+    per = 2 * wide // GU_ROWS
     plans = {
-        "turn": [("down", 0, 2, model)],
-        "warm_q": [("down", 2, 3, model)],
-        "scores": [("down", 5, n_down - 5, model)],
-        "merge": [(0, 0, 2, ff)],
-        "gate_up_own": [(2, 0, 2, ff)],
-        "gate_up_x": [(1, 0, 2, ff)],
+        "turn": [(0, 0, 4, ff)],
+        "warm_q": [(0, 4, 2, ff)],
+        "scores": [(0, 6, per - 6, ff)],
+        "merge": [(2, 0, 2, ff)],
+        "regroup": [(2, 2, 2, ff)],
+        "gate_up_own": [(2, 4, per - 4, ff), (1, 0, 4, ff)],
+        "gate_up_x": [(1, 4, per - 4, ff), (3, 0, 4, ff)],
+        "rest": [(3, 4, per - 4, ff)],
     }
     held = []
 
     def keep_pieces(name, values):
         held.extend(zip(plans[name], values))
 
+    def pieces_for(*flips):
+        found = [h for h in held if h[0][0] in flips]
+        return [h[0] for h in found], [in_vmem(h[1]) for h in found]
+
+    def has_tokens(i):
+        return i < devices // 2
+
     def warm(name, dep):
         plan = plans[name]
-        keep_pieces(
-            name,
-            call(
-                lambda *r: warm_body(plan, *r),
-                [hbm()] * 4,
-                [],
-                (dep, *weights),
-                1,
-                [pltpu.SemaphoreType.DMA((count_of(plan),))],
-                plan,
-                8,
-            ),
+        values = call(
+            lambda *r: warm_body(plan, *r),
+            [hbm()] * 3,
+            [],
+            (dep, *weights),
+            1,
+            [pltpu.SemaphoreType.DMA((count_of(plan),))],
+            plan,
+            8,
         )
+        keep_pieces(name, values)
 
     sources = (queries, new_kv, resid, gain.reshape(model // HD, HD))
     prepared = call(
@@ -662,9 +650,10 @@
     sources = (lengths, new_slot[None, :], old_cache, old_angle.T, new_angle.T)
     turned = call(
         lambda *r: turn_body(requests, devices, plan, *r),
-        [hbm()] * 8,
+        [hbm()] * 7,
         [((tok_n, 2 * key_cols), BF16)] * CELL
-        + [((tok_n // CELL, width + EXTRA), BF16)] * CELL,
+        + [((tok_n // CELL, width + EXTRA), BF16)] * CELL
+        + [((1, CELL * tok_n), jnp.int32)],
         (*[in_hbm(x) for x in sources], *weights),
         10,
         [pltpu.SMEM(lengths.shape, lengths.dtype)]
@@ -674,8 +663,9 @@
         8,
     )
     sends, relays = turned[:CELL], turned[CELL : 2 * CELL]
-    keep_pieces("turn", turned[2 * CELL :])
-    kvs = [sends[0]] + [swap(sends[k], k, devices) for k in range(1, CELL)]
+    token_row = turned[2 * CELL]
+    keep_pieces("turn", turned[2 * CELL + 1 :])
+    kvs = [sends[0]] + [swap(sends[k], k, devices, has_tokens) for k in range(1, CELL)]
     cat, own_q = call(
         assemble_body,
         [vmem()] * CELL,
@@ -683,30 +673,29 @@
         tuple(msgs),
         4,
     )
-    qs = [own_q] + [swap(own_q, CELL * k, devices) for k in range(1, planes)]
+    qs = [own_q] + [
+        swap(own_q, CELL * k, devices, lambda i: has_tokens(i ^ (CELL * k)))
+        for k in range(1, planes)
+    ]
     warm("warm_q", own_q)
-    relays = [relays[0]] + [swap(relays[k], k, devices) for k in range(1, CELL)]
+    relays = [relays[0]] + [swap(relays[k], k, devices, has_tokens) for k in range(1, CELL)]
     plan = plans["scores"]
     parts = call(
-        lambda *r: scores_body(requests, planes, plan, *r),
-        [hbm()] + [vmem()] * (planes + CELL) + [hbm()] * 3,
+        lambda *r: scores_body(planes, plan, *r),
+        [vmem()] * (1 + planes + CELL) + [hbm()] * 2,
         [((cell_rows, wide + EXTRA), BF16)] * planes,
-        (in_hbm(lengths), *qs, *kvs, *weights),
+        (token_row, *qs, *kvs, *weights),
         10,
-        [
-            pltpu.SMEM(lengths.shape, lengths.dtype),
-            pltpu.SemaphoreType.DMA((1,)),
-            pltpu.SemaphoreType.DMA((count_of(plan),)),
-        ],
+        [pltpu.SemaphoreType.DMA((count_of(plan),))],
         plan,
         5,
     )
     keep_pieces("scores", parts[planes:])
-    parts = [parts[0]] + [swap(parts[k], CELL * k, devices) for k in range(1, planes)]
+    parts = [parts[0]] + [swap(parts[k], CELL * k, devices, has_tokens) for k in range(1, planes)]
     plan = plans["merge"]
     merged = call(
         lambda *r: merge_body(planes, plan, *r),
-        [vmem()] * (planes + 2) + [hbm()] * 3,
+        [vmem()] * (planes + 2) + [hbm()] * 2,
         [((cell_rows, wide + EXTRA), BF16), ((cell_rows, wide), F32)],
         (*parts, cat, own_gain, *weights),
         6,
@@ -714,49 +703,55 @@
         plan,
         4,
     )
-    normed, hstate, own_held = merged
+    normed, hstate = merged[:2]
+    keep_pieces("merge", merged[2:])
     block = tok_n // planes
-    relay_mine, relay_far, relay_near = call(
-        lambda *r: regroup_body(planes, *r),
-        [vmem()] * CELL,
+    regroup_plan = plans["regroup"]
+    grouped = call(
+        lambda *r: regroup_body(planes, regroup_plan, *r),
+        [vmem()] * CELL + [hbm()] * 2,
         [((n * block, width + EXTRA), BF16) for n in (1, 2, 1)],
-        tuple(relays),
+        (*relays, *weights),
         4,
-    )
-    relay_far = swap(relay_far, 2 * CELL, devices)
+        [pltpu.SemaphoreType.DMA((count_of(regroup_plan),))],
+        regroup_plan,
+        4,
+    )
+    relay_mine, relay_far, relay_near = grouped[:3]
+    keep_pieces("regroup", grouped[3:])
+    relay_far = swap(relay_far, 2 * CELL, devices, has_tokens)
     blocks = [normed] + [swap(normed, CELL * k, devices) for k in range(1, planes)]
     own = jnp.concatenate(blocks, axis=0)
     across = swap(own, 2, devices)
     near = swap(own, 1, devices)
-    gu_scratch = [pltpu.VMEM((6, GU_ROWS, ff), BF16), pltpu.SemaphoreType.DMA((6,))]
-    fetch_sem = [pltpu.SemaphoreType.DMA((2,))]
-    acc, x_held = call(
-        lambda *r: gate_up_body(0, plans["gate_up_own"], False, *r),
-        [vmem()] * 2 + [hbm()] * 3,
-        [((all_rows, 2 * ff), F32)],
-        (own, in_vmem(own_held), *weights),
-        12,
-        gu_scratch + fetch_sem,
-        plans["gate_up_own"],
-        14,
-    )
+
+    def gate_up(name, flip, x, acc):
+        specs, values = pieces_for(flip)
+        plan = plans[name]
+        more = [] if acc is None else [acc]
+        acc, *pieces = call(
+            lambda *r: gate_up_body(flip, specs, plan, len(more) > 0, *r),
+            [vmem()] * (1 + len(more) + len(values)) + [hbm()] * 2,
+            [((all_rows, 2 * ff), F32)],
+            (x, *more, *values, *weights),
+            4,
+            [pltpu.SemaphoreType.DMA((count_of(plan),))],
+            plan,
+            14,
+        )
+        keep_pieces(name, pieces)
+        return acc
+
+    acc = gate_up("gate_up_own", 0, own, None)
     far = swap(across, 1, devices)
-    acc, near_held = call(
-        lambda *r: gate_up_body(2, plans["gate_up_x"], True, *r),
-        [vmem()] * 3 + [hbm()] * 3,
-        [((all_rows, 2 * ff), F32)],
-        (across, acc, in_vmem(x_held), *weights),
-        12,
-        gu_scratch + fetch_sem,
-        plans["gate_up_x"],
-        14,
-    )
+    acc = gate_up("gate_up_x", 2, across, acc)
     relay_near = jnp.concatenate([relay_near, relay_far[block:]], axis=0)
     relay_near = swap(relay_near, CELL, devices)
-    downs = [h for h in held if h[0][0] == "down"]
+    specs, values = pieces_for(1, 3)
+    late = plans["rest"][0]
     send, keep = call(
-        lambda *r: rest_body(planes, [h[0] for h in downs], *r),
-        [vmem()] * (7 + len(downs)) + [hbm()] * 2,
+        lambda *r: rest_body(planes, specs, late, *r),
+        [vmem()] * (6 + len(values)) + [hbm()] * 3,
         [((all_rows // 2, model), F32)] * 2,
         (
             own,
@@ -765,36 +760,36 @@
             in_vmem(far),
             acc,
             hstate,
-            in_vmem(near_held),
-            *[in_vmem(h[1]) for h in downs],
-            w_gate,
-            w_up,
+            *values,
+            *weights,
+            in_hbm(w_down),
         ),
-        18,
+        32,
         [
             pltpu.VMEM((all_rows, 2 * ff), F32),
             pltpu.VMEM((all_rows, model), F32),
-            pltpu.VMEM((8, GU_ROWS, ff), BF16),
-            pltpu.SemaphoreType.DMA((8,)),
+            pltpu.VMEM(piece_shape(late), BF16),
+            pltpu.SemaphoreType.DMA((count_of([late]),)),
+            pltpu.VMEM((6, ff, DOWN_COLS), BF16),
+            pltpu.SemaphoreType.DMA((6,)),
         ],
         moved=40,
         on_chip=True,
     )
     got = swap(send, 1, devices)
-    send, send_low, keep = call(
+    send, keep = call(
         lambda *r: halve_body(*r),
         [vmem(), vmem()],
-        [((all_rows // 4, model), BF16), ((rows_dev, model), BF16), ((all_rows // 4, model), F32)],
+        [((all_rows // 4, model), BF16), ((all_rows // 4, model), F32)],
         (in_vmem(keep), got),
         8,
     )
     got = swap(send, 2, devices)
-    got_low = swap(send_low, 2, devices)
     pieces = call(
         lambda *r: spread_body(planes, *r),
-        [vmem()] * 3,
+        [vmem()] * 2,
         [((rows_dev, model), F32)] + [((rows_dev, model), BF16)] * (planes - 1),
-        (keep, got, got_low),
+        (keep, got),
         8,
     )
     pieces = [pieces[0]] + [swap(pieces[k], CELL * k, devices) for k in range(1, planes)]

time: 108 us -> 114 us (1.056)
  starting transfers between devices: 35.8 us -> 47.8 us
  waiting for transfers between devices: 28.4 us -> 21.7 us
  local copies, waits for them, and re-layouts: 0.04 us -> 1.42 us
  Pallas kernels: 42.8 us -> 41.6 us
    ppermute x29 -> x28, starting transfers between devices: 35.8 us -> 47.8 us  [swap(): return lax.ppermute(x, 'ctx', pairs)]
    ppermute x29 -> x28, waiting for transfers between devices: 28.4 us -> 21.7 us  [swap(): return lax.ppermute(x, 'ctx', pairs)]
    unnamed x3 -> x11, local copies, waits for them, and re-layouts: 0.02 us -> 1.4 us
    pallas_call x14, Pallas kernels: 42.8 us -> 41.6 us  [call(): pl.pallas_call(body, in_specs=ins, out_specs=[vmem() for _ in shapes], ou...]
  transfers between devices with their start and end apart: 29 -> 28, of which waited for: 12 -> 9; matrix products, arithmetic and copies ran while one was open for 0% -> 0% of each run, Pallas kernels for 32% -> 31%
where the time goes in v2:
time: 114 us; the launch traced here: 113 us
  starting transfers between devices  47.8 us (42%)
  Pallas kernels  41.6 us (36%)
  waiting for transfers between devices  21.7 us (19%)
  local copies, waits for them, and re-layouts  1.42 us (1%)
    ppermute x28, starting transfers between devices, swap(): return lax.ppermute(x, 'ctx', pairs)  47.8 us
    pallas_call x14, Pallas kernels, call(): pl.pallas_call(body, in_specs=ins, out_specs=[vmem() for _ in shapes], ou...  41.6 us
    ppermute x28, waiting for transfers between devices, swap(): return lax.ppermute(x, 'ctx', pairs)  21.7 us
  transfers between devices with their start and end apart: 28, of which 9 were waited for; matrix products, arithmetic and copies ran while one was open for 0% of the time, Pallas kernels for 31%

profile of v2, /device:TPU:0, one launch (start us, length us, event | category | flops | bytes accessed | tf_op | source)
XLA Modules:
  0.0 113.5 jit_solution(808308966748076327)
XLA Ops:
  0.6 3.5 %shard_map.131 = (bf16[128,512]{1,0:T(8,128)(2,1)S(1)}, bf16[128,512]{1,0:T(8,128)(2,1)S(1)}, bf16[128,512]{1,0:T(8,128)(2,1)S(1)}, bf16[128,512]{1,0:T(8,128)(2...) custom-call(s32[4]{0:T(128)} %r_0_.1, ...), custom_call_target="tpu_custom_call" | custom-call | bytes 8388608 | tf_op jit(solution)/shard_map/pallas_call | solution.py:40
  4.2 2.4 %collective-permute-start.11 = (bf16[128,512]{1,0:T(8,128)(2,1)S(1)}, bf16[128,512]{1,0:T(8,128)(2,1)S(1)}, u32[]{:S(2)}, u32[]{:S(2)}) collective-permute-start(bf16[128,512]{1,0:T(8,128)(2,1)S(1)} %get-tuple-element.59), channel_id=1, source_target_pairs={{0,1},{1,0},{2,3},{3,2},{4,5},{5,4},{6,7},{7,6},{16,17},{17,16},{1... | collective-permute-start | bytes 393224 | tf_op jit(solution)/shard_map/ppermute | solution.py:568
  6.6 4.4 %collective-permute-start.12 = (bf16[128,512]{1,0:T(8,128)(2,1)S(1)}, bf16[128,512]{1,0:T(8,128)(2,1)S(1)}, u32[]{:S(2)}, u32[]{:S(2)}) collective-permute-start(bf16[128,512]{1,0:T(8,128)(2,1)S(1)} %get-tuple-element.60), channel_id=1, source_target_pairs={{0,2},{1,3},{2,0},{3,1},{4,6},{5,7},{6,4},{7,5},{16,18},{17,19},{1... | collective-permute-start | bytes 393224 | tf_op jit(solution)/shard_map/ppermute | solution.py:568
  11.0 2.0 %collective-permute-start.13 = (bf16[128,512]{1,0:T(8,128)(2,1)S(1)}, bf16[128,512]{1,0:T(8,128)(2,1)S(1)}, u32[]{:S(2)}, u32[]{:S(2)}) collective-permute-start(bf16[128,512]{1,0:T(8,128)(2,1)S(1)} %get-tuple-element.61), channel_id=1, source_target_pairs={{0,3},{1,2},{2,1},{3,0},{4,7},{5,6},{6,5},{7,4},{16,19},{17,18},{1... | collective-permute-start | bytes 393224 | tf_op jit(solution)/shard_map/ppermute | solution.py:568
  14.2 1.9 %collective-permute-start.6 = (bf16[2,4608]{1,0:T(2,128)(2,1)S(1)}, bf16[2,4608]{1,0:T(2,128)(2,1)S(1)}, u32[]{:S(2)}, u32[]{:S(2)}) collective-permute-start(bf16[2,4608]{1,0:T(2,128)(2,1)S(1)} %get-tuple-element.55), channel_id=1, source_target_pairs={{0,2},{1,3},{2,0},{3,1},{4,6},{5,7},{6,4},{7,5},{8,10},{9,11},{10,... | collective-permute-start | bytes 55304 | tf_op jit(solution)/shard_map/ppermute | solution.py:568
  16.9 2.1 %collective-permute-done.6.refs_2_ = bf16[2,4608]{1,0:T(2,128)(2,1)S(1)} collective-permute-done((bf16[2,4608]{1,0:T(2,128)(2,1)S(1)}, bf16[2,4608]{1,0:T(2,128)(2,1)S(1)}, u32[]{:S(2)}, u32[]{:S(2)}) %collective-permute-start.6) | collective-permute-done | bytes 18464 | tf_op jit(solution)/shard_map/ppermute | solution.py:568
  19.5 1.3 %collective-permute-start.10 = (bf16[8,2048]{1,0:T(8,128)(2,1)S(1)}, bf16[8,2048]{1,0:T(8,128)(2,1)S(1)}, u32[]{:S(2)}, u32[]{:S(2)}) collective-permute-start(bf16[8,2048]{1,0:T(8,128)(2,1)S(1)} %get-tuple-element.57.r_1_.r_0_), channel_id=1, source_target_pairs={{8,4},{9,5},{10,6},{11,7},{12,0},{13,1},{14,2},{15,3},{24,20},{25,... | collective-permute-start | bytes 98312 | tf_op jit(solution)/shard_map/ppermute | solution.py:568
  20.8 1.3 %collective-permute-start.9 = (bf16[8,2048]{1,0:T(8,128)(2,1)S(1)}, bf16[8,2048]{1,0:T(8,128)(2,1)S(1)}, u32[]{:S(2)}, u32[]{:S(2)}) collective-permute-start(bf16[8,2048]{1,0:T(8,128)(2,1)S(1)} %get-tuple-element.57.r_1_.r_0_), channel_id=1, source_target_pairs={{8,0},{9,1},{10,2},{11,3},{12,4},{13,5},{14,6},{15,7},{24,16},{25,... | collective-permute-start | bytes 98312 | tf_op jit(solution)/shard_map/ppermute | solution.py:568
  22.1 5.1 %collective-permute-done.10.r_4_ = bf16[8,2048]{1,0:T(8,128)(2,1)S(1)} collective-permute-done((bf16[8,2048]{1,0:T(8,128)(2,1)S(1)}, bf16[8,2048]{1,0:T(8,128)(2,1)S(1)}, u32[]{:S(2)}, u32[]{:S(2)}) %collective-permute-start.10) | collective-permute-done | bytes 32800 | tf_op jit(solution)/shard_map/ppermute | solution.py:568
  27.2 2.1 %collective-permute-start.8 = (bf16[8,2048]{1,0:T(8,128)(2,1)S(1)}, bf16[8,2048]{1,0:T(8,128)(2,1)S(1)}, u32[]{:S(2)}, u32[]{:S(2)}) collective-permute-start(bf16[8,2048]{1,0:T(8,128)(2,1)S(1)} %get-tuple-element.57.r_1_.r_0_), channel_id=1, source_target_pairs={{0,4},{1,5},{2,6},{3,7},{4,0},{5,1},{6,2},{7,3},{16,20},{17,21},{1... | collective-permute-start | bytes 98312 | tf_op jit(solution)/shard_map/ppermute | solution.py:568
  29.3 3.7 %collective-permute-done.8.r_2_ = bf16[8,2048]{1,0:T(8,128)(2,1)S(1)} collective-permute-done((bf16[8,2048]{1,0:T(8,128)(2,1)S(1)}, bf16[8,2048]{1,0:T(8,128)(2,1)S(1)}, u32[]{:S(2)}, u32[]{:S(2)}) %collective-permute-start.8) | collective-permute-done | bytes 32800 | tf_op jit(solution)/shard_map/ppermute | solution.py:568
  33.0 2.1 %shard_map.136 = (bf16[8,2176]{1,0:T(8,128)(2,1)S(1)}, bf16[8,2176]{1,0:T(8,128)(2,1)S(1)}, bf16[8,2176]{1,0:T(8,128)(2,1)S(1)}, bf16[8,2176]{1,0:T(8,128)(2,1)S(1)}, bf16[2,512,1792]{2,1,0:T(8,128)(2,1)S(1)}) custom-call(s32[1,512]{1,0:T(1,128)S(1)} %get-tuple-element.52.r_0_, bf16[8,2048]{1,0:T(8,128)(2,1)S(1)} %get-tuple-element.57.r_1_.r_0_, ...), custom_call_target="tpu_custom_call" | custom-call | bytes 5242880 | tf_op jit(solution)/shard_map/pallas_call | solution.py:40
  35.1 2.1 %collective-permute-start.14 = (bf16[8,2176]{1,0:T(8,128)(2,1)S(1)}, bf16[8,2176]{1,0:T(8,128)(2,1)S(1)}, u32[]{:S(2)}, u32[]{:S(2)}) collective-permute-start(bf16[8,2176]{1,0:T(8,128)(2,1)S(1)} %get-tuple-element.63), channel_id=1, source_target_pairs={{0,4},{1,5},{2,6},{3,7},{4,0},{5,1},{6,2},{7,3},{16,20},{17,21},{1... | collective-permute-start | bytes 104456 | tf_op jit(solution)/shard_map/ppermute | solution.py:568
  37.2 1.3 %collective-permute-start.15 = (bf16[8,2176]{1,0:T(8,128)(2,1)S(1)}, bf16[8,2176]{1,0:T(8,128)(2,1)S(1)}, u32[]{:S(2)}, u32[]{:S(2)}) collective-permute-start(bf16[8,2176]{1,0:T(8,128)(2,1)S(1)} %get-tuple-element.64), channel_id=1, source_target_pairs={{0,8},{1,9},{2,10},{3,11},{4,12},{5,13},{6,14},{7,15},{16,24},{17,... | collective-permute-start | bytes 104456 | tf_op jit(solution)/shard_map/ppermute | solution.py:568
  39.8 1.9 %collective-permute-start = (bf16[32,2176]{1,0:T(8,128)(2,1)S(1)}, bf16[32,2176]{1,0:T(8,128)(2,1)S(1)}, u32[]{:S(2)}, u32[]{:S(2)}) collective-permute-start(bf16[32,2176]{1,0:T(8,128)(2,1)S(1)} %get-tuple-element.46), channel_id=1, source_target_pairs={{0,1},{1,0},{2,3},{3,2},{4,5},{5,4},{6,7},{7,6},{16,17},{17,16},{1... | collective-permute-start | bytes 417800 | tf_op jit(solution)/shard_map/ppermute | solution.py:568
  41.7 3.1 %collective-permute-start.1 = (bf16[32,2176]{1,0:T(8,128)(2,1)S(1)}, bf16[32,2176]{1,0:T(8,128)(2,1)S(1)}, u32[]{:S(2)}, u32[]{:S(2)}) collective-permute-start(bf16[32,2176]{1,0:T(8,128)(2,1)S(1)} %get-tuple-element.47), channel_id=1, source_target_pairs={{0,2},{1,3},{2,0},{3,1},{4,6},{5,7},{6,4},{7,5},{16,18},{17,19},{1... | collective-permute-start | bytes 417800 | tf_op jit(solution)/shard_map/ppermute | solution.py:568
  44.8 2.6 %collective-permute-start.2 = (bf16[32,2176]{1,0:T(8,128)(2,1)S(1)}, bf16[32,2176]{1,0:T(8,128)(2,1)S(1)}, u32[]{:S(2)}, u32[]{:S(2)}) collective-permute-start(bf16[32,2176]{1,0:T(8,128)(2,1)S(1)} %get-tuple-element.48), channel_id=1, source_target_pairs={{0,3},{1,2},{2,1},{3,0},{4,7},{5,6},{6,5},{7,4},{16,19},{17,18},{1... | collective-permute-start | bytes 417800 | tf_op jit(solution)/shard_map/ppermute | solution.py:568
  47.4 2.1 %shard_map.137 = (bf16[8,2176]{1,0:T(8,128)(2,1)S(1)}, f32[8,2048]{1,0:T(8,128)S(1)}, bf16[2,512,1792]{2,1,0:T(8,128)(2,1)S(1)}) custom-call(bf16[8,2176]{1,0:T(8,128)(2,1)S(1)} %get-tuple-element.62.r_0_, bf16[8,2176]{1,0:T(8,128)(2,1)S(1)} %collective-permute-done.14.r_1_, bf16[8,2176]{1,0:T(8,128)(2,1)S(1)} %collective-permute-done.15.r_2_, ...), custom_call_target="tpu_custom_call" | custom-call | bytes 4194304 | tf_op jit(solution)/shard_map/pallas_call | solution.py:40
  50.1 1.9 %collective-permute-start.17 = (bf16[8,2176]{1,0:T(8,128)(2,1)S(1)}, bf16[8,2176]{1,0:T(8,128)(2,1)S(1)}, u32[]{:S(2)}, u32[]{:S(2)}) collective-permute-start(bf16[8,2176]{1,0:T(8,128)(2,1)S(1)} %get-tuple-element.68), channel_id=1, source_target_pairs={{0,4},{1,5},{2,6},{3,7},{4,0},{5,1},{6,2},{7,3},{8,12},{9,13},{10,... | collective-permute-start | bytes 104456 | tf_op jit(solution)/shard_map/ppermute | solution.py:568
  52.0 2.1 %collective-permute-done.17 = bf16[8,2176]{1,0:T(8,128)(2,1)S(1)} collective-permute-done((bf16[8,2176]{1,0:T(8,128)(2,1)S(1)}, bf16[8,2176]{1,0:T(8,128)(2,1)S(1)}, u32[]{:S(2)}, u32[]{:S(2)}) %collective-permute-start.17) | collective-permute-done | bytes 34848 | tf_op jit(solution)/shard_map/ppermute | solution.py:568
  54.0 3.3 %collective-permute-start.18 = (bf16[8,2176]{1,0:T(8,128)(2,1)S(1)}, bf16[8,2176]{1,0:T(8,128)(2,1)S(1)}, u32[]{:S(2)}, u32[]{:S(2)}) collective-permute-start(bf16[8,2176]{1,0:T(8,128)(2,1)S(1)} %get-tuple-element.68), channel_id=1, source_target_pairs={{0,8},{1,9},{2,10},{3,11},{4,12},{5,13},{6,14},{7,15},{8,0},{9,1},... | collective-permute-start | bytes 104456 | tf_op jit(solution)/shard_map/ppermute | solution.py:568
  57.4 1.9 %collective-permute-done.18 = bf16[8,2176]{1,0:T(8,128)(2,1)S(1)} collective-permute-done((bf16[8,2176]{1,0:T(8,128)(2,1)S(1)}, bf16[8,2176]{1,0:T(8,128)(2,1)S(1)}, u32[]{:S(2)}, u32[]{:S(2)}) %collective-permute-start.18) | collective-permute-done | bytes 34848 | tf_op jit(solution)/shard_map/ppermute | solution.py:568
  60.2 2.1 %shard_map.132 = (bf16[32,2176]{1,0:T(8,128)(2,1)S(1)}, bf16[64,2176]{1,0:T(8,128)(2,1)S(1)}, bf16[32,2176]{1,0:T(8,128)(2,1)S(1)}, bf16[2,512,1792]{2,1,0:T(8,128)(2,1)S(1)}) custom-call(bf16[32,2176]{1,0:T(8,128)(2,1)S(1)} %get-tuple-element.45.r_0_, bf16[32,2176]{1,0:T(8,128)(2,1)S(1)} %collective-permute-done.r_1_, ...), custom_call_target="tpu_custom_call" | custom-call | bytes 4194304 | tf_op jit(solution)/shard_map/pallas_call | solution.py:40
  62.3 4.8 %collective-permute-start.3 = (bf16[64,2176]{1,0:T(8,128)(2,1)S(1)}, bf16[64,2176]{1,0:T(8,128)(2,1)S(1)}, u32[]{:S(2)}, u32[]{:S(2)}) collective-permute-start(bf16[64,2176]{1,0:T(8,128)(2,1)S(1)} %get-tuple-element.50), channel_id=1, source_target_pairs={{0,8},{1,9},{2,10},{3,11},{4,12},{5,13},{6,14},{7,15},{16,24},{17,... | collective-permute-start | bytes 835592 | tf_op jit(solution)/shard_map/ppermute | solution.py:568
  67.7 2.1 %shard_map.138.r_2_ = bf16[2,512,1792]{2,1,0:T(8,128)(2,1)S(1)} custom-call(bf16[8,2048]{1,0:T(8,128)(2,1)S(1)} %get-tuple-element.57.r_1_.r_0_, bf16[8192,1792]{1,0:T(8,128)(2,1)} %r_9_.3, bf16[8192,1792]{1,0:T(8,128)(2,1)} %r_10_.3), custom_call_target="tpu_custom_call" | custom-call | bytes 8388608 | tf_op jit(solution)/shard_map/pallas_call | solution.py:40
  69.8 5.3 %shard_map.139 = (f32[32,3584]{1,0:T(8,128)S(1)}, bf16[4,512,1792]{2,1,0:T(8,128)(2,1)S(1)}, bf16[4,512,1792]{2,1,0:T(8,128)(2,1)S(1)}) custom-call(bf16[32,2176]{1,0:T(8,128)(2,1)S(1)} %constant_dynamic-update-slice_fusion.r_0_, bf16[4,512,1792]{2,1,0:T(8,128)(2,1)S(1)} %get-tuple-element.69.r_1_, bf16[2,512,1792]{2,1,0:T(8,128)(2,1)S(1)} %shard_map.138.r_2_, ...), custom_call_target="tpu_custom_call" | custom-call | bytes 14680064 | tf_op jit(solution)/shard_map/pallas_call | solution.py:40
  75.2 5.3 %shard_map.140 = (f32[32,3584]{1,0:T(8,128)S(1)}, bf16[4,512,1792]{2,1,0:T(8,128)(2,1)S(1)}, bf16[4,512,1792]{2,1,0:T(8,128)(2,1)S(1)}) custom-call(bf16[32,2176]{1,0:T(8,128)(2,1)S(1)} %collective-permute-done.20.r_0_.r_1_, f32[32,3584]{1,0:T(8,128)S(1)} %get-tuple-element.71.r_1_, bf16[2,512,1792]{2,1,0:T(8,128)(2,1)S(1)} %get-tuple-element.72.r_2_, ...), custom_call_target="tpu_custom_call" | custom-call | bytes 14680064 | tf_op jit(solution)/shard_map/pallas_call | solution.py:40
  81.3 16.2 %shard_map.141 = (f32[16,8192]{1,0:T(8,128)S(1)}, f32[16,8192]{1,0:T(8,128)S(1)}) custom-call(bf16[32,2176]{1,0:T(8,128)(2,1)} %copy-done, bf16[32,2176]{1,0:T(8,128)(2,1)} %copy-done.1, bf16[32,2176]{1,0:T(8,128)(2,1)S(1)} %collective-permute-done.21.r_2_, bf16[32,2176]{1,0:T(8,128)(2,1)S(1)} %collective-permute-done.22.r_3_, f32[32,3584]{1,0:T(8,128)} %copy-done.2, ...), custom_call_target="tpu_custom_call" | custom-call | bytes 41943040 | tf_op jit(solution)/shard_map/pallas_call | solution.py:40
  97.7 1.9 %collective-permute-start.4 = (bf16[64,2176]{1,0:T(8,128)(2,1)S(1)}, bf16[64,2176]{1,0:T(8,128)(2,1)S(1)}, u32[]{:S(2)}, u32[]{:S(2)}) collective-permute-start(bf16[64,2176]{1,0:T(8,128)(2,1)S(1)} %pad_maximum_fusion), channel_id=1, source_target_pairs={{0,4},{1,5},{2,6},{3,7},{4,0},{5,1},{6,2},{7,3},{8,12},{9,13},{10,... | collective-permute-start | bytes 835592 | tf_op jit(solution)/shard_map/ppermute | solution.py:568
  100.9 4.3 %collective-permute-done.24.r_1_ = bf16[8,8192]{1,0:T(8,128)(2,1)S(1)} collective-permute-done((bf16[8,8192]{1,0:T(8,128)(2,1)S(1)}, bf16[8,8192]{1,0:T(8,128)(2,1)S(1)}, u32[]{:S(2)}, u32[]{:S(2)}) %collective-permute-start.24) | collective-permute-done | bytes 131104 | tf_op jit(solution)/shard_map/ppermute | solution.py:568
  105.3 1.8 %collective-permute-start.25 = (bf16[2,8192]{1,0:T(2,128)(2,1)S(1)}, bf16[2,8192]{1,0:T(2,128)(2,1)S(1)}, u32[]{:S(2)}, u32[]{:S(2)}) collective-permute-start(bf16[2,8192]{1,0:T(2,128)(2,1)S(1)} %get-tuple-element.85), channel_id=1, source_target_pairs={{0,4},{1,5},{2,6},{3,7},{4,0},{5,1},{6,2},{7,3},{8,12},{9,13},{10,... | collective-permute-start | bytes 98312 | tf_op jit(solution)/shard_map/ppermute | solution.py:568
  107.1 2.7 %collective-permute-start.27 = (bf16[2,8192]{1,0:T(2,128)(2,1)S(1)}, bf16[2,8192]{1,0:T(2,128)(2,1)S(1)}, u32[]{:S(2)}, u32[]{:S(2)}) collective-permute-start(bf16[2,8192]{1,0:T(2,128)(2,1)S(1)} %get-tuple-element.87), channel_id=1, source_target_pairs={{0,12},{1,13},{2,14},{3,15},{4,8},{5,9},{6,10},{7,11},{8,4},{9,5},... | collective-permute-start | bytes 98312 | tf_op jit(solution)/shard_map/ppermute | solution.py:568
  (52 shorter events, 11.9 us)
Async XLA Ops:
  4.2 28.8 %collective-permute-start.11 = (bf16[128,512]{1,0:T(8,128)(2,1)S(1)}, bf16[128,512]{1,0:T(8,128)(2,1)S(1)}, u32[]{:S(2)}, u32[]{:S(2)}) collective-permute-start(bf16[128,512]{1,0:T(8,128)(2,1)S(1)} %get-tuple-element.59), channel_id=1, source_target_pairs={{0,1},{1,0},{2,3},{3,2},{4,5},{5,4},{6,7},{7,6},{16,17},{17,16},{1... | collective-permute-start | bytes 393224 | tf_op jit(solution)/shard_map/ppermute | solution.py:568
  6.6 26.4 %collective-permute-start.12 = (bf16[128,512]{1,0:T(8,128)(2,1)S(1)}, bf16[128,512]{1,0:T(8,128)(2,1)S(1)}, u32[]{:S(2)}, u32[]{:S(2)}) collective-permute-start(bf16[128,512]{1,0:T(8,128)(2,1)S(1)} %get-tuple-element.60), channel_id=1, source_target_pairs={{0,2},{1,3},{2,0},{3,1},{4,6},{5,7},{6,4},{7,5},{16,18},{17,19},{1... | collective-permute-start | bytes 393224 | tf_op jit(solution)/shard_map/ppermute | solution.py:568
  11.0 22.0 %collective-permute-start.13 = (bf16[128,512]{1,0:T(8,128)(2,1)S(1)}, bf16[128,512]{1,0:T(8,128)(2,1)S(1)}, u32[]{:S(2)}, u32[]{:S(2)}) collective-permute-start(bf16[128,512]{1,0:T(8,128)(2,1)S(1)} %get-tuple-element.61), channel_id=1, source_target_pairs={{0,3},{1,2},{2,1},{3,0},{4,7},{5,6},{6,5},{7,4},{16,19},{17,18},{1... | collective-permute-start | bytes 393224 | tf_op jit(solution)/shard_map/ppermute | solution.py:568
  14.0 2.1 %collective-permute-start.5 = (bf16[2,4608]{1,0:T(2,128)(2,1)S(1)}, bf16[2,4608]{1,0:T(2,128)(2,1)S(1)}, u32[]{:S(2)}, u32[]{:S(2)}) collective-permute-start(bf16[2,4608]{1,0:T(2,128)(2,1)S(1)} %get-tuple-element.54), channel_id=1, source_target_pairs={{0,1},{1,0},{2,3},{3,2},{4,5},{5,4},{6,7},{7,6},{8,9},{9,8},{10,11... | collective-permute-start | bytes 55304 | tf_op jit(solution)/shard_map/ppermute | solution.py:568
  14.2 4.8 %collective-permute-start.6 = (bf16[2,4608]{1,0:T(2,128)(2,1)S(1)}, bf16[2,4608]{1,0:T(2,128)(2,1)S(1)}, u32[]{:S(2)}, u32[]{:S(2)}) collective-permute-start(bf16[2,4608]{1,0:T(2,128)(2,1)S(1)} %get-tuple-element.55), channel_id=1, source_target_pairs={{0,2},{1,3},{2,0},{3,1},{4,6},{5,7},{6,4},{7,5},{8,10},{9,11},{10,... | collective-permute-start | bytes 55304 | tf_op jit(solution)/shard_map/ppermute | solution.py:568
  16.1 3.3 %collective-permute-start.7 = (bf16[2,4608]{1,0:T(2,128)(2,1)S(1)}, bf16[2,4608]{1,0:T(2,128)(2,1)S(1)}, u32[]{:S(2)}, u32[]{:S(2)}) collective-permute-start(bf16[2,4608]{1,0:T(2,128)(2,1)S(1)} %get-tuple-element.56), channel_id=1, source_target_pairs={{0,3},{1,2},{2,1},{3,0},{4,7},{5,6},{6,5},{7,4},{8,11},{9,10},{10,... | collective-permute-start | bytes 55304 | tf_op jit(solution)/shard_map/ppermute | solution.py:568
  19.5 7.7 %collective-permute-start.10 = (bf16[8,2048]{1,0:T(8,128)(2,1)S(1)}, bf16[8,2048]{1,0:T(8,128)(2,1)S(1)}, u32[]{:S(2)}, u32[]{:S(2)}) collective-permute-start(bf16[8,2048]{1,0:T(8,128)(2,1)S(1)} %get-tuple-element.57.r_1_.r_0_), channel_id=1, source_target_pairs={{8,4},{9,5},{10,6},{11,7},{12,0},{13,1},{14,2},{15,3},{24,20},{25,... | collective-permute-start | bytes 98312 | tf_op jit(solution)/shard_map/ppermute | solution.py:568
  20.8 8.5 %collective-permute-start.9 = (bf16[8,2048]{1,0:T(8,128)(2,1)S(1)}, bf16[8,2048]{1,0:T(8,128)(2,1)S(1)}, u32[]{:S(2)}, u32[]{:S(2)}) collective-permute-start(bf16[8,2048]{1,0:T(8,128)(2,1)S(1)} %get-tuple-element.57.r_1_.r_0_), channel_id=1, source_target_pairs={{8,0},{9,1},{10,2},{11,3},{12,4},{13,5},{14,6},{15,7},{24,16},{25,... | collective-permute-start | bytes 98312 | tf_op jit(solution)/shard_map/ppermute | solution.py:568
  27.2 5.8 %collective-permute-start.8 = (bf16[8,2048]{1,0:T(8,128)(2,1)S(1)}, bf16[8,2048]{1,0:T(8,128)(2,1)S(1)}, u32[]{:S(2)}, u32[]{:S(2)}) collective-permute-start(bf16[8,2048]{1,0:T(8,128)(2,1)S(1)} %get-tuple-element.57.r_1_.r_0_), channel_id=1, source_target_pairs={{0,4},{1,5},{2,6},{3,7},{4,0},{5,1},{6,2},{7,3},{16,20},{17,21},{1... | collective-permute-start | bytes 98312 | tf_op jit(solution)/shard_map/ppermute | solution.py:568
  35.1 9.7 %collective-permute-start.14 = (bf16[8,2176]{1,0:T(8,128)(2,1)S(1)}, bf16[8,2176]{1,0:T(8,128)(2,1)S(1)}, u32[]{:S(2)}, u32[]{:S(2)}) collective-permute-start(bf16[8,2176]{1,0:T(8,128)(2,1)S(1)} %get-tuple-element.63), channel_id=1, source_target_pairs={{0,4},{1,5},{2,6},{3,7},{4,0},{5,1},{6,2},{7,3},{16,20},{17,21},{1... | collective-permute-start | bytes 104456 | tf_op jit(solution)/shard_map/ppermute | solution.py:568
  37.2 10.2 %collective-permute-start.15 = (bf16[8,2176]{1,0:T(8,128)(2,1)S(1)}, bf16[8,2176]{1,0:T(8,128)(2,1)S(1)}, u32[]{:S(2)}, u32[]{:S(2)}) collective-permute-start(bf16[8,2176]{1,0:T(8,128)(2,1)S(1)} %get-tuple-element.64), channel_id=1, source_target_pairs={{0,8},{1,9},{2,10},{3,11},{4,12},{5,13},{6,14},{7,15},{16,24},{17,... | collective-permute-start | bytes 104456 | tf_op jit(solution)/shard_map/ppermute | solution.py:568
  38.5 8.9 %collective-permute-start.16 = (bf16[8,2176]{1,0:T(8,128)(2,1)S(1)}, bf16[8,2176]{1,0:T(8,128)(2,1)S(1)}, u32[]{:S(2)}, u32[]{:S(2)}) collective-permute-start(bf16[8,2176]{1,0:T(8,128)(2,1)S(1)} %get-tuple-element.65), channel_id=1, source_target_pairs={{0,12},{1,13},{2,14},{3,15},{4,8},{5,9},{6,10},{7,11},{16,28},{17,... | collective-permute-start | bytes 104456 | tf_op jit(solution)/shard_map/ppermute | solution.py:568
  39.8 20.4 %collective-permute-start = (bf16[32,2176]{1,0:T(8,128)(2,1)S(1)}, bf16[32,2176]{1,0:T(8,128)(2,1)S(1)}, u32[]{:S(2)}, u32[]{:S(2)}) collective-permute-start(bf16[32,2176]{1,0:T(8,128)(2,1)S(1)} %get-tuple-element.46), channel_id=1, source_target_pairs={{0,1},{1,0},{2,3},{3,2},{4,5},{5,4},{6,7},{7,6},{16,17},{17,16},{1... | collective-permute-start | bytes 417800 | tf_op jit(solution)/shard_map/ppermute | solution.py:568
  41.7 18.5 %collective-permute-start.1 = (bf16[32,2176]{1,0:T(8,128)(2,1)S(1)}, bf16[32,2176]{1,0:T(8,128)(2,1)S(1)}, u32[]{:S(2)}, u32[]{:S(2)}) collective-permute-start(bf16[32,2176]{1,0:T(8,128)(2,1)S(1)} %get-tuple-element.47), channel_id=1, source_target_pairs={{0,2},{1,3},{2,0},{3,1},{4,6},{5,7},{6,4},{7,5},{16,18},{17,19},{1... | collective-permute-start | bytes 417800 | tf_op jit(solution)/shard_map/ppermute | solution.py:568
  44.8 15.4 %collective-permute-start.2 = (bf16[32,2176]{1,0:T(8,128)(2,1)S(1)}, bf16[32,2176]{1,0:T(8,128)(2,1)S(1)}, u32[]{:S(2)}, u32[]{:S(2)}) collective-permute-start(bf16[32,2176]{1,0:T(8,128)(2,1)S(1)} %get-tuple-element.48), channel_id=1, source_target_pairs={{0,3},{1,2},{2,1},{3,0},{4,7},{5,6},{6,5},{7,4},{16,19},{17,18},{1... | collective-permute-start | bytes 417800 | tf_op jit(solution)/shard_map/ppermute | solution.py:568
  49.5 0.6 copy-start.3
  50.1 9.2 %collective-permute-start.19 = (bf16[8,2176]{1,0:T(8,128)(2,1)S(1)}, bf16[8,2176]{1,0:T(8,128)(2,1)S(1)}, u32[]{:S(2)}, u32[]{:S(2)}) collective-permute-start(bf16[8,2176]{1,0:T(8,128)(2,1)S(1)} %get-tuple-element.68), channel_id=1, source_target_pairs={{0,12},{1,13},{2,14},{3,15},{4,8},{5,9},{6,10},{7,11},{8,4},{9,5},... | collective-permute-start | bytes 104456 | tf_op jit(solution)/shard_map/ppermute | solution.py:568
  50.1 3.9 %collective-permute-start.17 = (bf16[8,2176]{1,0:T(8,128)(2,1)S(1)}, bf16[8,2176]{1,0:T(8,128)(2,1)S(1)}, u32[]{:S(2)}, u32[]{:S(2)}) collective-permute-start(bf16[8,2176]{1,0:T(8,128)(2,1)S(1)} %get-tuple-element.68), channel_id=1, source_target_pairs={{0,4},{1,5},{2,6},{3,7},{4,0},{5,1},{6,2},{7,3},{8,12},{9,13},{10,... | collective-permute-start | bytes 104456 | tf_op jit(solution)/shard_map/ppermute | solution.py:568
  54.0 5.2 %collective-permute-start.18 = (bf16[8,2176]{1,0:T(8,128)(2,1)S(1)}, bf16[8,2176]{1,0:T(8,128)(2,1)S(1)}, u32[]{:S(2)}, u32[]{:S(2)}) collective-permute-start(bf16[8,2176]{1,0:T(8,128)(2,1)S(1)} %get-tuple-element.68), channel_id=1, source_target_pairs={{0,8},{1,9},{2,10},{3,11},{4,12},{5,13},{6,14},{7,15},{8,0},{9,1},... | collective-permute-start | bytes 104456 | tf_op jit(solution)/shard_map/ppermute | solution.py:568
  59.3 10.5 %copy-start = (bf16[32,2176]{1,0:T(8,128)(2,1)}, bf16[32,2176]{1,0:T(8,128)(2,1)S(1)}, u32[]{:S(2)}) copy-start(bf16[32,2176]{1,0:T(8,128)(2,1)S(1)} %constant_dynamic-update-slice_fusion.r_0_) | copy-start | bytes 417796
  59.3 7.9 %collective-permute-start.20 = (bf16[32,2176]{1,0:T(8,128)(2,1)S(1)}, bf16[32,2176]{1,0:T(8,128)(2,1)S(1)}, u32[]{:S(2)}, u32[]{:S(2)}) collective-permute-start(bf16[32,2176]{1,0:T(8,128)(2,1)S(1)} %constant_dynamic-update-slice_fusion.r_0_), channel_id=1, source_target_pairs={{0,2},{1,3},{2,0},{3,1},{4,6},{5,7},{6,4},{7,5},{8,10},{9,11},{10,... | collective-permute-start | bytes 417800 | tf_op jit(solution)/shard_map/ppermute | solution.py:568
  62.3 35.4 %collective-permute-start.3 = (bf16[64,2176]{1,0:T(8,128)(2,1)S(1)}, bf16[64,2176]{1,0:T(8,128)(2,1)S(1)}, u32[]{:S(2)}, u32[]{:S(2)}) collective-permute-start(bf16[64,2176]{1,0:T(8,128)(2,1)S(1)} %get-tuple-element.50), channel_id=1, source_target_pairs={{0,8},{1,9},{2,10},{3,11},{4,12},{5,13},{6,14},{7,15},{16,24},{17,... | collective-permute-start | bytes 835592 | tf_op jit(solution)/shard_map/ppermute | solution.py:568
  67.1 14.1 %collective-permute-start.21 = (bf16[32,2176]{1,0:T(8,128)(2,1)S(1)}, bf16[32,2176]{1,0:T(8,128)(2,1)S(1)}, u32[]{:S(2)}, u32[]{:S(2)}) collective-permute-start(bf16[32,2176]{1,0:T(8,128)(2,1)S(1)} %constant_dynamic-update-slice_fusion.r_0_), channel_id=1, source_target_pairs={{0,1},{1,0},{2,3},{3,2},{4,5},{5,4},{6,7},{7,6},{8,9},{9,8},{10,11... | collective-permute-start | bytes 417800 | tf_op jit(solution)/shard_map/ppermute | solution.py:568
  67.2 7.9 %copy-start.1 = (bf16[32,2176]{1,0:T(8,128)(2,1)}, bf16[32,2176]{1,0:T(8,128)(2,1)S(1)}, u32[]{:S(2)}) copy-start(bf16[32,2176]{1,0:T(8,128)(2,1)S(1)} %collective-permute-done.20.r_0_.r_1_) | copy-start | bytes 417796
  67.2 14.0 %collective-permute-start.22 = (bf16[32,2176]{1,0:T(8,128)(2,1)S(1)}, bf16[32,2176]{1,0:T(8,128)(2,1)S(1)}, u32[]{:S(2)}, u32[]{:S(2)}) collective-permute-start(bf16[32,2176]{1,0:T(8,128)(2,1)S(1)} %collective-permute-done.20.r_0_.r_1_), channel_id=1, source_target_pairs={{0,1},{1,0},{2,3},{3,2},{4,5},{5,4},{6,7},{7,6},{8,9},{9,8},{10,11... | collective-permute-start | bytes 417800 | tf_op jit(solution)/shard_map/ppermute | solution.py:568
  80.5 0.8 copy-start.2
  97.5 2.1 %collective-permute-start.23 = (f32[16,8192]{1,0:T(8,128)S(1)}, f32[16,8192]{1,0:T(8,128)S(1)}, u32[]{:S(2)}, u32[]{:S(2)}) collective-permute-start(f32[16,8192]{1,0:T(8,128)S(1)} %get-tuple-element.81), channel_id=1, source_target_pairs={{0,1},{1,0},{2,3},{3,2},{4,5},{5,4},{6,7},{7,6},{8,9},{9,8},{10,11... | collective-permute-start | bytes 1572872 | tf_op jit(solution)/shard_map/ppermute | solution.py:568
  97.7 12.0 %collective-permute-start.4 = (bf16[64,2176]{1,0:T(8,128)(2,1)S(1)}, bf16[64,2176]{1,0:T(8,128)(2,1)S(1)}, u32[]{:S(2)}, u32[]{:S(2)}) collective-permute-start(bf16[64,2176]{1,0:T(8,128)(2,1)S(1)} %pad_maximum_fusion), channel_id=1, source_target_pairs={{0,4},{1,5},{2,6},{3,7},{4,0},{5,1},{6,2},{7,3},{8,12},{9,13},{10,... | collective-permute-start | bytes 835592 | tf_op jit(solution)/shard_map/ppermute | solution.py:568
  99.7 5.6 %collective-permute-start.24 = (bf16[8,8192]{1,0:T(8,128)(2,1)S(1)}, bf16[8,8192]{1,0:T(8,128)(2,1)S(1)}, u32[]{:S(2)}, u32[]{:S(2)}) collective-permute-start(bf16[8,8192]{1,0:T(8,128)(2,1)S(1)} %get-tuple-element.83), channel_id=1, source_target_pairs={{0,2},{1,3},{2,0},{3,1},{4,6},{5,7},{6,4},{7,5},{8,10},{9,11},{10,... | collective-permute-start | bytes 393224 | tf_op jit(solution)/shard_map/ppermute | solution.py:568
  105.3 5.4 %collective-permute-start.25 = (bf16[2,8192]{1,0:T(2,128)(2,1)S(1)}, bf16[2,8192]{1,0:T(2,128)(2,1)S(1)}, u32[]{:S(2)}, u32[]{:S(2)}) collective-permute-start(bf16[2,8192]{1,0:T(2,128)(2,1)S(1)} %get-tuple-element.85), channel_id=1, source_target_pairs={{0,4},{1,5},{2,6},{3,7},{4,0},{5,1},{6,2},{7,3},{8,12},{9,13},{10,... | collective-permute-start | bytes 98312 | tf_op jit(solution)/shard_map/ppermute | solution.py:568
  107.1 4.9 %collective-permute-start.26 = (bf16[2,8192]{1,0:T(2,128)(2,1)S(1)}, bf16[2,8192]{1,0:T(2,128)(2,1)S(1)}, u32[]{:S(2)}, u32[]{:S(2)}) collective-permute-start(bf16[2,8192]{1,0:T(2,128)(2,1)S(1)} %get-tuple-element.86), channel_id=1, source_target_pairs={{0,8},{1,9},{2,10},{3,11},{4,12},{5,13},{6,14},{7,15},{8,0},{9,1},... | collective-permute-start | bytes 98312 | tf_op jit(solution)/shard_map/ppermute | solution.py:568
  107.1 5.7 %collective-permute-start.27 = (bf16[2,8192]{1,0:T(2,128)(2,1)S(1)}, bf16[2,8192]{1,0:T(2,128)(2,1)S(1)}, u32[]{:S(2)}, u32[]{:S(2)}) collective-permute-start(bf16[2,8192]{1,0:T(2,128)(2,1)S(1)} %get-tuple-element.87), channel_id=1, source_target_pairs={{0,12},{1,13},{2,14},{3,15},{4,8},{5,9},{6,10},{7,11},{8,4},{9,5},... | collective-permute-start | bytes 98312 | tf_op jit(solution)/shard_map/ppermute | solution.py:568

commit v3 on v2

--- a/solution.py
+++ b/solution.py
@@ -80,7 +80,7 @@
 
 
 GU_ROWS = 512
-DOWN_COLS = 1024
+DOWN_ROWS = 256
 
 
 def piece_shape(piece):
@@ -474,8 +474,8 @@
     depth = dbuf.shape[0]
     fetched = fetch_copies([late], (w_gate, w_up), [buf], sem)
     downs = []
-    for n in range(out.shape[1] // DOWN_COLS):
-        src = w_down.at[:, n * DOWN_COLS : (n + 1) * DOWN_COLS]
+    for n in range(ff // DOWN_ROWS):
+        src = w_down.at[pl.ds(n * DOWN_ROWS, DOWN_ROWS), :]
         downs.append(pltpu.make_async_copy(src, dbuf.at[n % depth], dsem.at[n % depth]))
     for c in fetched + downs[:depth]:
         c.start()
@@ -520,9 +520,15 @@
     ).astype(BF16)
     for n, c in enumerate(downs):
         c.wait()
-        out[:, n * DOWN_COLS : (n + 1) * DOWN_COLS] = jnp.dot(
-            hidden, dbuf[n % depth], preferred_element_type=F32
+        part = jnp.dot(
+            hidden[:, n * DOWN_ROWS : (n + 1) * DOWN_ROWS],
+            dbuf[n % depth],
+            preferred_element_type=F32,
         )
+        if n == 0:
+            out[...] = part
+        else:
+            out[...] += part
         if n + depth < len(downs):
             downs[n + depth].start()
     per = 2 * planes
@@ -563,9 +569,8 @@
     refs[-1][...] = total.astype(BF16)
 
 
-def swap(x, k, devices, sends=None):
-    pairs = [(i, i ^ k) for i in range(devices) if sends is None or sends(i)]
-    return lax.ppermute(x, "ctx", pairs)
+def swap(x, k, devices):
+    return lax.ppermute(x, "ctx", [(i, i ^ k) for i in range(devices)])
 
 
 def cells_program(*args):
@@ -618,9 +623,6 @@
         found = [h for h in held if h[0][0] in flips]
         return [h[0] for h in found], [in_vmem(h[1]) for h in found]
 
-    def has_tokens(i):
-        return i < devices // 2
-
     def warm(name, dep):
         plan = plans[name]
         values = call(
@@ -665,7 +667,7 @@
     sends, relays = turned[:CELL], turned[CELL : 2 * CELL]
     token_row = turned[2 * CELL]
     keep_pieces("turn", turned[2 * CELL + 1 :])
-    kvs = [sends[0]] + [swap(sends[k], k, devices, has_tokens) for k in range(1, CELL)]
+    kvs = [sends[0]] + [swap(sends[k], k, devices) for k in range(1, CELL)]
     cat, own_q = call(
         assemble_body,
         [vmem()] * CELL,
@@ -673,12 +675,9 @@
         tuple(msgs),
         4,
     )
-    qs = [own_q] + [
-        swap(own_q, CELL * k, devices, lambda i: has_tokens(i ^ (CELL * k)))
-        for k in range(1, planes)
-    ]
+    qs = [own_q] + [swap(own_q, CELL * k, devices) for k in range(1, planes)]
     warm("warm_q", own_q)
-    relays = [relays[0]] + [swap(relays[k], k, devices, has_tokens) for k in range(1, CELL)]
+    relays = [relays[0]] + [swap(relays[k], k, devices) for k in range(1, CELL)]
     plan = plans["scores"]
     parts = call(
         lambda *r: scores_body(planes, plan, *r),
@@ -691,7 +690,7 @@
         5,
     )
     keep_pieces("scores", parts[planes:])
-    parts = [parts[0]] + [swap(parts[k], CELL * k, devices, has_tokens) for k in range(1, planes)]
+    parts = [parts[0]] + [swap(parts[k], CELL * k, devices) for k in range(1, planes)]
     plan = plans["merge"]
     merged = call(
         lambda *r: merge_body(planes, plan, *r),
@@ -719,7 +718,7 @@
     )
     relay_mine, relay_far, relay_near = grouped[:3]
     keep_pieces("regroup", grouped[3:])
-    relay_far = swap(relay_far, 2 * CELL, devices, has_tokens)
+    relay_far = swap(relay_far, 2 * CELL, devices)
     blocks = [normed] + [swap(normed, CELL * k, devices) for k in range(1, planes)]
     own = jnp.concatenate(blocks, axis=0)
     across = swap(own, 2, devices)
@@ -754,24 +753,19 @@
         [vmem()] * (6 + len(values)) + [hbm()] * 3,
         [((all_rows // 2, model), F32)] * 2,
         (
-            own,
-            across,
-            in_vmem(near),
-            in_vmem(far),
-            acc,
-            hstate,
+            *[in_vmem(x) for x in (own, across, near, far, acc, hstate)],
             *values,
             *weights,
             in_hbm(w_down),
         ),
-        32,
+        30,
         [
             pltpu.VMEM((all_rows, 2 * ff), F32),
             pltpu.VMEM((all_rows, model), F32),
             pltpu.VMEM(piece_shape(late), BF16),
             pltpu.SemaphoreType.DMA((count_of([late]),)),
-            pltpu.VMEM((6, ff, DOWN_COLS), BF16),
-            pltpu.SemaphoreType.DMA((6,)),
+            pltpu.VMEM((5, DOWN_ROWS, model), BF16),
+            pltpu.SemaphoreType.DMA((5,)),
         ],
         moved=40,
         on_chip=True,

time: 114 us -> 98.8 us (0.87)
  starting transfers between devices: 47.8 us -> 31.5 us
  waiting for transfers between devices: 21.7 us -> 27.2 us
  Pallas kernels: 41.6 us -> 39.1 us
  local copies, waits for them, and re-layouts: 1.42 us -> 0.04 us
    ppermute x28, starting transfers between devices: 47.8 us -> 31.5 us  [swap(): return lax.ppermute(x, 'ctx', [(i, i ^ k) for i in range(devices)])]
    ppermute x28, waiting for transfers between devices: 21.7 us -> 27.2 us  [swap(): return lax.ppermute(x, 'ctx', [(i, i ^ k) for i in range(devices)])]
    pallas_call x14, Pallas kernels: 41.6 us -> 39.1 us  [call(): pl.pallas_call(body, in_specs=ins, out_specs=[vmem() for _ in shapes], ou...]
    unnamed x11 -> x3, local copies, waits for them, and re-layouts: 1.4 us -> 0.02 us
  transfers between devices with their start and end apart: 28 -> 28, of which waited for: 9 -> 11; matrix products, arithmetic and copies ran while one was open for 0% -> 0% of each run, Pallas kernels for 31% -> 33%
where the time goes in v3:
time: 98.8 us; the launch traced here: 98.6 us
  Pallas kernels  39.1 us (40%)
  starting transfers between devices  31.5 us (32%)
  waiting for transfers between devices  27.2 us (28%)
    pallas_call x14, Pallas kernels, call(): pl.pallas_call(body, in_specs=ins, out_specs=[vmem() for _ in shapes], ou...  39.1 us
    ppermute x28, starting transfers between devices, swap(): return lax.ppermute(x, 'ctx', [(i, i ^ k) for i in range(devices)])  31.5 us
    ppermute x28, waiting for transfers between devices, swap(): return lax.ppermute(x, 'ctx', [(i, i ^ k) for i in range(devices)])  27.2 us
  transfers between devices with their start and end apart: 28, of which 11 were waited for; matrix products, arithmetic and copies ran while one was open for 0% of the time, Pallas kernels for 33%

profile of v3, /device:TPU:0, one launch (start us, length us, event | category | flops | bytes accessed | tf_op | source)
XLA Modules:
  0.0 98.6 jit_solution(9368311038480907436)
XLA Ops:
  0.6 3.5 %shard_map.131 = (bf16[128,512]{1,0:T(8,128)(2,1)S(1)}, bf16[128,512]{1,0:T(8,128)(2,1)S(1)}, bf16[128,512]{1,0:T(8,128)(2,1)S(1)}, bf16[128,512]{1,0:T(8,128)(2...) custom-call(s32[4]{0:T(128)} %r_0_.1, ...), custom_call_target="tpu_custom_call" | custom-call | bytes 8388608 | tf_op jit(solution)/shard_map/pallas_call | solution.py:40
  4.7 2.6 %collective-permute-start.12 = (bf16[128,512]{1,0:T(8,128)(2,1)S(1)}, bf16[128,512]{1,0:T(8,128)(2,1)S(1)}, u32[]{:S(2)}, u32[]{:S(2)}) collective-permute-start(bf16[128,512]{1,0:T(8,128)(2,1)S(1)} %get-tuple-element.60), channel_id=1, source_target_pairs={{0,2},{1,3},{2,0},{3,1},{4,6},{5,7},{6,4},{7,5},{8,10},{9,11},{10,... | collective-permute-start | bytes 393224 | tf_op jit(solution)/shard_map/ppermute | solution.py:573
  7.3 1.0 %shard_map.134 = (bf16[2,4608]{1,0:T(2,128)(2,1)S(1)}, bf16[2,4608]{1,0:T(2,128)(2,1)S(1)}, bf16[2,4608]{1,0:T(2,128)(2,1)S(1)}, bf16[2,4608]{1,0:T(2,128)(2,1)S(1)}, bf16[16,128]{1,0:T(8,128)(2,1)S(1)}) custom-call(bf16[2,8192]{1,0:T(2,128)(2,1)} %q.1, bf16[2,2048]{1,0:T(2,128)(2,1)} %kv.1, bf16[2,8192]{1,0:T(2,128)(2,1)} %res.1, bf16[64,128]{1,0:T(8,128)(2,1)} %bitcast.6), custom_call_target="tpu_custom_call" | custom-call | tf_op jit(solution)/shard_map/pallas_call | solution.py:40
  8.6 1.9 %collective-permute-start.6 = (bf16[2,4608]{1,0:T(2,128)(2,1)S(1)}, bf16[2,4608]{1,0:T(2,128)(2,1)S(1)}, u32[]{:S(2)}, u32[]{:S(2)}) collective-permute-start(bf16[2,4608]{1,0:T(2,128)(2,1)S(1)} %get-tuple-element.55), channel_id=1, source_target_pairs={{0,2},{1,3},{2,0},{3,1},{4,6},{5,7},{6,4},{7,5},{8,10},{9,11},{10,... | collective-permute-start | bytes 55304 | tf_op jit(solution)/shard_map/ppermute | solution.py:573
  11.3 3.5 %collective-permute-done.6.refs_2_ = bf16[2,4608]{1,0:T(2,128)(2,1)S(1)} collective-permute-done((bf16[2,4608]{1,0:T(2,128)(2,1)S(1)}, bf16[2,4608]{1,0:T(2,128)(2,1)S(1)}, u32[]{:S(2)}, u32[]{:S(2)}) %collective-permute-start.6) | collective-permute-done | bytes 18464 | tf_op jit(solution)/shard_map/ppermute | solution.py:573
  14.9 3.9 %collective-permute-start.10 = (bf16[8,2048]{1,0:T(8,128)(2,1)S(1)}, bf16[8,2048]{1,0:T(8,128)(2,1)S(1)}, u32[]{:S(2)}, u32[]{:S(2)}) collective-permute-start(bf16[8,2048]{1,0:T(8,128)(2,1)S(1)} %get-tuple-element.57.r_1_.r_0_), channel_id=1, source_target_pairs={{0,12},{1,13},{2,14},{3,15},{4,8},{5,9},{6,10},{7,11},{8,4},{9,5},... | collective-permute-start | bytes 98312 | tf_op jit(solution)/shard_map/ppermute | solution.py:573
  18.8 1.9 %collective-permute-done.10.r_4_ = bf16[8,2048]{1,0:T(8,128)(2,1)S(1)} collective-permute-done((bf16[8,2048]{1,0:T(8,128)(2,1)S(1)}, bf16[8,2048]{1,0:T(8,128)(2,1)S(1)}, u32[]{:S(2)}, u32[]{:S(2)}) %collective-permute-start.10) | collective-permute-done | bytes 32800 | tf_op jit(solution)/shard_map/ppermute | solution.py:573
  21.3 2.2 %collective-permute-done.9.r_3_ = bf16[8,2048]{1,0:T(8,128)(2,1)S(1)} collective-permute-done((bf16[8,2048]{1,0:T(8,128)(2,1)S(1)}, bf16[8,2048]{1,0:T(8,128)(2,1)S(1)}, u32[]{:S(2)}, u32[]{:S(2)}) %collective-permute-start.9) | collective-permute-done | bytes 32800 | tf_op jit(solution)/shard_map/ppermute | solution.py:573
  23.6 1.0 %collective-permute-done.8.r_2_ = bf16[8,2048]{1,0:T(8,128)(2,1)S(1)} collective-permute-done((bf16[8,2048]{1,0:T(8,128)(2,1)S(1)}, bf16[8,2048]{1,0:T(8,128)(2,1)S(1)}, u32[]{:S(2)}, u32[]{:S(2)}) %collective-permute-start.8) | collective-permute-done | bytes 32800 | tf_op jit(solution)/shard_map/ppermute | solution.py:573
  24.6 2.1 %shard_map.136 = (bf16[8,2176]{1,0:T(8,128)(2,1)S(1)}, bf16[8,2176]{1,0:T(8,128)(2,1)S(1)}, bf16[8,2176]{1,0:T(8,128)(2,1)S(1)}, bf16[8,2176]{1,0:T(8,128)(2,1)S(1)}, bf16[2,512,1792]{2,1,0:T(8,128)(2,1)S(1)}) custom-call(s32[1,512]{1,0:T(1,128)S(1)} %get-tuple-element.52.r_0_, bf16[8,2048]{1,0:T(8,128)(2,1)S(1)} %get-tuple-element.57.r_1_.r_0_, ...), custom_call_target="tpu_custom_call" | custom-call | bytes 5242880 | tf_op jit(solution)/shard_map/pallas_call | solution.py:40
  27.4 3.7 %collective-permute-start.15 = (bf16[8,2176]{1,0:T(8,128)(2,1)S(1)}, bf16[8,2176]{1,0:T(8,128)(2,1)S(1)}, u32[]{:S(2)}, u32[]{:S(2)}) collective-permute-start(bf16[8,2176]{1,0:T(8,128)(2,1)S(1)} %get-tuple-element.64), channel_id=1, source_target_pairs={{0,8},{1,9},{2,10},{3,11},{4,12},{5,13},{6,14},{7,15},{8,0},{9,1},... | collective-permute-start | bytes 104456 | tf_op jit(solution)/shard_map/ppermute | solution.py:573
  31.1 1.7 %collective-permute-start.1 = (bf16[32,2176]{1,0:T(8,128)(2,1)S(1)}, bf16[32,2176]{1,0:T(8,128)(2,1)S(1)}, u32[]{:S(2)}, u32[]{:S(2)}) collective-permute-start(bf16[32,2176]{1,0:T(8,128)(2,1)S(1)} %get-tuple-element.47), channel_id=1, source_target_pairs={{0,2},{1,3},{2,0},{3,1},{4,6},{5,7},{6,4},{7,5},{8,10},{9,11},{10,... | collective-permute-start | bytes 417800 | tf_op jit(solution)/shard_map/ppermute | solution.py:573
  33.8 3.1 %collective-permute-done.16.r_3_ = bf16[8,2176]{1,0:T(8,128)(2,1)S(1)} collective-permute-done((bf16[8,2176]{1,0:T(8,128)(2,1)S(1)}, bf16[8,2176]{1,0:T(8,128)(2,1)S(1)}, u32[]{:S(2)}, u32[]{:S(2)}) %collective-permute-start.16) | collective-permute-done | bytes 34848 | tf_op jit(solution)/shard_map/ppermute | solution.py:573
  36.9 2.1 %shard_map.137 = (bf16[8,2176]{1,0:T(8,128)(2,1)S(1)}, f32[8,2048]{1,0:T(8,128)S(1)}, bf16[2,512,1792]{2,1,0:T(8,128)(2,1)S(1)}) custom-call(bf16[8,2176]{1,0:T(8,128)(2,1)S(1)} %get-tuple-element.62.r_0_, bf16[8,2176]{1,0:T(8,128)(2,1)S(1)} %collective-permute-done.14.r_1_, bf16[8,2176]{1,0:T(8,128)(2,1)S(1)} %collective-permute-done.15.r_2_, ...), custom_call_target="tpu_custom_call" | custom-call | bytes 4194304 | tf_op jit(solution)/shard_map/pallas_call | solution.py:40
  39.4 3.9 %collective-permute-done.17 = bf16[8,2176]{1,0:T(8,128)(2,1)S(1)} collective-permute-done((bf16[8,2176]{1,0:T(8,128)(2,1)S(1)}, bf16[8,2176]{1,0:T(8,128)(2,1)S(1)}, u32[]{:S(2)}, u32[]{:S(2)}) %collective-permute-start.17) | collective-permute-done | bytes 34848 | tf_op jit(solution)/shard_map/ppermute | solution.py:573
  43.3 2.4 %collective-permute-start.18 = (bf16[8,2176]{1,0:T(8,128)(2,1)S(1)}, bf16[8,2176]{1,0:T(8,128)(2,1)S(1)}, u32[]{:S(2)}, u32[]{:S(2)}) collective-permute-start(bf16[8,2176]{1,0:T(8,128)(2,1)S(1)} %get-tuple-element.68), channel_id=1, source_target_pairs={{0,8},{1,9},{2,10},{3,11},{4,12},{5,13},{6,14},{7,15},{8,0},{9,1},... | collective-permute-start | bytes 104456 | tf_op jit(solution)/shard_map/ppermute | solution.py:573
  45.7 2.5 %collective-permute-done.18 = bf16[8,2176]{1,0:T(8,128)(2,1)S(1)} collective-permute-done((bf16[8,2176]{1,0:T(8,128)(2,1)S(1)}, bf16[8,2176]{1,0:T(8,128)(2,1)S(1)}, u32[]{:S(2)}, u32[]{:S(2)}) %collective-permute-start.18) | collective-permute-done | bytes 34848 | tf_op jit(solution)/shard_map/ppermute | solution.py:573
  48.2 1.6 %collective-permute-start.20 = (bf16[32,2176]{1,0:T(8,128)(2,1)S(1)}, bf16[32,2176]{1,0:T(8,128)(2,1)S(1)}, u32[]{:S(2)}, u32[]{:S(2)}) collective-permute-start(bf16[32,2176]{1,0:T(8,128)(2,1)S(1)} %constant_dynamic-update-slice_fusion.r_0_), channel_id=1, source_target_pairs={{0,2},{1,3},{2,0},{3,1},{4,6},{5,7},{6,4},{7,5},{8,10},{9,11},{10,... | collective-permute-start | bytes 417800 | tf_op jit(solution)/shard_map/ppermute | solution.py:573
  49.8 2.1 %shard_map.132 = (bf16[32,2176]{1,0:T(8,128)(2,1)S(1)}, bf16[64,2176]{1,0:T(8,128)(2,1)S(1)}, bf16[32,2176]{1,0:T(8,128)(2,1)S(1)}, bf16[2,512,1792]{2,1,0:T(8,128)(2,1)S(1)}) custom-call(bf16[32,2176]{1,0:T(8,128)(2,1)S(1)} %get-tuple-element.45.r_0_, bf16[32,2176]{1,0:T(8,128)(2,1)S(1)} %collective-permute-done.r_1_, ...), custom_call_target="tpu_custom_call" | custom-call | bytes 4194304 | tf_op jit(solution)/shard_map/pallas_call | solution.py:40
  51.9 2.4 %collective-permute-start.3 = (bf16[64,2176]{1,0:T(8,128)(2,1)S(1)}, bf16[64,2176]{1,0:T(8,128)(2,1)S(1)}, u32[]{:S(2)}, u32[]{:S(2)}) collective-permute-start(bf16[64,2176]{1,0:T(8,128)(2,1)S(1)} %get-tuple-element.50), channel_id=1, source_target_pairs={{0,8},{1,9},{2,10},{3,11},{4,12},{5,13},{6,14},{7,15},{8,0},{9,1},... | collective-permute-start | bytes 835592 | tf_op jit(solution)/shard_map/ppermute | solution.py:573
  54.8 2.1 %shard_map.138.r_2_ = bf16[2,512,1792]{2,1,0:T(8,128)(2,1)S(1)} custom-call(bf16[8,2048]{1,0:T(8,128)(2,1)S(1)} %get-tuple-element.57.r_1_.r_0_, bf16[8192,1792]{1,0:T(8,128)(2,1)} %r_9_.3, bf16[8192,1792]{1,0:T(8,128)(2,1)} %r_10_.3), custom_call_target="tpu_custom_call" | custom-call | bytes 8388608 | tf_op jit(solution)/shard_map/pallas_call | solution.py:40
  56.9 5.3 %shard_map.139 = (f32[32,3584]{1,0:T(8,128)S(1)}, bf16[4,512,1792]{2,1,0:T(8,128)(2,1)S(1)}, bf16[4,512,1792]{2,1,0:T(8,128)(2,1)S(1)}) custom-call(bf16[32,2176]{1,0:T(8,128)(2,1)S(1)} %constant_dynamic-update-slice_fusion.r_0_, bf16[4,512,1792]{2,1,0:T(8,128)(2,1)S(1)} %get-tuple-element.69.r_1_, bf16[2,512,1792]{2,1,0:T(8,128)(2,1)S(1)} %shard_map.138.r_2_, ...), custom_call_target="tpu_custom_call" | custom-call | bytes 14680064 | tf_op jit(solution)/shard_map/pallas_call | solution.py:40
  62.2 5.3 %shard_map.140 = (f32[32,3584]{1,0:T(8,128)S(1)}, bf16[4,512,1792]{2,1,0:T(8,128)(2,1)S(1)}, bf16[4,512,1792]{2,1,0:T(8,128)(2,1)S(1)}) custom-call(bf16[32,2176]{1,0:T(8,128)(2,1)S(1)} %collective-permute-done.20.r_0_.r_1_, f32[32,3584]{1,0:T(8,128)S(1)} %get-tuple-element.71.r_1_, bf16[2,512,1792]{2,1,0:T(8,128)(2,1)S(1)} %get-tuple-element.72.r_2_, ...), custom_call_target="tpu_custom_call" | custom-call | bytes 14680064 | tf_op jit(solution)/shard_map/pallas_call | solution.py:40
  67.6 13.7 %shard_map.141 = (f32[16,8192]{1,0:T(8,128)S(1)}, f32[16,8192]{1,0:T(8,128)S(1)}) custom-call(bf16[32,2176]{1,0:T(8,128)(2,1)S(1)} %constant_dynamic-update-slice_fusion.r_0_, bf16[32,2176]{1,0:T(8,128)(2,1)S(1)} %collective-permute-done.20.r_0_.r_1_, bf16[32,2176]{1,0:T(8,128)(2,1)S(1)} %collective-permute-done.21.r_2_, ...), custom_call_target="tpu_custom_call" | custom-call | bytes 41943040 | tf_op jit(solution)/shard_map/pallas_call | solution.py:40
  81.5 1.9 %collective-permute-start.4 = (bf16[64,2176]{1,0:T(8,128)(2,1)S(1)}, bf16[64,2176]{1,0:T(8,128)(2,1)S(1)}, u32[]{:S(2)}, u32[]{:S(2)}) collective-permute-start(bf16[64,2176]{1,0:T(8,128)(2,1)S(1)} %pad_maximum_fusion), channel_id=1, source_target_pairs={{0,4},{1,5},{2,6},{3,7},{4,0},{5,1},{6,2},{7,3},{8,12},{9,13},{10,... | collective-permute-start | bytes 835592 | tf_op jit(solution)/shard_map/ppermute | solution.py:573
  84.1 5.0 %collective-permute-done.24.r_1_ = bf16[8,8192]{1,0:T(8,128)(2,1)S(1)} collective-permute-done((bf16[8,8192]{1,0:T(8,128)(2,1)S(1)}, bf16[8,8192]{1,0:T(8,128)(2,1)S(1)}, u32[]{:S(2)}, u32[]{:S(2)}) %collective-permute-start.24) | collective-permute-done | bytes 131104 | tf_op jit(solution)/shard_map/ppermute | solution.py:573
  89.2 1.8 %collective-permute-start.25 = (bf16[2,8192]{1,0:T(2,128)(2,1)S(1)}, bf16[2,8192]{1,0:T(2,128)(2,1)S(1)}, u32[]{:S(2)}, u32[]{:S(2)}) collective-permute-start(bf16[2,8192]{1,0:T(2,128)(2,1)S(1)} %get-tuple-element.85), channel_id=1, source_target_pairs={{0,4},{1,5},{2,6},{3,7},{4,0},{5,1},{6,2},{7,3},{8,12},{9,13},{10,... | collective-permute-start | bytes 98312 | tf_op jit(solution)/shard_map/ppermute | solution.py:573
  90.9 1.3 %collective-permute-start.26 = (bf16[2,8192]{1,0:T(2,128)(2,1)S(1)}, bf16[2,8192]{1,0:T(2,128)(2,1)S(1)}, u32[]{:S(2)}, u32[]{:S(2)}) collective-permute-start(bf16[2,8192]{1,0:T(2,128)(2,1)S(1)} %get-tuple-element.86), channel_id=1, source_target_pairs={{0,8},{1,9},{2,10},{3,11},{4,12},{5,13},{6,14},{7,15},{8,0},{9,1},... | collective-permute-start | bytes 98312 | tf_op jit(solution)/shard_map/ppermute | solution.py:573
  92.2 1.4 %collective-permute-start.27 = (bf16[2,8192]{1,0:T(2,128)(2,1)S(1)}, bf16[2,8192]{1,0:T(2,128)(2,1)S(1)}, u32[]{:S(2)}, u32[]{:S(2)}) collective-permute-start(bf16[2,8192]{1,0:T(2,128)(2,1)S(1)} %get-tuple-element.87), channel_id=1, source_target_pairs={{0,12},{1,13},{2,14},{3,15},{4,8},{5,9},{6,10},{7,11},{8,4},{9,5},... | collective-permute-start | bytes 98312 | tf_op jit(solution)/shard_map/ppermute | solution.py:573
  93.6 1.0 shard_map.133
  94.6 1.6 %collective-permute-done.26.refs_1_ = bf16[2,8192]{1,0:T(2,128)(2,1)S(1)} collective-permute-done((bf16[2,8192]{1,0:T(2,128)(2,1)S(1)}, bf16[2,8192]{1,0:T(2,128)(2,1)S(1)}, u32[]{:S(2)}, u32[]{:S(2)}) %collective-permute-start.26) | collective-permute-done | bytes 32800 | tf_op jit(solution)/shard_map/ppermute | solution.py:573
  96.2 1.7 %collective-permute-done.27.refs_2_ = bf16[2,8192]{1,0:T(2,128)(2,1)S(1)} collective-permute-done((bf16[2,8192]{1,0:T(2,128)(2,1)S(1)}, bf16[2,8192]{1,0:T(2,128)(2,1)S(1)}, u32[]{:S(2)}, u32[]{:S(2)}) %collective-permute-start.27) | collective-permute-done | bytes 32800 | tf_op jit(solution)/shard_map/ppermute | solution.py:573
  (44 shorter events, 6.7 us)
Async XLA Ops:
  4.2 20.4 %collective-permute-start.11 = (bf16[128,512]{1,0:T(8,128)(2,1)S(1)}, bf16[128,512]{1,0:T(8,128)(2,1)S(1)}, u32[]{:S(2)}, u32[]{:S(2)}) collective-permute-start(bf16[128,512]{1,0:T(8,128)(2,1)S(1)} %get-tuple-element.59), channel_id=1, source_target_pairs={{0,1},{1,0},{2,3},{3,2},{4,5},{5,4},{6,7},{7,6},{8,9},{9,8},{10,11... | collective-permute-start | bytes 393224 | tf_op jit(solution)/shard_map/ppermute | solution.py:573
  4.7 19.9 %collective-permute-start.12 = (bf16[128,512]{1,0:T(8,128)(2,1)S(1)}, bf16[128,512]{1,0:T(8,128)(2,1)S(1)}, u32[]{:S(2)}, u32[]{:S(2)}) collective-permute-start(bf16[128,512]{1,0:T(8,128)(2,1)S(1)} %get-tuple-element.60), channel_id=1, source_target_pairs={{0,2},{1,3},{2,0},{3,1},{4,6},{5,7},{6,4},{7,5},{8,10},{9,11},{10,... | collective-permute-start | bytes 393224 | tf_op jit(solution)/shard_map/ppermute | solution.py:573
  7.3 17.3 %collective-permute-start.13 = (bf16[128,512]{1,0:T(8,128)(2,1)S(1)}, bf16[128,512]{1,0:T(8,128)(2,1)S(1)}, u32[]{:S(2)}, u32[]{:S(2)}) collective-permute-start(bf16[128,512]{1,0:T(8,128)(2,1)S(1)} %get-tuple-element.61), channel_id=1, source_target_pairs={{0,3},{1,2},{2,1},{3,0},{4,7},{5,6},{6,5},{7,4},{8,11},{9,10},{10,... | collective-permute-start | bytes 393224 | tf_op jit(solution)/shard_map/ppermute | solution.py:573
  8.3 2.2 %collective-permute-start.5 = (bf16[2,4608]{1,0:T(2,128)(2,1)S(1)}, bf16[2,4608]{1,0:T(2,128)(2,1)S(1)}, u32[]{:S(2)}, u32[]{:S(2)}) collective-permute-start(bf16[2,4608]{1,0:T(2,128)(2,1)S(1)} %get-tuple-element.54), channel_id=1, source_target_pairs={{0,1},{1,0},{2,3},{3,2},{4,5},{5,4},{6,7},{7,6},{8,9},{9,8},{10,11... | collective-permute-start | bytes 55304 | tf_op jit(solution)/shard_map/ppermute | solution.py:573
  8.6 6.2 %collective-permute-start.6 = (bf16[2,4608]{1,0:T(2,128)(2,1)S(1)}, bf16[2,4608]{1,0:T(2,128)(2,1)S(1)}, u32[]{:S(2)}, u32[]{:S(2)}) collective-permute-start(bf16[2,4608]{1,0:T(2,128)(2,1)S(1)} %get-tuple-element.55), channel_id=1, source_target_pairs={{0,2},{1,3},{2,0},{3,1},{4,6},{5,7},{6,4},{7,5},{8,10},{9,11},{10,... | collective-permute-start | bytes 55304 | tf_op jit(solution)/shard_map/ppermute | solution.py:573
  10.5 4.3 %collective-permute-start.7 = (bf16[2,4608]{1,0:T(2,128)(2,1)S(1)}, bf16[2,4608]{1,0:T(2,128)(2,1)S(1)}, u32[]{:S(2)}, u32[]{:S(2)}) collective-permute-start(bf16[2,4608]{1,0:T(2,128)(2,1)S(1)} %get-tuple-element.56), channel_id=1, source_target_pairs={{0,3},{1,2},{2,1},{3,0},{4,7},{5,6},{6,5},{7,4},{8,11},{9,10},{10,... | collective-permute-start | bytes 55304 | tf_op jit(solution)/shard_map/ppermute | solution.py:573
  14.9 5.8 %collective-permute-start.10 = (bf16[8,2048]{1,0:T(8,128)(2,1)S(1)}, bf16[8,2048]{1,0:T(8,128)(2,1)S(1)}, u32[]{:S(2)}, u32[]{:S(2)}) collective-permute-start(bf16[8,2048]{1,0:T(8,128)(2,1)S(1)} %get-tuple-element.57.r_1_.r_0_), channel_id=1, source_target_pairs={{0,12},{1,13},{2,14},{3,15},{4,8},{5,9},{6,10},{7,11},{8,4},{9,5},... | collective-permute-start | bytes 98312 | tf_op jit(solution)/shard_map/ppermute | solution.py:573
  18.8 4.8 %collective-permute-start.9 = (bf16[8,2048]{1,0:T(8,128)(2,1)S(1)}, bf16[8,2048]{1,0:T(8,128)(2,1)S(1)}, u32[]{:S(2)}, u32[]{:S(2)}) collective-permute-start(bf16[8,2048]{1,0:T(8,128)(2,1)S(1)} %get-tuple-element.57.r_1_.r_0_), channel_id=1, source_target_pairs={{0,8},{1,9},{2,10},{3,11},{4,12},{5,13},{6,14},{7,15},{8,0},{9,1},... | collective-permute-start | bytes 98312 | tf_op jit(solution)/shard_map/ppermute | solution.py:573
  20.7 3.9 %collective-permute-start.8 = (bf16[8,2048]{1,0:T(8,128)(2,1)S(1)}, bf16[8,2048]{1,0:T(8,128)(2,1)S(1)}, u32[]{:S(2)}, u32[]{:S(2)}) collective-permute-start(bf16[8,2048]{1,0:T(8,128)(2,1)S(1)} %get-tuple-element.57.r_1_.r_0_), channel_id=1, source_target_pairs={{0,4},{1,5},{2,6},{3,7},{4,0},{5,1},{6,2},{7,3},{8,12},{9,13},{10,... | collective-permute-start | bytes 98312 | tf_op jit(solution)/shard_map/ppermute | solution.py:573
  26.7 6.2 %collective-permute-start.14 = (bf16[8,2176]{1,0:T(8,128)(2,1)S(1)}, bf16[8,2176]{1,0:T(8,128)(2,1)S(1)}, u32[]{:S(2)}, u32[]{:S(2)}) collective-permute-start(bf16[8,2176]{1,0:T(8,128)(2,1)S(1)} %get-tuple-element.63), channel_id=1, source_target_pairs={{0,4},{1,5},{2,6},{3,7},{4,0},{5,1},{6,2},{7,3},{8,12},{9,13},{10,... | collective-permute-start | bytes 104456 | tf_op jit(solution)/shard_map/ppermute | solution.py:573
  27.4 6.4 %collective-permute-start.15 = (bf16[8,2176]{1,0:T(8,128)(2,1)S(1)}, bf16[8,2176]{1,0:T(8,128)(2,1)S(1)}, u32[]{:S(2)}, u32[]{:S(2)}) collective-permute-start(bf16[8,2176]{1,0:T(8,128)(2,1)S(1)} %get-tuple-element.64), channel_id=1, source_target_pairs={{0,8},{1,9},{2,10},{3,11},{4,12},{5,13},{6,14},{7,15},{8,0},{9,1},... | collective-permute-start | bytes 104456 | tf_op jit(solution)/shard_map/ppermute | solution.py:573
  31.1 5.7 %collective-permute-start.16 = (bf16[8,2176]{1,0:T(8,128)(2,1)S(1)}, bf16[8,2176]{1,0:T(8,128)(2,1)S(1)}, u32[]{:S(2)}, u32[]{:S(2)}) collective-permute-start(bf16[8,2176]{1,0:T(8,128)(2,1)S(1)} %get-tuple-element.65), channel_id=1, source_target_pairs={{0,12},{1,13},{2,14},{3,15},{4,8},{5,9},{6,10},{7,11},{8,4},{9,5},... | collective-permute-start | bytes 104456 | tf_op jit(solution)/shard_map/ppermute | solution.py:573
  31.1 18.6 %collective-permute-start = (bf16[32,2176]{1,0:T(8,128)(2,1)S(1)}, bf16[32,2176]{1,0:T(8,128)(2,1)S(1)}, u32[]{:S(2)}, u32[]{:S(2)}) collective-permute-start(bf16[32,2176]{1,0:T(8,128)(2,1)S(1)} %get-tuple-element.46), channel_id=1, source_target_pairs={{0,1},{1,0},{2,3},{3,2},{4,5},{5,4},{6,7},{7,6},{8,9},{9,8},{10,11... | collective-permute-start | bytes 417800 | tf_op jit(solution)/shard_map/ppermute | solution.py:573
  31.1 18.6 %collective-permute-start.1 = (bf16[32,2176]{1,0:T(8,128)(2,1)S(1)}, bf16[32,2176]{1,0:T(8,128)(2,1)S(1)}, u32[]{:S(2)}, u32[]{:S(2)}) collective-permute-start(bf16[32,2176]{1,0:T(8,128)(2,1)S(1)} %get-tuple-element.47), channel_id=1, source_target_pairs={{0,2},{1,3},{2,0},{3,1},{4,6},{5,7},{6,4},{7,5},{8,10},{9,11},{10,... | collective-permute-start | bytes 417800 | tf_op jit(solution)/shard_map/ppermute | solution.py:573
  32.9 16.9 %collective-permute-start.2 = (bf16[32,2176]{1,0:T(8,128)(2,1)S(1)}, bf16[32,2176]{1,0:T(8,128)(2,1)S(1)}, u32[]{:S(2)}, u32[]{:S(2)}) collective-permute-start(bf16[32,2176]{1,0:T(8,128)(2,1)S(1)} %get-tuple-element.48), channel_id=1, source_target_pairs={{0,3},{1,2},{2,1},{3,0},{4,7},{5,6},{6,5},{7,4},{8,11},{9,10},{10,... | collective-permute-start | bytes 417800 | tf_op jit(solution)/shard_map/ppermute | solution.py:573
  39.0 9.2 %collective-permute-start.19 = (bf16[8,2176]{1,0:T(8,128)(2,1)S(1)}, bf16[8,2176]{1,0:T(8,128)(2,1)S(1)}, u32[]{:S(2)}, u32[]{:S(2)}) collective-permute-start(bf16[8,2176]{1,0:T(8,128)(2,1)S(1)} %get-tuple-element.68), channel_id=1, source_target_pairs={{0,12},{1,13},{2,14},{3,15},{4,8},{5,9},{6,10},{7,11},{8,4},{9,5},... | collective-permute-start | bytes 104456 | tf_op jit(solution)/shard_map/ppermute | solution.py:573
  39.4 3.9 %collective-permute-start.17 = (bf16[8,2176]{1,0:T(8,128)(2,1)S(1)}, bf16[8,2176]{1,0:T(8,128)(2,1)S(1)}, u32[]{:S(2)}, u32[]{:S(2)}) collective-permute-start(bf16[8,2176]{1,0:T(8,128)(2,1)S(1)} %get-tuple-element.68), channel_id=1, source_target_pairs={{0,4},{1,5},{2,6},{3,7},{4,0},{5,1},{6,2},{7,3},{8,12},{9,13},{10,... | collective-permute-start | bytes 104456 | tf_op jit(solution)/shard_map/ppermute | solution.py:573
  43.3 4.8 %collective-permute-start.18 = (bf16[8,2176]{1,0:T(8,128)(2,1)S(1)}, bf16[8,2176]{1,0:T(8,128)(2,1)S(1)}, u32[]{:S(2)}, u32[]{:S(2)}) collective-permute-start(bf16[8,2176]{1,0:T(8,128)(2,1)S(1)} %get-tuple-element.68), channel_id=1, source_target_pairs={{0,8},{1,9},{2,10},{3,11},{4,12},{5,13},{6,14},{7,15},{8,0},{9,1},... | collective-permute-start | bytes 104456 | tf_op jit(solution)/shard_map/ppermute | solution.py:573
  48.2 6.1 %collective-permute-start.20 = (bf16[32,2176]{1,0:T(8,128)(2,1)S(1)}, bf16[32,2176]{1,0:T(8,128)(2,1)S(1)}, u32[]{:S(2)}, u32[]{:S(2)}) collective-permute-start(bf16[32,2176]{1,0:T(8,128)(2,1)S(1)} %constant_dynamic-update-slice_fusion.r_0_), channel_id=1, source_target_pairs={{0,2},{1,3},{2,0},{3,1},{4,6},{5,7},{6,4},{7,5},{8,10},{9,11},{10,... | collective-permute-start | bytes 417800 | tf_op jit(solution)/shard_map/ppermute | solution.py:573
  51.9 29.6 %collective-permute-start.3 = (bf16[64,2176]{1,0:T(8,128)(2,1)S(1)}, bf16[64,2176]{1,0:T(8,128)(2,1)S(1)}, u32[]{:S(2)}, u32[]{:S(2)}) collective-permute-start(bf16[64,2176]{1,0:T(8,128)(2,1)S(1)} %get-tuple-element.50), channel_id=1, source_target_pairs={{0,8},{1,9},{2,10},{3,11},{4,12},{5,13},{6,14},{7,15},{8,0},{9,1},... | collective-permute-start | bytes 835592 | tf_op jit(solution)/shard_map/ppermute | solution.py:573
  54.3 13.3 %collective-permute-start.21 = (bf16[32,2176]{1,0:T(8,128)(2,1)S(1)}, bf16[32,2176]{1,0:T(8,128)(2,1)S(1)}, u32[]{:S(2)}, u32[]{:S(2)}) collective-permute-start(bf16[32,2176]{1,0:T(8,128)(2,1)S(1)} %constant_dynamic-update-slice_fusion.r_0_), channel_id=1, source_target_pairs={{0,1},{1,0},{2,3},{3,2},{4,5},{5,4},{6,7},{7,6},{8,9},{9,8},{10,11... | collective-permute-start | bytes 417800 | tf_op jit(solution)/shard_map/ppermute | solution.py:573
  54.3 13.3 %collective-permute-start.22 = (bf16[32,2176]{1,0:T(8,128)(2,1)S(1)}, bf16[32,2176]{1,0:T(8,128)(2,1)S(1)}, u32[]{:S(2)}, u32[]{:S(2)}) collective-permute-start(bf16[32,2176]{1,0:T(8,128)(2,1)S(1)} %collective-permute-done.20.r_0_.r_1_), channel_id=1, source_target_pairs={{0,1},{1,0},{2,3},{3,2},{4,5},{5,4},{6,7},{7,6},{8,9},{9,8},{10,11... | collective-permute-start | bytes 417800 | tf_op jit(solution)/shard_map/ppermute | solution.py:573
  81.3 2.0 %collective-permute-start.23 = (f32[16,8192]{1,0:T(8,128)S(1)}, f32[16,8192]{1,0:T(8,128)S(1)}, u32[]{:S(2)}, u32[]{:S(2)}) collective-permute-start(f32[16,8192]{1,0:T(8,128)S(1)} %get-tuple-element.81), channel_id=1, source_target_pairs={{0,1},{1,0},{2,3},{3,2},{4,5},{5,4},{6,7},{7,6},{8,9},{9,8},{10,11... | collective-permute-start | bytes 1572872 | tf_op jit(solution)/shard_map/ppermute | solution.py:573
  81.5 12.1 %collective-permute-start.4 = (bf16[64,2176]{1,0:T(8,128)(2,1)S(1)}, bf16[64,2176]{1,0:T(8,128)(2,1)S(1)}, u32[]{:S(2)}, u32[]{:S(2)}) collective-permute-start(bf16[64,2176]{1,0:T(8,128)(2,1)S(1)} %pad_maximum_fusion), channel_id=1, source_target_pairs={{0,4},{1,5},{2,6},{3,7},{4,0},{5,1},{6,2},{7,3},{8,12},{9,13},{10,... | collective-permute-start | bytes 835592 | tf_op jit(solution)/shard_map/ppermute | solution.py:573
  83.5 5.7 %collective-permute-start.24 = (bf16[8,8192]{1,0:T(8,128)(2,1)S(1)}, bf16[8,8192]{1,0:T(8,128)(2,1)S(1)}, u32[]{:S(2)}, u32[]{:S(2)}) collective-permute-start(bf16[8,8192]{1,0:T(8,128)(2,1)S(1)} %get-tuple-element.83), channel_id=1, source_target_pairs={{0,2},{1,3},{2,0},{3,1},{4,6},{5,7},{6,4},{7,5},{8,10},{9,11},{10,... | collective-permute-start | bytes 393224 | tf_op jit(solution)/shard_map/ppermute | solution.py:573
  89.2 5.4 %collective-permute-start.25 = (bf16[2,8192]{1,0:T(2,128)(2,1)S(1)}, bf16[2,8192]{1,0:T(2,128)(2,1)S(1)}, u32[]{:S(2)}, u32[]{:S(2)}) collective-permute-start(bf16[2,8192]{1,0:T(2,128)(2,1)S(1)} %get-tuple-element.85), channel_id=1, source_target_pairs={{0,4},{1,5},{2,6},{3,7},{4,0},{5,1},{6,2},{7,3},{8,12},{9,13},{10,... | collective-permute-start | bytes 98312 | tf_op jit(solution)/shard_map/ppermute | solution.py:573
  90.9 5.3 %collective-permute-start.26 = (bf16[2,8192]{1,0:T(2,128)(2,1)S(1)}, bf16[2,8192]{1,0:T(2,128)(2,1)S(1)}, u32[]{:S(2)}, u32[]{:S(2)}) collective-permute-start(bf16[2,8192]{1,0:T(2,128)(2,1)S(1)} %get-tuple-element.86), channel_id=1, source_target_pairs={{0,8},{1,9},{2,10},{3,11},{4,12},{5,13},{6,14},{7,15},{8,0},{9,1},... | collective-permute-start | bytes 98312 | tf_op jit(solution)/shard_map/ppermute | solution.py:573
  92.2 5.7 %collective-permute-start.27 = (bf16[2,8192]{1,0:T(2,128)(2,1)S(1)}, bf16[2,8192]{1,0:T(2,128)(2,1)S(1)}, u32[]{:S(2)}, u32[]{:S(2)}) collective-permute-start(bf16[2,8192]{1,0:T(2,128)(2,1)S(1)} %get-tuple-element.87), channel_id=1, source_target_pairs={{0,12},{1,13},{2,14},{3,15},{4,8},{5,9},{6,10},{7,11},{8,4},{9,5},... | collective-permute-start | bytes 98312 | tf_op jit(solution)/shard_map/ppermute | solution.py:573

commit v4 on v3

--- a/solution.py
+++ b/solution.py
@@ -465,19 +465,18 @@
         c.wait()
 
 
-def rest_body(planes, held, late, own, xs, near, far, acc_in, h, *refs):
+def hidden_body(planes, held, late, own, xs, near, far, acc_in, *refs):
     blocks, refs = blocks_of(held, refs[: len(held)]), refs[len(held) :]
-    w_gate, w_up, w_down, send, keep, acc, out, buf, sem, dbuf, dsem = refs
+    w_gate, w_up, w_down, out, down_out, acc, buf, sem, dsem = refs
     wide = near.shape[1] - EXTRA
     ff = w_gate.shape[1]
     pos = here() % CELL
-    depth = dbuf.shape[0]
     fetched = fetch_copies([late], (w_gate, w_up), [buf], sem)
     downs = []
-    for n in range(ff // DOWN_ROWS):
-        src = w_down.at[pl.ds(n * DOWN_ROWS, DOWN_ROWS), :]
-        downs.append(pltpu.make_async_copy(src, dbuf.at[n % depth], dsem.at[n % depth]))
-    for c in fetched + downs[:depth]:
+    for n in range(down_out.shape[0] // DOWN_ROWS):
+        rows = pl.ds(n * DOWN_ROWS, DOWN_ROWS)
+        downs.append(pltpu.make_async_copy(w_down.at[rows, :], down_out.at[rows, :], dsem.at[n]))
+    for c in fetched + downs:
         c.start()
     per = 2 * wide // GU_ROWS
     x_of = {1: near, 3: far}
@@ -518,19 +517,36 @@
         ],
         axis=0,
     ).astype(BF16)
-    for n, c in enumerate(downs):
+    out[...] = hidden
+    for c in downs:
         c.wait()
-        part = jnp.dot(
-            hidden[:, n * DOWN_ROWS : (n + 1) * DOWN_ROWS],
-            dbuf[n % depth],
-            preferred_element_type=F32,
-        )
-        if n == 0:
-            out[...] = part
-        else:
-            out[...] += part
-        if n + depth < len(downs):
-            downs[n + depth].start()
+
+
+def down_body(planes, hidden, h, held, w_down, send, keep, out, dbuf, dsem):
+    pos = here() % CELL
+    wide = h.shape[1]
+    n_held, total = held.shape[0] // DOWN_ROWS, w_down.shape[0] // DOWN_ROWS
+    downs = []
+    for n in range(n_held, total):
+        src = w_down.at[pl.ds(n * DOWN_ROWS, DOWN_ROWS), :]
+        downs.append(pltpu.make_async_copy(src, dbuf.at[n - n_held], dsem.at[n - n_held]))
+    for c in downs:
+        c.start()
+
+    @pl.when(pos >= 0)
+    def _():
+        for n in range(n_held):
+            rows = slice(n * DOWN_ROWS, (n + 1) * DOWN_ROWS)
+            part = jnp.dot(hidden[:, rows], held[rows, :], preferred_element_type=F32)
+            if n == 0:
+                out[...] = part
+            else:
+                out[...] += part
+
+    for n in range(n_held, total):
+        downs[n - n_held].wait()
+        rows = slice(n * DOWN_ROWS, (n + 1) * DOWN_ROWS)
+        out[...] += jnp.dot(hidden[:, rows], dbuf[n - n_held], preferred_element_type=F32)
     per = 2 * planes
     for g in range(CELL):
 
@@ -606,12 +622,12 @@
     per = 2 * wide // GU_ROWS
     plans = {
         "turn": [(0, 0, 4, ff)],
-        "warm_q": [(0, 4, 2, ff)],
+        "warm_z": [(0, 4, 2, ff)],
         "scores": [(0, 6, per - 6, ff)],
-        "merge": [(2, 0, 2, ff)],
-        "regroup": [(2, 2, 2, ff)],
-        "gate_up_own": [(2, 4, per - 4, ff), (1, 0, 4, ff)],
-        "gate_up_x": [(1, 4, per - 4, ff), (3, 0, 4, ff)],
+        "merge": [(2, 0, 1, ff)],
+        "regroup": [(2, 1, 2, ff)],
+        "gate_up_own": [(2, 3, per - 3, ff), (1, 0, 3, ff)],
+        "gate_up_x": [(1, 3, per - 3, ff), (3, 0, 4, ff)],
         "rest": [(3, 4, per - 4, ff)],
     }
     held = []
@@ -676,7 +692,6 @@
         4,
     )
     qs = [own_q] + [swap(own_q, CELL * k, devices) for k in range(1, planes)]
-    warm("warm_q", own_q)
     relays = [relays[0]] + [swap(relays[k], k, devices) for k in range(1, CELL)]
     plan = plans["scores"]
     parts = call(
@@ -719,6 +734,7 @@
     relay_mine, relay_far, relay_near = grouped[:3]
     keep_pieces("regroup", grouped[3:])
     relay_far = swap(relay_far, 2 * CELL, devices)
+    warm("warm_z", normed)
     blocks = [normed] + [swap(normed, CELL * k, devices) for k in range(1, planes)]
     own = jnp.concatenate(blocks, axis=0)
     across = swap(own, 2, devices)
@@ -748,26 +764,40 @@
     relay_near = swap(relay_near, CELL, devices)
     specs, values = pieces_for(1, 3)
     late = plans["rest"][0]
-    send, keep = call(
-        lambda *r: rest_body(planes, specs, late, *r),
-        [vmem()] * (6 + len(values)) + [hbm()] * 3,
-        [((all_rows // 2, model), F32)] * 2,
+    n_first = 3
+    n_later = ff // DOWN_ROWS - n_first
+    hidden, down_held = call(
+        lambda *r: hidden_body(planes, specs, late, *r),
+        [vmem()] * (5 + len(values)) + [hbm()] * 3,
+        [((all_rows, ff), BF16), ((n_first * DOWN_ROWS, model), BF16)],
         (
-            *[in_vmem(x) for x in (own, across, near, far, acc, hstate)],
+            *[in_vmem(x) for x in (own, across, near, far, acc)],
             *values,
             *weights,
             in_hbm(w_down),
         ),
-        30,
+        12,
         [
             pltpu.VMEM((all_rows, 2 * ff), F32),
-            pltpu.VMEM((all_rows, model), F32),
             pltpu.VMEM(piece_shape(late), BF16),
             pltpu.SemaphoreType.DMA((count_of([late]),)),
-            pltpu.VMEM((5, DOWN_ROWS, model), BF16),
-            pltpu.SemaphoreType.DMA((5,)),
+            pltpu.SemaphoreType.DMA((n_first,)),
         ],
-        moved=40,
+        moved=20,
+        on_chip=True,
+    )
+    send, keep = call(
+        lambda *r: down_body(planes, *r),
+        [vmem()] * 3 + [hbm()],
+        [((all_rows // 2, model), F32)] * 2,
+        (in_vmem(hidden), in_vmem(hstate), in_vmem(down_held), in_hbm(w_down)),
+        19,
+        [
+            pltpu.VMEM((all_rows, model), F32),
+            pltpu.VMEM((n_later, DOWN_ROWS, model), BF16),
+            pltpu.SemaphoreType.DMA((n_later,)),
+        ],
+        moved=20,
         on_chip=True,
     )
     got = swap(send, 1, devices)

time: 98.8 us -> 98.9 us (level)
    pallas_call x14 -> x15, Pallas kernels: 39.1 us -> 39 us  [call(): pl.pallas_call(body, in_specs=ins, out_specs=[vmem() for _ in shapes], ou...]
where the time goes in v4:
time: 98.9 us; the launch traced here: 98.7 us
  Pallas kernels  39 us (39%)
  starting transfers between devices  31.3 us (32%)
  waiting for transfers between devices  27.5 us (28%)
    pallas_call x15, Pallas kernels, call(): pl.pallas_call(body, in_specs=ins, out_specs=[vmem() for _ in shapes], ou...  39 us
    ppermute x28, starting transfers between devices, swap(): return lax.ppermute(x, 'ctx', [(i, i ^ k) for i in range(devices)])  31.3 us
    ppermute x28, waiting for transfers between devices, swap(): return lax.ppermute(x, 'ctx', [(i, i ^ k) for i in range(devices)])  27.5 us
  transfers between devices with their start and end apart: 28, of which 11 were waited for; matrix products, arithmetic and copies ran while one was open for 0% of the time, Pallas kernels for 33%

profile of v4, /device:TPU:0, one launch (start us, length us, event | category | flops | bytes accessed | tf_op | source)
XLA Modules:
  0.0 98.7 jit_solution(12990001057079351616)
XLA Ops:
  0.6 3.5 %shard_map.131 = (bf16[128,512]{1,0:T(8,128)(2,1)S(1)}, bf16[128,512]{1,0:T(8,128)(2,1)S(1)}, bf16[128,512]{1,0:T(8,128)(2,1)S(1)}, bf16[128,512]{1,0:T(8,128)(2...) custom-call(s32[4]{0:T(128)} %r_0_.1, ...), custom_call_target="tpu_custom_call" | custom-call | bytes 8388608 | tf_op jit(solution)/shard_map/pallas_call | solution.py:40
  4.7 2.6 %collective-permute-start.12 = (bf16[128,512]{1,0:T(8,128)(2,1)S(1)}, bf16[128,512]{1,0:T(8,128)(2,1)S(1)}, u32[]{:S(2)}, u32[]{:S(2)}) collective-permute-start(bf16[128,512]{1,0:T(8,128)(2,1)S(1)} %get-tuple-element.62), channel_id=1, source_target_pairs={{0,2},{1,3},{2,0},{3,1},{4,6},{5,7},{6,4},{7,5},{8,10},{9,11},{10,... | collective-permute-start | bytes 393224 | tf_op jit(solution)/shard_map/ppermute | solution.py:589
  7.3 1.0 %shard_map.134 = (bf16[2,4608]{1,0:T(2,128)(2,1)S(1)}, bf16[2,4608]{1,0:T(2,128)(2,1)S(1)}, bf16[2,4608]{1,0:T(2,128)(2,1)S(1)}, bf16[2,4608]{1,0:T(2,128)(2,1)S(1)}, bf16[16,128]{1,0:T(8,128)(2,1)S(1)}) custom-call(bf16[2,8192]{1,0:T(2,128)(2,1)} %q.1, bf16[2,2048]{1,0:T(2,128)(2,1)} %kv.1, bf16[2,8192]{1,0:T(2,128)(2,1)} %res.1, bf16[64,128]{1,0:T(8,128)(2,1)} %bitcast.6), custom_call_target="tpu_custom_call" | custom-call | tf_op jit(solution)/shard_map/pallas_call | solution.py:40
  8.6 1.9 %collective-permute-start.6 = (bf16[2,4608]{1,0:T(2,128)(2,1)S(1)}, bf16[2,4608]{1,0:T(2,128)(2,1)S(1)}, u32[]{:S(2)}, u32[]{:S(2)}) collective-permute-start(bf16[2,4608]{1,0:T(2,128)(2,1)S(1)} %get-tuple-element.57), channel_id=1, source_target_pairs={{0,2},{1,3},{2,0},{3,1},{4,6},{5,7},{6,4},{7,5},{8,10},{9,11},{10,... | collective-permute-start | bytes 55304 | tf_op jit(solution)/shard_map/ppermute | solution.py:589
  11.3 3.5 %collective-permute-done.6.refs_2_ = bf16[2,4608]{1,0:T(2,128)(2,1)S(1)} collective-permute-done((bf16[2,4608]{1,0:T(2,128)(2,1)S(1)}, bf16[2,4608]{1,0:T(2,128)(2,1)S(1)}, u32[]{:S(2)}, u32[]{:S(2)}) %collective-permute-start.6) | collective-permute-done | bytes 18464 | tf_op jit(solution)/shard_map/ppermute | solution.py:589
  14.9 3.9 %collective-permute-start.10 = (bf16[8,2048]{1,0:T(8,128)(2,1)S(1)}, bf16[8,2048]{1,0:T(8,128)(2,1)S(1)}, u32[]{:S(2)}, u32[]{:S(2)}) collective-permute-start(bf16[8,2048]{1,0:T(8,128)(2,1)S(1)} %get-tuple-element.59.r_1_), channel_id=1, source_target_pairs={{0,12},{1,13},{2,14},{3,15},{4,8},{5,9},{6,10},{7,11},{8,4},{9,5},... | collective-permute-start | bytes 98312 | tf_op jit(solution)/shard_map/ppermute | solution.py:589
  18.8 1.9 %collective-permute-done.10.r_4_ = bf16[8,2048]{1,0:T(8,128)(2,1)S(1)} collective-permute-done((bf16[8,2048]{1,0:T(8,128)(2,1)S(1)}, bf16[8,2048]{1,0:T(8,128)(2,1)S(1)}, u32[]{:S(2)}, u32[]{:S(2)}) %collective-permute-start.10) | collective-permute-done | bytes 32800 | tf_op jit(solution)/shard_map/ppermute | solution.py:589
  21.3 2.2 %collective-permute-done.9.r_3_ = bf16[8,2048]{1,0:T(8,128)(2,1)S(1)} collective-permute-done((bf16[8,2048]{1,0:T(8,128)(2,1)S(1)}, bf16[8,2048]{1,0:T(8,128)(2,1)S(1)}, u32[]{:S(2)}, u32[]{:S(2)}) %collective-permute-start.9) | collective-permute-done | bytes 32800 | tf_op jit(solution)/shard_map/ppermute | solution.py:589
  23.6 1.0 %collective-permute-done.8.r_2_ = bf16[8,2048]{1,0:T(8,128)(2,1)S(1)} collective-permute-done((bf16[8,2048]{1,0:T(8,128)(2,1)S(1)}, bf16[8,2048]{1,0:T(8,128)(2,1)S(1)}, u32[]{:S(2)}, u32[]{:S(2)}) %collective-permute-start.8) | collective-permute-done | bytes 32800 | tf_op jit(solution)/shard_map/ppermute | solution.py:589
  24.6 2.1 %shard_map.136 = (bf16[8,2176]{1,0:T(8,128)(2,1)S(1)}, bf16[8,2176]{1,0:T(8,128)(2,1)S(1)}, bf16[8,2176]{1,0:T(8,128)(2,1)S(1)}, bf16[8,2176]{1,0:T(8,128)(2,1)S(1)}, bf16[2,512,1792]{2,1,0:T(8,128)(2,1)S(1)}) custom-call(s32[1,512]{1,0:T(1,128)S(1)} %get-tuple-element.54.r_0_, bf16[8,2048]{1,0:T(8,128)(2,1)S(1)} %get-tuple-element.59.r_1_, ...), custom_call_target="tpu_custom_call" | custom-call | bytes 5242880 | tf_op jit(solution)/shard_map/pallas_call | solution.py:40
  27.4 3.7 %collective-permute-start.15 = (bf16[8,2176]{1,0:T(8,128)(2,1)S(1)}, bf16[8,2176]{1,0:T(8,128)(2,1)S(1)}, u32[]{:S(2)}, u32[]{:S(2)}) collective-permute-start(bf16[8,2176]{1,0:T(8,128)(2,1)S(1)} %get-tuple-element.66), channel_id=1, source_target_pairs={{0,8},{1,9},{2,10},{3,11},{4,12},{5,13},{6,14},{7,15},{8,0},{9,1},... | collective-permute-start | bytes 104456 | tf_op jit(solution)/shard_map/ppermute | solution.py:589
  31.1 1.7 %collective-permute-start.1 = (bf16[32,2176]{1,0:T(8,128)(2,1)S(1)}, bf16[32,2176]{1,0:T(8,128)(2,1)S(1)}, u32[]{:S(2)}, u32[]{:S(2)}) collective-permute-start(bf16[32,2176]{1,0:T(8,128)(2,1)S(1)} %get-tuple-element.49), channel_id=1, source_target_pairs={{0,2},{1,3},{2,0},{3,1},{4,6},{5,7},{6,4},{7,5},{8,10},{9,11},{10,... | collective-permute-start | bytes 417800 | tf_op jit(solution)/shard_map/ppermute | solution.py:589
  33.8 3.1 %collective-permute-done.16.r_3_ = bf16[8,2176]{1,0:T(8,128)(2,1)S(1)} collective-permute-done((bf16[8,2176]{1,0:T(8,128)(2,1)S(1)}, bf16[8,2176]{1,0:T(8,128)(2,1)S(1)}, u32[]{:S(2)}, u32[]{:S(2)}) %collective-permute-start.16) | collective-permute-done | bytes 34848 | tf_op jit(solution)/shard_map/ppermute | solution.py:589
  36.9 1.5 %shard_map.137 = (bf16[8,2176]{1,0:T(8,128)(2,1)S(1)}, f32[8,2048]{1,0:T(8,128)S(1)}, bf16[1,512,1792]{2,1,0:T(8,128)(2,1)S(1)}) custom-call(bf16[8,2176]{1,0:T(8,128)(2,1)S(1)} %get-tuple-element.64.r_0_, bf16[8,2176]{1,0:T(8,128)(2,1)S(1)} %collective-permute-done.14.r_1_, bf16[8,2176]{1,0:T(8,128)(2,1)S(1)} %collective-permute-done.15.r_2_, ...), custom_call_target="tpu_custom_call" | custom-call | bytes 4194304 | tf_op jit(solution)/shard_map/pallas_call | solution.py:40
  38.8 3.9 %collective-permute-done.17 = bf16[8,2176]{1,0:T(8,128)(2,1)S(1)} collective-permute-done((bf16[8,2176]{1,0:T(8,128)(2,1)S(1)}, bf16[8,2176]{1,0:T(8,128)(2,1)S(1)}, u32[]{:S(2)}, u32[]{:S(2)}) %collective-permute-start.17) | collective-permute-done | bytes 34848 | tf_op jit(solution)/shard_map/ppermute | solution.py:589
  42.8 2.4 %collective-permute-start.18 = (bf16[8,2176]{1,0:T(8,128)(2,1)S(1)}, bf16[8,2176]{1,0:T(8,128)(2,1)S(1)}, u32[]{:S(2)}, u32[]{:S(2)}) collective-permute-start(bf16[8,2176]{1,0:T(8,128)(2,1)S(1)} %get-tuple-element.70.r_0_), channel_id=1, source_target_pairs={{0,8},{1,9},{2,10},{3,11},{4,12},{5,13},{6,14},{7,15},{8,0},{9,1},... | collective-permute-start | bytes 104456 | tf_op jit(solution)/shard_map/ppermute | solution.py:589
  45.1 2.5 %collective-permute-done.18 = bf16[8,2176]{1,0:T(8,128)(2,1)S(1)} collective-permute-done((bf16[8,2176]{1,0:T(8,128)(2,1)S(1)}, bf16[8,2176]{1,0:T(8,128)(2,1)S(1)}, u32[]{:S(2)}, u32[]{:S(2)}) %collective-permute-start.18) | collective-permute-done | bytes 34848 | tf_op jit(solution)/shard_map/ppermute | solution.py:589
  47.6 1.6 %collective-permute-start.20 = (bf16[32,2176]{1,0:T(8,128)(2,1)S(1)}, bf16[32,2176]{1,0:T(8,128)(2,1)S(1)}, u32[]{:S(2)}, u32[]{:S(2)}) collective-permute-start(bf16[32,2176]{1,0:T(8,128)(2,1)S(1)} %constant_dynamic-update-slice_fusion.r_0_), channel_id=1, source_target_pairs={{0,2},{1,3},{2,0},{3,1},{4,6},{5,7},{6,4},{7,5},{8,10},{9,11},{10,... | collective-permute-start | bytes 417800 | tf_op jit(solution)/shard_map/ppermute | solution.py:589
  49.2 2.1 %shard_map.132 = (bf16[32,2176]{1,0:T(8,128)(2,1)S(1)}, bf16[64,2176]{1,0:T(8,128)(2,1)S(1)}, bf16[32,2176]{1,0:T(8,128)(2,1)S(1)}, bf16[2,512,1792]{2,1,0:T(8,128)(2,1)S(1)}) custom-call(bf16[32,2176]{1,0:T(8,128)(2,1)S(1)} %get-tuple-element.47.r_0_, bf16[32,2176]{1,0:T(8,128)(2,1)S(1)} %collective-permute-done.r_1_, ...), custom_call_target="tpu_custom_call" | custom-call | bytes 4194304 | tf_op jit(solution)/shard_map/pallas_call | solution.py:40
  51.3 2.4 %collective-permute-start.3 = (bf16[64,2176]{1,0:T(8,128)(2,1)S(1)}, bf16[64,2176]{1,0:T(8,128)(2,1)S(1)}, u32[]{:S(2)}, u32[]{:S(2)}) collective-permute-start(bf16[64,2176]{1,0:T(8,128)(2,1)S(1)} %get-tuple-element.52), channel_id=1, source_target_pairs={{0,8},{1,9},{2,10},{3,11},{4,12},{5,13},{6,14},{7,15},{8,0},{9,1},... | collective-permute-start | bytes 835592 | tf_op jit(solution)/shard_map/ppermute | solution.py:589
  54.3 2.1 %shard_map.138.r_3_ = bf16[2,512,1792]{2,1,0:T(8,128)(2,1)S(1)} custom-call(bf16[8,2176]{1,0:T(8,128)(2,1)S(1)} %get-tuple-element.70.r_0_, bf16[8192,1792]{1,0:T(8,128)(2,1)} %r_8_.1, bf16[8192,1792]{1,0:T(8,128)(2,1)} %r_9_.3), custom_call_target="tpu_custom_call" | custom-call | bytes 8388608 | tf_op jit(solution)/shard_map/pallas_call | solution.py:40
  56.3 5.3 %shard_map.139 = (f32[32,3584]{1,0:T(8,128)S(1)}, bf16[5,512,1792]{2,1,0:T(8,128)(2,1)S(1)}, bf16[3,512,1792]{2,1,0:T(8,128)(2,1)S(1)}) custom-call(bf16[32,2176]{1,0:T(8,128)(2,1)S(1)} %constant_dynamic-update-slice_fusion.r_0_, bf16[4,512,1792]{2,1,0:T(8,128)(2,1)S(1)} %get-tuple-element.71.r_1_, bf16[2,512,1792]{2,1,0:T(8,128)(2,1)S(1)} %get-tuple-element.72.r_2_, ...), custom_call_target="tpu_custom_call" | custom-call | bytes 14680064 | tf_op jit(solution)/shard_map/pallas_call | solution.py:40
  61.7 5.9 %shard_map.140 = (f32[32,3584]{1,0:T(8,128)S(1)}, bf16[5,512,1792]{2,1,0:T(8,128)(2,1)S(1)}, bf16[4,512,1792]{2,1,0:T(8,128)(2,1)S(1)}) custom-call(bf16[32,2176]{1,0:T(8,128)(2,1)S(1)} %collective-permute-done.20.r_0_.r_1_, f32[32,3584]{1,0:T(8,128)S(1)} %get-tuple-element.73.r_1_, bf16[1,512,1792]{2,1,0:T(8,128)(2,1)S(1)} %get-tuple-element.74.r_2_, ...), custom_call_target="tpu_custom_call" | custom-call | bytes 14680064 | tf_op jit(solution)/shard_map/pallas_call | solution.py:40
  67.6 6.8 %shard_map.141 = (bf16[32,1792]{1,0:T(8,128)(2,1)S(1)}, bf16[768,8192]{1,0:T(8,128)(2,1)S(1)}) custom-call(bf16[32,2176]{1,0:T(8,128)(2,1)S(1)} %constant_dynamic-update-slice_fusion.r_0_, bf16[32,2176]{1,0:T(8,128)(2,1)S(1)} %collective-permute-done.20.r_0_.r_1_, bf16[32,2176]{1,0:T(8,128)(2,1)S(1)} %collective-permute-done.21.r_2_, ...), custom_call_target="tpu_custom_call" | custom-call | bytes 20971520 | tf_op jit(solution)/shard_map/pallas_call | solution.py:40
  74.4 6.9 %shard_map.142 = (f32[16,8192]{1,0:T(8,128)S(1)}, f32[16,8192]{1,0:T(8,128)S(1)}) custom-call(bf16[32,1792]{1,0:T(8,128)(2,1)S(1)} %get-tuple-element.81.r_0_, f32[8,2048]{1,0:T(8,128)S(1)} %get-tuple-element.82.r_1_, bf16[768,8192]{1,0:T(8,128)(2,1)S(1)} %get-tuple-element.83.r_2_, bf16[1792,8192]{1,0:T(8,128)(2,1)} %r_3_.1), custom_call_target="tpu_custom_call" | custom-call | bytes 20971520 | tf_op jit(solution)/shard_map/pallas_call | solution.py:40
  81.5 1.9 %collective-permute-start.4 = (bf16[64,2176]{1,0:T(8,128)(2,1)S(1)}, bf16[64,2176]{1,0:T(8,128)(2,1)S(1)}, u32[]{:S(2)}, u32[]{:S(2)}) collective-permute-start(bf16[64,2176]{1,0:T(8,128)(2,1)S(1)} %pad_maximum_fusion), channel_id=1, source_target_pairs={{0,4},{1,5},{2,6},{3,7},{4,0},{5,1},{6,2},{7,3},{8,12},{9,13},{10,... | collective-permute-start | bytes 835592 | tf_op jit(solution)/shard_map/ppermute | solution.py:589
  84.0 5.1 %collective-permute-done.24.r_1_ = bf16[8,8192]{1,0:T(8,128)(2,1)S(1)} collective-permute-done((bf16[8,8192]{1,0:T(8,128)(2,1)S(1)}, bf16[8,8192]{1,0:T(8,128)(2,1)S(1)}, u32[]{:S(2)}, u32[]{:S(2)}) %collective-permute-start.24) | collective-permute-done | bytes 131104 | tf_op jit(solution)/shard_map/ppermute | solution.py:589
  89.1 1.8 %collective-permute-start.25 = (bf16[2,8192]{1,0:T(2,128)(2,1)S(1)}, bf16[2,8192]{1,0:T(2,128)(2,1)S(1)}, u32[]{:S(2)}, u32[]{:S(2)}) collective-permute-start(bf16[2,8192]{1,0:T(2,128)(2,1)S(1)} %get-tuple-element.89), channel_id=1, source_target_pairs={{0,4},{1,5},{2,6},{3,7},{4,0},{5,1},{6,2},{7,3},{8,12},{9,13},{10,... | collective-permute-start | bytes 98312 | tf_op jit(solution)/shard_map/ppermute | solution.py:589
  90.9 1.4 %collective-permute-start.26 = (bf16[2,8192]{1,0:T(2,128)(2,1)S(1)}, bf16[2,8192]{1,0:T(2,128)(2,1)S(1)}, u32[]{:S(2)}, u32[]{:S(2)}) collective-permute-start(bf16[2,8192]{1,0:T(2,128)(2,1)S(1)} %get-tuple-element.90), channel_id=1, source_target_pairs={{0,8},{1,9},{2,10},{3,11},{4,12},{5,13},{6,14},{7,15},{8,0},{9,1},... | collective-permute-start | bytes 98312 | tf_op jit(solution)/shard_map/ppermute | solution.py:589
  92.3 1.3 %collective-permute-start.27 = (bf16[2,8192]{1,0:T(2,128)(2,1)S(1)}, bf16[2,8192]{1,0:T(2,128)(2,1)S(1)}, u32[]{:S(2)}, u32[]{:S(2)}) collective-permute-start(bf16[2,8192]{1,0:T(2,128)(2,1)S(1)} %get-tuple-element.91), channel_id=1, source_target_pairs={{0,12},{1,13},{2,14},{3,15},{4,8},{5,9},{6,10},{7,11},{8,4},{9,5},... | collective-permute-start | bytes 98312 | tf_op jit(solution)/shard_map/ppermute | solution.py:589
  94.5 1.6 %collective-permute-done.26.refs_1_ = bf16[2,8192]{1,0:T(2,128)(2,1)S(1)} collective-permute-done((bf16[2,8192]{1,0:T(2,128)(2,1)S(1)}, bf16[2,8192]{1,0:T(2,128)(2,1)S(1)}, u32[]{:S(2)}, u32[]{:S(2)}) %collective-permute-start.26) | collective-permute-done | bytes 32800 | tf_op jit(solution)/shard_map/ppermute | solution.py:589
  96.1 1.9 %collective-permute-done.27.refs_2_ = bf16[2,8192]{1,0:T(2,128)(2,1)S(1)} collective-permute-done((bf16[2,8192]{1,0:T(2,128)(2,1)S(1)}, bf16[2,8192]{1,0:T(2,128)(2,1)S(1)}, u32[]{:S(2)}, u32[]{:S(2)}) %collective-permute-start.27) | collective-permute-done | bytes 32800 | tf_op jit(solution)/shard_map/ppermute | solution.py:589
  (45 shorter events, 7.6 us)
Async XLA Ops:
  4.2 20.4 %collective-permute-start.11 = (bf16[128,512]{1,0:T(8,128)(2,1)S(1)}, bf16[128,512]{1,0:T(8,128)(2,1)S(1)}, u32[]{:S(2)}, u32[]{:S(2)}) collective-permute-start(bf16[128,512]{1,0:T(8,128)(2,1)S(1)} %get-tuple-element.61), channel_id=1, source_target_pairs={{0,1},{1,0},{2,3},{3,2},{4,5},{5,4},{6,7},{7,6},{8,9},{9,8},{10,11... | collective-permute-start | bytes 393224 | tf_op jit(solution)/shard_map/ppermute | solution.py:589
  4.7 19.9 %collective-permute-start.12 = (bf16[128,512]{1,0:T(8,128)(2,1)S(1)}, bf16[128,512]{1,0:T(8,128)(2,1)S(1)}, u32[]{:S(2)}, u32[]{:S(2)}) collective-permute-start(bf16[128,512]{1,0:T(8,128)(2,1)S(1)} %get-tuple-element.62), channel_id=1, source_target_pairs={{0,2},{1,3},{2,0},{3,1},{4,6},{5,7},{6,4},{7,5},{8,10},{9,11},{10,... | collective-permute-start | bytes 393224 | tf_op jit(solution)/shard_map/ppermute | solution.py:589
  7.3 17.3 %collective-permute-start.13 = (bf16[128,512]{1,0:T(8,128)(2,1)S(1)}, bf16[128,512]{1,0:T(8,128)(2,1)S(1)}, u32[]{:S(2)}, u32[]{:S(2)}) collective-permute-start(bf16[128,512]{1,0:T(8,128)(2,1)S(1)} %get-tuple-element.63), channel_id=1, source_target_pairs={{0,3},{1,2},{2,1},{3,0},{4,7},{5,6},{6,5},{7,4},{8,11},{9,10},{10,... | collective-permute-start | bytes 393224 | tf_op jit(solution)/shard_map/ppermute | solution.py:589
  8.3 2.2 %collective-permute-start.5 = (bf16[2,4608]{1,0:T(2,128)(2,1)S(1)}, bf16[2,4608]{1,0:T(2,128)(2,1)S(1)}, u32[]{:S(2)}, u32[]{:S(2)}) collective-permute-start(bf16[2,4608]{1,0:T(2,128)(2,1)S(1)} %get-tuple-element.56), channel_id=1, source_target_pairs={{0,1},{1,0},{2,3},{3,2},{4,5},{5,4},{6,7},{7,6},{8,9},{9,8},{10,11... | collective-permute-start | bytes 55304 | tf_op jit(solution)/shard_map/ppermute | solution.py:589
  8.6 6.2 %collective-permute-start.6 = (bf16[2,4608]{1,0:T(2,128)(2,1)S(1)}, bf16[2,4608]{1,0:T(2,128)(2,1)S(1)}, u32[]{:S(2)}, u32[]{:S(2)}) collective-permute-start(bf16[2,4608]{1,0:T(2,128)(2,1)S(1)} %get-tuple-element.57), channel_id=1, source_target_pairs={{0,2},{1,3},{2,0},{3,1},{4,6},{5,7},{6,4},{7,5},{8,10},{9,11},{10,... | collective-permute-start | bytes 55304 | tf_op jit(solution)/shard_map/ppermute | solution.py:589
  10.5 4.3 %collective-permute-start.7 = (bf16[2,4608]{1,0:T(2,128)(2,1)S(1)}, bf16[2,4608]{1,0:T(2,128)(2,1)S(1)}, u32[]{:S(2)}, u32[]{:S(2)}) collective-permute-start(bf16[2,4608]{1,0:T(2,128)(2,1)S(1)} %get-tuple-element.58), channel_id=1, source_target_pairs={{0,3},{1,2},{2,1},{3,0},{4,7},{5,6},{6,5},{7,4},{8,11},{9,10},{10,... | collective-permute-start | bytes 55304 | tf_op jit(solution)/shard_map/ppermute | solution.py:589
  14.9 5.8 %collective-permute-start.10 = (bf16[8,2048]{1,0:T(8,128)(2,1)S(1)}, bf16[8,2048]{1,0:T(8,128)(2,1)S(1)}, u32[]{:S(2)}, u32[]{:S(2)}) collective-permute-start(bf16[8,2048]{1,0:T(8,128)(2,1)S(1)} %get-tuple-element.59.r_1_), channel_id=1, source_target_pairs={{0,12},{1,13},{2,14},{3,15},{4,8},{5,9},{6,10},{7,11},{8,4},{9,5},... | collective-permute-start | bytes 98312 | tf_op jit(solution)/shard_map/ppermute | solution.py:589
  18.8 4.8 %collective-permute-start.9 = (bf16[8,2048]{1,0:T(8,128)(2,1)S(1)}, bf16[8,2048]{1,0:T(8,128)(2,1)S(1)}, u32[]{:S(2)}, u32[]{:S(2)}) collective-permute-start(bf16[8,2048]{1,0:T(8,128)(2,1)S(1)} %get-tuple-element.59.r_1_), channel_id=1, source_target_pairs={{0,8},{1,9},{2,10},{3,11},{4,12},{5,13},{6,14},{7,15},{8,0},{9,1},... | collective-permute-start | bytes 98312 | tf_op jit(solution)/shard_map/ppermute | solution.py:589
  20.7 3.9 %collective-permute-start.8 = (bf16[8,2048]{1,0:T(8,128)(2,1)S(1)}, bf16[8,2048]{1,0:T(8,128)(2,1)S(1)}, u32[]{:S(2)}, u32[]{:S(2)}) collective-permute-start(bf16[8,2048]{1,0:T(8,128)(2,1)S(1)} %get-tuple-element.59.r_1_), channel_id=1, source_target_pairs={{0,4},{1,5},{2,6},{3,7},{4,0},{5,1},{6,2},{7,3},{8,12},{9,13},{10,... | collective-permute-start | bytes 98312 | tf_op jit(solution)/shard_map/ppermute | solution.py:589
  26.7 6.2 %collective-permute-start.14 = (bf16[8,2176]{1,0:T(8,128)(2,1)S(1)}, bf16[8,2176]{1,0:T(8,128)(2,1)S(1)}, u32[]{:S(2)}, u32[]{:S(2)}) collective-permute-start(bf16[8,2176]{1,0:T(8,128)(2,1)S(1)} %get-tuple-element.65), channel_id=1, source_target_pairs={{0,4},{1,5},{2,6},{3,7},{4,0},{5,1},{6,2},{7,3},{8,12},{9,13},{10,... | collective-permute-start | bytes 104456 | tf_op jit(solution)/shard_map/ppermute | solution.py:589
  27.4 6.4 %collective-permute-start.15 = (bf16[8,2176]{1,0:T(8,128)(2,1)S(1)}, bf16[8,2176]{1,0:T(8,128)(2,1)S(1)}, u32[]{:S(2)}, u32[]{:S(2)}) collective-permute-start(bf16[8,2176]{1,0:T(8,128)(2,1)S(1)} %get-tuple-element.66), channel_id=1, source_target_pairs={{0,8},{1,9},{2,10},{3,11},{4,12},{5,13},{6,14},{7,15},{8,0},{9,1},... | collective-permute-start | bytes 104456 | tf_op jit(solution)/shard_map/ppermute | solution.py:589
  31.1 5.7 %collective-permute-start.16 = (bf16[8,2176]{1,0:T(8,128)(2,1)S(1)}, bf16[8,2176]{1,0:T(8,128)(2,1)S(1)}, u32[]{:S(2)}, u32[]{:S(2)}) collective-permute-start(bf16[8,2176]{1,0:T(8,128)(2,1)S(1)} %get-tuple-element.67), channel_id=1, source_target_pairs={{0,12},{1,13},{2,14},{3,15},{4,8},{5,9},{6,10},{7,11},{8,4},{9,5},... | collective-permute-start | bytes 104456 | tf_op jit(solution)/shard_map/ppermute | solution.py:589
  31.1 18.0 %collective-permute-start = (bf16[32,2176]{1,0:T(8,128)(2,1)S(1)}, bf16[32,2176]{1,0:T(8,128)(2,1)S(1)}, u32[]{:S(2)}, u32[]{:S(2)}) collective-permute-start(bf16[32,2176]{1,0:T(8,128)(2,1)S(1)} %get-tuple-element.48), channel_id=1, source_target_pairs={{0,1},{1,0},{2,3},{3,2},{4,5},{5,4},{6,7},{7,6},{8,9},{9,8},{10,11... | collective-permute-start | bytes 417800 | tf_op jit(solution)/shard_map/ppermute | solution.py:589
  31.1 18.0 %collective-permute-start.1 = (bf16[32,2176]{1,0:T(8,128)(2,1)S(1)}, bf16[32,2176]{1,0:T(8,128)(2,1)S(1)}, u32[]{:S(2)}, u32[]{:S(2)}) collective-permute-start(bf16[32,2176]{1,0:T(8,128)(2,1)S(1)} %get-tuple-element.49), channel_id=1, source_target_pairs={{0,2},{1,3},{2,0},{3,1},{4,6},{5,7},{6,4},{7,5},{8,10},{9,11},{10,... | collective-permute-start | bytes 417800 | tf_op jit(solution)/shard_map/ppermute | solution.py:589
  32.9 16.3 %collective-permute-start.2 = (bf16[32,2176]{1,0:T(8,128)(2,1)S(1)}, bf16[32,2176]{1,0:T(8,128)(2,1)S(1)}, u32[]{:S(2)}, u32[]{:S(2)}) collective-permute-start(bf16[32,2176]{1,0:T(8,128)(2,1)S(1)} %get-tuple-element.50), channel_id=1, source_target_pairs={{0,3},{1,2},{2,1},{3,0},{4,7},{5,6},{6,5},{7,4},{8,11},{9,10},{10,... | collective-permute-start | bytes 417800 | tf_op jit(solution)/shard_map/ppermute | solution.py:589
  38.4 9.2 %collective-permute-start.19 = (bf16[8,2176]{1,0:T(8,128)(2,1)S(1)}, bf16[8,2176]{1,0:T(8,128)(2,1)S(1)}, u32[]{:S(2)}, u32[]{:S(2)}) collective-permute-start(bf16[8,2176]{1,0:T(8,128)(2,1)S(1)} %get-tuple-element.70.r_0_), channel_id=1, source_target_pairs={{0,12},{1,13},{2,14},{3,15},{4,8},{5,9},{6,10},{7,11},{8,4},{9,5},... | collective-permute-start | bytes 104456 | tf_op jit(solution)/shard_map/ppermute | solution.py:589
  38.8 3.9 %collective-permute-start.17 = (bf16[8,2176]{1,0:T(8,128)(2,1)S(1)}, bf16[8,2176]{1,0:T(8,128)(2,1)S(1)}, u32[]{:S(2)}, u32[]{:S(2)}) collective-permute-start(bf16[8,2176]{1,0:T(8,128)(2,1)S(1)} %get-tuple-element.70.r_0_), channel_id=1, source_target_pairs={{0,4},{1,5},{2,6},{3,7},{4,0},{5,1},{6,2},{7,3},{8,12},{9,13},{10,... | collective-permute-start | bytes 104456 | tf_op jit(solution)/shard_map/ppermute | solution.py:589
  42.8 4.8 %collective-permute-start.18 = (bf16[8,2176]{1,0:T(8,128)(2,1)S(1)}, bf16[8,2176]{1,0:T(8,128)(2,1)S(1)}, u32[]{:S(2)}, u32[]{:S(2)}) collective-permute-start(bf16[8,2176]{1,0:T(8,128)(2,1)S(1)} %get-tuple-element.70.r_0_), channel_id=1, source_target_pairs={{0,8},{1,9},{2,10},{3,11},{4,12},{5,13},{6,14},{7,15},{8,0},{9,1},... | collective-permute-start | bytes 104456 | tf_op jit(solution)/shard_map/ppermute | solution.py:589
  47.6 6.1 %collective-permute-start.20 = (bf16[32,2176]{1,0:T(8,128)(2,1)S(1)}, bf16[32,2176]{1,0:T(8,128)(2,1)S(1)}, u32[]{:S(2)}, u32[]{:S(2)}) collective-permute-start(bf16[32,2176]{1,0:T(8,128)(2,1)S(1)} %constant_dynamic-update-slice_fusion.r_0_), channel_id=1, source_target_pairs={{0,2},{1,3},{2,0},{3,1},{4,6},{5,7},{6,4},{7,5},{8,10},{9,11},{10,... | collective-permute-start | bytes 417800 | tf_op jit(solution)/shard_map/ppermute | solution.py:589
  51.3 30.2 %collective-permute-start.3 = (bf16[64,2176]{1,0:T(8,128)(2,1)S(1)}, bf16[64,2176]{1,0:T(8,128)(2,1)S(1)}, u32[]{:S(2)}, u32[]{:S(2)}) collective-permute-start(bf16[64,2176]{1,0:T(8,128)(2,1)S(1)} %get-tuple-element.52), channel_id=1, source_target_pairs={{0,8},{1,9},{2,10},{3,11},{4,12},{5,13},{6,14},{7,15},{8,0},{9,1},... | collective-permute-start | bytes 835592 | tf_op jit(solution)/shard_map/ppermute | solution.py:589
  53.7 13.8 %collective-permute-start.21 = (bf16[32,2176]{1,0:T(8,128)(2,1)S(1)}, bf16[32,2176]{1,0:T(8,128)(2,1)S(1)}, u32[]{:S(2)}, u32[]{:S(2)}) collective-permute-start(bf16[32,2176]{1,0:T(8,128)(2,1)S(1)} %constant_dynamic-update-slice_fusion.r_0_), channel_id=1, source_target_pairs={{0,1},{1,0},{2,3},{3,2},{4,5},{5,4},{6,7},{7,6},{8,9},{9,8},{10,11... | collective-permute-start | bytes 417800 | tf_op jit(solution)/shard_map/ppermute | solution.py:589
  53.7 13.8 %collective-permute-start.22 = (bf16[32,2176]{1,0:T(8,128)(2,1)S(1)}, bf16[32,2176]{1,0:T(8,128)(2,1)S(1)}, u32[]{:S(2)}, u32[]{:S(2)}) collective-permute-start(bf16[32,2176]{1,0:T(8,128)(2,1)S(1)} %collective-permute-done.20.r_0_.r_1_), channel_id=1, source_target_pairs={{0,1},{1,0},{2,3},{3,2},{4,5},{5,4},{6,7},{7,6},{8,9},{9,8},{10,11... | collective-permute-start | bytes 417800 | tf_op jit(solution)/shard_map/ppermute | solution.py:589
  81.3 2.2 %collective-permute-start.23 = (f32[16,8192]{1,0:T(8,128)S(1)}, f32[16,8192]{1,0:T(8,128)S(1)}, u32[]{:S(2)}, u32[]{:S(2)}) collective-permute-start(f32[16,8192]{1,0:T(8,128)S(1)} %get-tuple-element.85), channel_id=1, source_target_pairs={{0,1},{1,0},{2,3},{3,2},{4,5},{5,4},{6,7},{7,6},{8,9},{9,8},{10,11... | collective-permute-start | bytes 1572872 | tf_op jit(solution)/shard_map/ppermute | solution.py:589
  81.5 12.0 %collective-permute-start.4 = (bf16[64,2176]{1,0:T(8,128)(2,1)S(1)}, bf16[64,2176]{1,0:T(8,128)(2,1)S(1)}, u32[]{:S(2)}, u32[]{:S(2)}) collective-permute-start(bf16[64,2176]{1,0:T(8,128)(2,1)S(1)} %pad_maximum_fusion), channel_id=1, source_target_pairs={{0,4},{1,5},{2,6},{3,7},{4,0},{5,1},{6,2},{7,3},{8,12},{9,13},{10,... | collective-permute-start | bytes 835592 | tf_op jit(solution)/shard_map/ppermute | solution.py:589
  83.5 5.5 %collective-permute-start.24 = (bf16[8,8192]{1,0:T(8,128)(2,1)S(1)}, bf16[8,8192]{1,0:T(8,128)(2,1)S(1)}, u32[]{:S(2)}, u32[]{:S(2)}) collective-permute-start(bf16[8,8192]{1,0:T(8,128)(2,1)S(1)} %get-tuple-element.87), channel_id=1, source_target_pairs={{0,2},{1,3},{2,0},{3,1},{4,6},{5,7},{6,4},{7,5},{8,10},{9,11},{10,... | collective-permute-start | bytes 393224 | tf_op jit(solution)/shard_map/ppermute | solution.py:589
  89.1 5.4 %collective-permute-start.25 = (bf16[2,8192]{1,0:T(2,128)(2,1)S(1)}, bf16[2,8192]{1,0:T(2,128)(2,1)S(1)}, u32[]{:S(2)}, u32[]{:S(2)}) collective-permute-start(bf16[2,8192]{1,0:T(2,128)(2,1)S(1)} %get-tuple-element.89), channel_id=1, source_target_pairs={{0,4},{1,5},{2,6},{3,7},{4,0},{5,1},{6,2},{7,3},{8,12},{9,13},{10,... | collective-permute-start | bytes 98312 | tf_op jit(solution)/shard_map/ppermute | solution.py:589
  90.9 5.2 %collective-permute-start.26 = (bf16[2,8192]{1,0:T(2,128)(2,1)S(1)}, bf16[2,8192]{1,0:T(2,128)(2,1)S(1)}, u32[]{:S(2)}, u32[]{:S(2)}) collective-permute-start(bf16[2,8192]{1,0:T(2,128)(2,1)S(1)} %get-tuple-element.90), channel_id=1, source_target_pairs={{0,8},{1,9},{2,10},{3,11},{4,12},{5,13},{6,14},{7,15},{8,0},{9,1},... | collective-permute-start | bytes 98312 | tf_op jit(solution)/shard_map/ppermute | solution.py:589
  92.3 5.7 %collective-permute-start.27 = (bf16[2,8192]{1,0:T(2,128)(2,1)S(1)}, bf16[2,8192]{1,0:T(2,128)(2,1)S(1)}, u32[]{:S(2)}, u32[]{:S(2)}) collective-permute-start(bf16[2,8192]{1,0:T(2,128)(2,1)S(1)} %get-tuple-element.91), channel_id=1, source_target_pairs={{0,12},{1,13},{2,14},{3,15},{4,8},{5,9},{6,10},{7,11},{8,4},{9,5},... | collective-permute-start | bytes 98312 | tf_op jit(solution)/shard_map/ppermute | solution.py:589
